TPU v7x, 32 devices: a whole 2x2x4 slice. The times are simulated.
32 devices in a mesh: occ: 16 (over z, y, core), vir: 2 (over x).
Axes of the slice: x: 2, y: 2, z: 4, core: 2. Of those that a mesh axis runs over, the one named last changes fastest.
Arguments:
- lambda_triples: bfloat16 [256, 320, 320], P('occ', 'vir'), may hold values from -6 to 6
- amplitude_triples: bfloat16 [256, 320, 320], P('occ', 'vir'), may hold values from -6 to 6
- spin_extent: int32 [256], P('occ'), may hold values from 80 to 320
- ladder_weight: bfloat16 [320, 320], P(None, 'vir'), may hold values from -0.3125 to 0.3125
- cycle_weight: bfloat16 [320, 40], replicated, may hold values from -0.3125 to 0.3125
- lambda_doubles: bfloat16 [40, 320], P(None, 'vir'), may hold values from -1 to 1
Outputs:
- residual: bfloat16 [256, 320, 320], P('occ', 'vir')
All inputs are finite; a program needn't handle non-finite values.
Results may differ from a plain program's by a relative error of at most 0.0043.
Values may be sent and summed in bfloat16 or wider, within the bound.
No kernel may reach another device: no remote copies, remote signals or barrier semaphores. Data moves between devices by JAX's collectives and lax.ppermute only.
A program may use at most 64 MiB of HBM per device.

v0:
```python
import jax
import jax.numpy as jnp
from jax import lax
from jax.sharding import PartitionSpec as P


def on_device(
    lambda_triples, amplitude_triples, spin_extent, ladder_weight, cycle_weight, lambda_doubles
):
    f32 = jnp.float32
    width = lambda_triples.shape[2]
    triples_all = lambda_triples.shape[0] * lax.axis_size("occ")
    columns = jnp.arange(width, dtype=jnp.int32)
    keep = columns[None, :] < spin_extent[:, None]
    masked = jnp.where(keep[:, None, :], lambda_triples, jnp.zeros_like(lambda_triples))
    ladder_full, doubles_full = (
        lax.all_gather(ladder_weight, "vir", axis=1, tiled=True),
        lax.all_gather(lambda_doubles, "vir", axis=1, tiled=True),
    )
    ladder_term = jnp.einsum("tae,eb->tab", masked, ladder_full, preferred_element_type=f32)
    cycle_mid = jnp.einsum(
        "tae,em->tam", amplitude_triples, cycle_weight, preferred_element_type=f32
    ).astype(jnp.bfloat16)
    cycle_term = jnp.einsum("tam,mb->tab", cycle_mid, doubles_full, preferred_element_type=f32)
    partial_density = jnp.einsum(
        "tae,tbe->ab",
        masked,
        lax.all_gather(amplitude_triples, "vir", axis=1, tiled=True),
        preferred_element_type=f32,
    )
    density = lax.psum(partial_density, "occ")
    density = (density / jnp.sqrt(f32(triples_all * width))).astype(jnp.bfloat16)
    density_term = jnp.einsum(
        "ac,tcb->tab",
        density,
        lax.all_gather(masked, "vir", axis=1, tiled=True),
        preferred_element_type=f32,
    )
    density_term = density_term / jnp.sqrt(f32(width))
    return (ladder_term + cycle_term + density_term).astype(jnp.bfloat16)


def solution(mesh):
    return jax.shard_map(
        on_device,
        mesh=mesh,
        in_specs=(
            P("occ", "vir", None),
            P("occ", "vir", None),
            P("occ"),
            P(None, "vir"),
            P(),
            P(None, "vir"),
        ),
        out_specs=P("occ", "vir", None),
        check_vma=False,
    )
```

profile of v0, /device:TPU:0, one launch (start us, length us, event | category | flops | bytes accessed | tf_op | source)
XLA Modules:
  0.0 227.0 jit_solution(11360172198900712387)
XLA Ops:
  6.5 0.0 copy-start
  6.5 0.0 copy-start.3
  6.5 0.0 copy-start.2
  6.5 0.0 all-gather.6.cloned.1.call-start
  6.5 0.7 all-gather.6.cloned.1.call-update
  7.3 0.0 all-gather.4.cloned.1.call-start
  7.3 0.7 iota_compare_fusion
  8.0 3.0 %broadcast_select_fusion = bf16[16,160,320]{2,1,0:T(8,128)(2,1)} fusion(bf16[16,160,320]{2,1,0:T(8,128)(2,1)} %param.6, pred[16,320]{1,0:T(8,128)(4,1)S(1)} %iota_compare_fusion), kind=kLoop, calls=%fused_computation.2 | loop fusion | flops 819200 | bytes 3281920 | tf_op jit(solution)/shard_map/jit(_where)/select_n | solution.py:15
  11.1 0.0 copy-start.1
  11.1 0.0 all-gather.4.cloned.1.call-update
  11.1 0.0 all-reduce.2.cloned.1.call-start
  11.2 0.0 copy-done.3
  11.2 5.5 %all-gather = bf16[2,160,40]{1,2,0:T(8,128)(2,1)S(1)} all-gather(bf16[1,160,40]{1,2,0:T(8,128)(2,1)S(1)} %bitcast.27), channel_id=1, replica_groups=mesh['occ'=16,'vir'=2] {'vir'}, dimensions={0}, use_global_device_ids=true | all-gather | bytes 38400 | tf_op jit(solution)/shard_map/all_gather | solution.py:18
  16.7 0.1 reshape.21
  16.8 0.0 copy-done.2
  16.8 7.2 %all_gather.12 = bf16[320,320]{0,1:T(8,128)(2,1)S(1)} all-gather(bf16[320,160]{0,1:T(8,128)(2,1)S(1)} %copy-done.2), channel_id=1, replica_groups=mesh['occ'=16,'vir'=2] {'vir'}, dimensions={1}, use_global_device_ids=true | all-gather | bytes 307200 | tf_op jit(solution)/shard_map/all_gather | solution.py:17
  24.0 4.8 %fusion.2 = f32[16,160,320]{2,1,0:T(8,128)} fusion(bf16[16,160,320]{2,1,0:T(8,128)(2,1)} %broadcast_select_fusion, bf16[320,320]{0,1:T(8,128)(2,1)S(1)} %all_gather.12), kind=kOutput, calls=%fused_computation.6 | convolution fusion | flops 524288000 | bytes 5120000 | tf_op jit(solution)/shard_map/tae,eb->tab/dot_general | solution.py:20
  28.8 36.7 %all-gather.6.cloned.1.call-done = bf16[16,320,320]{2,1,0:T(8,128)(2,1)} async-done(((bf16[16,160,320]{2,1,0:T(8,128)(2,1)}), bf16[16,320,320]{2,1,0:T(8,128)(2,1)}) %all-gather.6.cloned.1.call-update) | async-done | bytes 3276816 | tf_op jit(solution)/shard_map/all_gather | solution.py:28
  65.4 0.0 copy-done.1
  65.4 4.4 %convolution_bitcast_fusion = f32[160,320]{1,0:T(8,128)} fusion(bf16[16,160,320]{2,1,0:T(8,128)(2,1)S(1)} %copy-done.1, bf16[16,320,320]{2,1,0:T(8,128)(2,1)} %all-gather.6.cloned.1.call-done), kind=kOutput, calls=%fused_computation.5 | convolution fusion | flops 524288000 | bytes 5120000 | tf_op jit(solution)/shard_map/tae,tbe->ab/dot_general | solution.py:25
  69.8 0.0 all-reduce.2.cloned.1.call-update
  69.9 0.0 copy-done
  69.9 5.2 %fusion.1 = f32[16,160,320]{2,1,0:T(8,128)} fusion(bf16[320,40,1]{0,1,2:T(8,128)(2,1)S(1)} %reshape.21, bf16[16,160,320]{2,1,0:T(8,128)(2,1)} %param.7, bf16[320,40]{0,1:T(8,128)(2,1)S(1)} %copy-done), kind=kOutput, calls=%fused_computation.4 | convolution fusion | flops 131174400 | bytes 4966400 | tf_op jit(solution)/shard_map/tam,mb->tab/dot_general | solution.py:24
  75.0 46.9 %all-gather.4.cloned.1.call-done = bf16[16,320,320]{2,1,0:T(8,128)(2,1)} async-done(((bf16[16,160,320]{2,1,0:T(8,128)(2,1)}), bf16[16,320,320]{2,1,0:T(8,128)(2,1)}) %all-gather.4.cloned.1.call-update) | async-done | bytes 3276816 | tf_op jit(solution)/shard_map/all_gather | solution.py:36
  121.9 91.6 %all-reduce.2.cloned.1.call-done = f32[160,320]{1,0:T(8,128)} async-done(((f32[160,320]{1,0:T(8,128)}), f32[160,320]{1,0:T(8,128)}) %all-reduce.2.cloned.1.call-update) | async-done | bytes 204816 | tf_op jit(solution)/shard_map/psum | solution.py:31
  213.5 7.0 %fusion = bf16[16,160,320]{2,1,0:T(8,128)(2,1)} fusion(f32[16,160,320]{2,1,0:T(8,128)} %fusion.2, f32[16,160,320]{2,1,0:T(8,128)} %fusion.1, bf16[16,320,320]{2,1,0:T(8,128)(2,1)} %all-gather.4.cloned.1.call-done, f32[160,320]{1,0:T(8,128)} %all-reduce.2.cloned.1.call-done), kind=kOutput, calls=%fused_computation.1 | convolution fusion | flops 527667200 | bytes 11673600 | tf_op jit(solution)/shard_map/ac,tcb->tab/dot_general | solution.py:33
  (1 shorter events, 0.0 us)
Async XLA Ops:
  6.5 63.3 %copy-start = (bf16[320,40]{0,1:T(8,128)(2,1)S(1)}, bf16[320,40]{0,1:T(8,128)(2,1)}, u32[]{:S(2)}) copy-start(bf16[320,40]{0,1:T(8,128)(2,1)} %param.10) | copy-start | bytes 76804
  6.5 4.6 %copy-start.3 = (bf16[40,160]{1,0:T(8,128)(2,1)S(1)}, bf16[40,160]{1,0:T(8,128)(2,1)}, u32[]{:S(2)}) copy-start(bf16[40,160]{1,0:T(8,128)(2,1)} %param.11) | copy-start | bytes 38404
  6.5 10.2 %copy-start.2 = (bf16[320,160]{0,1:T(8,128)(2,1)S(1)}, bf16[320,160]{0,1:T(8,128)(2,1)}, u32[]{:S(2)}) copy-start(bf16[320,160]{0,1:T(8,128)(2,1)} %param.9) | copy-start | bytes 307204
  6.5 58.9 %all-gather.6.cloned.1.call-start = ((), (), s32[]{:S(2)}) async-start(), calls=%async_computation.1 | async-start | bytes 5898240 | tf_op jit(solution)/shard_map/all_gather | solution.py:28
  7.3 114.6 %all-gather.4.cloned.1.call-start = ((), (), s32[]{:S(2)}) async-start(), calls=%async_computation | async-start | bytes 5898240 | tf_op jit(solution)/shard_map/all_gather | solution.py:36
  11.1 54.4 %copy-start.1 = (bf16[16,160,320]{2,1,0:T(8,128)(2,1)S(1)}, bf16[16,160,320]{2,1,0:T(8,128)(2,1)}, u32[]{:S(2)}) copy-start(bf16[16,160,320]{2,1,0:T(8,128)(2,1)} %broadcast_select_fusion) | copy-start | bytes 4915204
  11.1 202.4 %all-reduce.2.cloned.1.call-start = ((), (), s32[]{:S(2)}) async-start(), calls=%async_computation.2 | async-start | bytes 491520 | tf_op jit(solution)/shard_map/psum | solution.py:31
Sparse Core Ops, SparseCore 0:
  8.9 56.4 all-gather.5
  67.0 54.8 all-gather.3
  125.3 88.1 all-reduce.1
where the time goes:
time: 228 us; the launch traced here: 227 us
  waiting for transfers between devices  176 us (77%)
  matrix products  21.4 us (9%)
  between operations  13.1 us (6%)
  blocking collectives  12.7 us (6%)
  other arithmetic  3.77 us (2%)
    psum x1, waiting for transfers between devices, on_device(): density = lax.psum(partial_density, 'occ')  91.6 us
    all_gather x1, waiting for transfers between devices, on_device(): lax.all_gather(masked, 'vir', axis=1, tiled=True)  46.9 us
    all_gather x1, waiting for transfers between devices, on_device(): lax.all_gather(amplitude_triples, 'vir', axis=1, tiled=True)  36.7 us
    all_gather x1, blocking collectives, on_device(): lax.all_gather(ladder_weight, 'vir', axis=1, tiled=True)  7.17 us
    dot_general x1, matrix products, on_device(): jnp.einsum('ac,tcb->tab', density, lax.all_gather(masked, 'vir', axis=1,...  6.98 us
    all_gather x1, blocking collectives, on_device(): lax.all_gather(lambda_doubles, 'vir', axis=1, tiled=True)  5.48 us
    dot_general x1, matrix products, on_device(): jnp.einsum('tam,mb->tab', cycle_mid, doubles_full, preferred_element_type...  5.16 us
    dot_general x1, matrix products, on_device(): jnp.einsum('tae,eb->tab', masked, ladder_full, preferred_element_type=f32)  4.8 us
  transfers between devices with their start and end apart: 3, of which 3 were waited for; matrix products, arithmetic and copies ran while one was open for 8% of the time, Pallas kernels for 0%

commit v1 on v0

v1 whole, which is shorter than its diff:
```python
import functools

import jax
import jax.numpy as jnp
from jax import lax
from jax.experimental import pallas as pl
from jax.experimental.pallas import tpu as pltpu
from jax.sharding import PartitionSpec as P

F32, BF16 = jnp.float32, jnp.bfloat16
NT = (((1,), (1,)), ((), ()))
VMEM = functools.partial(pl.BlockSpec, memory_space=pltpu.VMEM)
SMEM = functools.partial(pl.BlockSpec, memory_space=pltpu.SMEM)
ROWS = (128, 32)


def params(mib, **kw):
    return pltpu.CompilerParams(vmem_limit_bytes=mib << 20, **kw)


def cost(flops, nbytes):
    return pl.CostEstimate(flops=flops, bytes_accessed=nbytes, transcendentals=0)


def keep_row(ext, t, width):
    lane = lax.broadcasted_iota(jnp.int32, (1, width), 1)
    return (lane < ext[t]).astype(F32).astype(BF16)


def pack_kernel(masked, ext, x_ref, o_ref):
    triples, _, width = x_ref.shape
    main = width // 128 * 128
    tail = width - main
    for t in range(0, triples, 2):
        pair = []
        for u in (t, t + 1):
            x = x_ref[u]
            if masked:
                x = x * keep_row(ext, u, width)
            o_ref[:, u * main : (u + 1) * main] = x[:, :main]
            pair.append(x[:, main:])
        at = triples * main + t * tail
        o_ref[:, at : at + 2 * tail] = jnp.concatenate(pair, axis=1)


def pack(x, ext, start, rows, masked):
    triples, _, width = x.shape
    return pl.pallas_call(
        functools.partial(pack_kernel, masked),
        grid=(1,),
        in_specs=[SMEM(), pl.BlockSpec((triples, rows, width), lambda i: (0, start // rows, 0))],
        out_specs=pl.BlockSpec((rows, triples * width), lambda i: (0, 0)),
        out_shape=jax.ShapeDtypeStruct((rows, triples * width), BF16),
        compiler_params=params(16),
        cost_estimate=cost(triples * rows * width * 2, triples * rows * width * 4),
        name="pack",
    )(ext, x)


def gram_kernel(x_ref, y_ref, o_ref):
    o_ref[...] = lax.dot_general(x_ref[...], y_ref[...], NT, preferred_element_type=F32)


def gram(x, y):
    m, n, k = x.shape[0], y.shape[0], x.shape[1]
    return pl.pallas_call(
        gram_kernel,
        in_specs=[VMEM(), VMEM()],
        out_specs=VMEM(),
        out_shape=jax.ShapeDtypeStruct((m, n), F32),
        compiler_params=params(16),
        cost_estimate=cost(2 * m * n * k, 2 * (m + n) * k),
        name="gram",
    )(x, y)


def base_kernel(step, scale, ext, lam_ref, amp_ref, cyc_ref, wl_ref, den_ref, o_ref):
    i = pl.program_id(0)
    width = lam_ref.shape[2]
    main = width // 128 * 128
    tail = width - main
    den = den_ref[...]
    for u in range(step):
        t = i * step + u
        lam = lam_ref[u] * keep_row(ext, t, width)
        mid = lax.dot_general(amp_ref[u], cyc_ref[...], NT, preferred_element_type=F32).astype(BF16)
        both = jnp.concatenate([lam, mid], axis=1)
        near = lax.dot_general(both, wl_ref[...], NT, preferred_element_type=F32)
        o_ref[u] = near + jnp.dot(den, lam, preferred_element_type=F32) * scale


def base(lam, amp, ext, cyc, wl, den, scale, step=4):
    triples, rows, width = lam.shape
    block = pl.BlockSpec((step, rows, width), lambda i: (i, 0, 0))
    whole = lambda x: pl.BlockSpec(x.shape, lambda i: (0, 0))
    return pl.pallas_call(
        functools.partial(base_kernel, step, scale),
        grid=(triples // step,),
        in_specs=[SMEM(), block, block, whole(cyc), whole(wl), whole(den)],
        out_specs=block,
        out_shape=jax.ShapeDtypeStruct(lam.shape, F32),
        compiler_params=params(24),
        cost_estimate=cost(2 * triples * rows * width * (width + 64 + rows), triples * rows * width * 8),
        name="near",
    )(ext, lam, amp, cyc, wl, den)


def last_kernel(scale, den_ref, *refs):
    *got, base_ref, _, o_ref = refs
    triples, rows, width = base_ref.shape
    main = width // 128 * 128
    tail = width - main
    den = den_ref[...]

    def product(lo, size):
        total, at = None, 0
        for g in got:
            k = g.shape[0]
            part = jnp.dot(den[:, at : at + k], g[:, lo : lo + size], preferred_element_type=F32)
            total = part if total is None else total + part
            at += k
        return total * scale

    for t in range(0, triples, 2):
        ends = product(triples * main + t * tail, 2 * tail)
        for u in (t, t + 1):
            s = (u - t) * tail
            o_ref[u, :, :main] = (base_ref[u, :, :main] + product(u * main, main)).astype(BF16)
            o_ref[u, :, main:] = (base_ref[u, :, main:] + ends[:, s : s + tail]).astype(BF16)


def last(den, got, near, out, start, scale):
    triples, _, width = near.shape
    rows = den.shape[0]
    block = pl.BlockSpec((triples, rows, width), lambda i: (0, start // rows, 0))
    whole = lambda x: pl.BlockSpec(x.shape, lambda i: (0, 0))
    if out is None:
        out, spec, alias = jnp.zeros((8, 128), BF16), pl.BlockSpec((8, 128), lambda i: (0, 0)), {}
    else:
        spec, alias = pl.BlockSpec(memory_space=pl.ANY), {len(got) + 2: 0}
    return pl.pallas_call(
        functools.partial(last_kernel, scale),
        grid=(1,),
        in_specs=[whole(den), *map(whole, got), block, spec],
        out_specs=block,
        out_shape=jax.ShapeDtypeStruct(near.shape, BF16),
        input_output_aliases=alias,
        compiler_params=params(32),
        cost_estimate=cost(2 * triples * rows * width * 160, triples * rows * width * 6),
        name="last",
    )(den, *got, near, out)


def permute(x, flip, swap=0):
    n, v = lax.axis_size("occ"), lax.axis_size("vir")
    if not swap:
        return lax.ppermute(x, "occ", [(i, i ^ flip) for i in range(n)])
    return lax.ppermute(x, ("occ", "vir"), [(i * v + j, (i ^ flip) * v + (j ^ swap)) for i in range(n) for j in range(v)])


def total_of(x, swap):
    n = lax.axis_size("occ")
    x = x + permute(x, 1)
    if swap:
        x = permute(x, 0, 1) + permute(x, 2, 1)
    else:
        x = x + permute(x, 2)
    bit = 4
    while bit < n:
        if 2 * bit < n:
            x = (x + permute(x, bit)) + (permute(x, 2 * bit) + permute(x, 3 * bit))
            bit *= 4
        else:
            x = x + permute(x, bit)
            bit *= 2
    return x


def on_device(lam, amp, ext, ladder, cycle, doubles):
    triples, rows, width = lam.shape
    all_triples = triples * lax.axis_size("occ")
    norm = jnp.sqrt(F32(all_triples * width))
    scale = 1.0 / float(width) ** 0.5
    vir = lax.axis_index("vir")

    starts = [sum(ROWS[:k]) for k in range(len(ROWS))]
    own = [pack(lam, ext, s, r, True) for s, r in zip(starts, ROWS)]
    got = [permute(x, 0, 1) for x in own]

    pad = jnp.zeros((rows, 128 - width % 128 - doubles.shape[0]), BF16)
    wl_own = jnp.concatenate([ladder.T, doubles.T, pad], axis=1)
    wl_got = permute(wl_own, 0, 1)
    wl = jnp.where(vir == 0, jnp.concatenate([wl_own, wl_got]), jnp.concatenate([wl_got, wl_own]))
    cyc = jnp.pad(cycle.T, ((0, 64 - cycle.shape[1]), (0, 0)))

    amp_all = pack(amp, ext, 0, rows, False)
    own_part = jnp.concatenate([gram(x, amp_all) for x in own])
    own_den = (total_of(own_part, 0) / norm).astype(BF16)
    near = base(lam, amp, ext, cyc, wl, own_den, scale)

    out = None
    for g, s in zip(got, starts):
        den = (total_of(gram(g, amp_all), 1) / norm).astype(BF16)
        out = last(den, got, near, out, s, scale)
    return out


def solution(mesh):
    return jax.shard_map(
        on_device,
        mesh=mesh,
        in_specs=(
            P("occ", "vir", None),
            P("occ", "vir", None),
            P("occ"),
            P(None, "vir"),
            P(),
            P(None, "vir"),
        ),
        out_specs=P("occ", "vir", None),
        check_vma=False,
    )
```

time: 228 us -> 81.9 us (0.36)
  waiting for transfers between devices: 176 us -> 28.5 us
  starting transfers between devices: 0.08 us -> 26.4 us
  matrix products: 21.4 us -> 0 us
  Pallas kernels: 0 us -> 17.2 us
  between operations: 13.1 us -> 0.21 us
  blocking collectives: 12.7 us -> 0 us
  local copies, waits for them, and re-layouts: 0.14 us -> 3.15 us
  other arithmetic: 3.77 us -> 6.19 us
    psum x1 -> x0, waiting for transfers between devices: 91.6 us -> none  [on_device(): density = lax.psum(partial_density, 'occ')]
    all_gather x2 -> x0, waiting for transfers between devices: 83.5 us -> none  [the longest x1 46.9 us: on_device(): lax.all_gather(masked, 'vir', axis=1, tiled=True)]
    ppermute x0 -> x20, waiting for transfers between devices: none -> 28.5 us  [the longest x7 16.3 us: permute(): lax.ppermute(x, ('occ', 'vir'), [(i * v + j, (i ^ flip) * v + (j ^ swap))...]
    ppermute x0 -> x20, starting transfers between devices: none -> 26.4 us  [the longest x13 16.3 us: permute(): return lax.ppermute(x, 'occ', [(i, i ^ flip) for i in range(n)])]
    dot_general x4 -> x0, matrix products: 21.4 us -> none  [the longest x1 6.98 us: on_device(): jnp.einsum('ac,tcb->tab', density, lax.all_gather(masked, 'vir', axis=1,...]
    pallas_call x0 -> x10, Pallas kernels: none -> 17.2 us  [the longest x1 5.31 us: base(): pl.pallas_call(functools.partial(base_kernel, step, scale), grid=(triples...]
    all_gather x2 -> x0, blocking collectives: 12.7 us -> none  [the longest x1 7.17 us: on_device(): lax.all_gather(ladder_weight, 'vir', axis=1, tiled=True)]
    add x0 -> x6, other arithmetic: none -> 2.66 us  [the longest x3 1.62 us: total_of(): x = x + permute(x, 1)]
  transfers between devices with their start and end apart: 3 -> 20, of which waited for: 3 -> 7; matrix products, arithmetic and copies ran while one was open for 8% -> 9% of each run, Pallas kernels for 0% -> 15%
where the time goes in v1:
time: 81.9 us; the launch traced here: 81.5 us
  waiting for transfers between devices  28.5 us (35%)
  starting transfers between devices  26.4 us (32%)
  Pallas kernels  17.2 us (21%)
  other arithmetic  6.19 us (8%)
  local copies, waits for them, and re-layouts  3.15 us (4%)
    ppermute x13, starting transfers between devices, permute(): return lax.ppermute(x, 'occ', [(i, i ^ flip) for i in range(n)])  16.3 us
    ppermute x7, waiting for transfers between devices, permute(): lax.ppermute(x, ('occ', 'vir'), [(i * v + j, (i ^ flip) * v + (j ^ swap))...  16.3 us
    ppermute x13, waiting for transfers between devices, permute(): return lax.ppermute(x, 'occ', [(i, i ^ flip) for i in range(n)])  12.2 us
    ppermute x7, starting transfers between devices, permute(): lax.ppermute(x, ('occ', 'vir'), [(i * v + j, (i ^ flip) * v + (j ^ swap))...  10.1 us
    pallas_call x1, Pallas kernels, base(): pl.pallas_call(functools.partial(base_kernel, step, scale), grid=(triples...  5.31 us
    pallas_call x4, Pallas kernels, gram(): pl.pallas_call(gram_kernel, in_specs=[VMEM(), VMEM()], out_specs=VMEM(),...  4.71 us
    pallas_call x3, Pallas kernels, pack(): pl.pallas_call(functools.partial(pack_kernel, masked), grid=(1,), in_spec...  3.96 us
    pallas_call x2, Pallas kernels, last(): pl.pallas_call(functools.partial(last_kernel, scale), grid=(1,), in_specs...  3.19 us
  transfers between devices with their start and end apart: 20, of which 7 were waited for; matrix products, arithmetic and copies ran while one was open for 9% of the time, Pallas kernels for 15%

profile of v1, /device:TPU:0, one launch (start us, length us, event | category | flops | bytes accessed | tf_op | source)
XLA Modules:
  0.0 81.5 jit_solution(15671888692694339102)
XLA Ops:
  0.0 1.5 %copy-done = bf16[16,160,320]{2,1,0:T(8,128)(2,1)S(1)} copy-done((bf16[16,160,320]{2,1,0:T(8,128)(2,1)S(1)}, bf16[16,160,320]{2,1,0:T(8,128)(2,1)}, u32[]{:S(2)}) %copy-start) | copy-done | bytes 1638424
  1.5 0.7 copy-done.4
  2.2 1.8 %pack.5.x_ref = bf16[128,5120]{1,0:T(8,128)(2,1)} custom-call(s32[16]{0:T(128)S(1)} %copy-done.4, bf16[16,160,320]{2,1,0:T(8,128)(2,1)S(1)} %copy-done), custom_call_target="tpu_custom_call" | custom-call | flops 1310720 | bytes 2621440 | tf_op jit(solution)/shard_map/pack/pallas_call | solution.py:48
  4.0 2.9 %collective-permute-start.7 = (bf16[128,5120]{1,0:T(8,128)(2,1)}, bf16[128,5120]{1,0:T(8,128)(2,1)S(1)}, u32[]{:S(2)}, u32[]{:S(2)}) collective-permute-start(bf16[128,5120]{1,0:T(8,128)(2,1)} %pack.5.x_ref), channel_id=1, source_target_pairs={{0,1},{1,0},{2,3},{3,2},{4,5},{5,4},{6,7},{7,6},{8,9},{9,8},{10,11... | collective-permute-start | bytes 3932168 | tf_op jit(solution)/shard_map/ppermute | solution.py:158
  6.9 1.4 %pack.3.x_ref = bf16[32,5120]{1,0:T(8,128)(2,1)} custom-call(s32[16]{0:T(128)S(1)} %copy-done.4, bf16[16,160,320]{2,1,0:T(8,128)(2,1)S(1)} %copy-done), custom_call_target="tpu_custom_call" | custom-call | flops 327680 | bytes 655360 | tf_op jit(solution)/shard_map/pack/pallas_call | solution.py:48
  8.3 0.0 collective-permute-start
  8.3 0.8 pack.4.y_ref
  9.1 1.5 %gram.6 = f32[32,160]{1,0:T(8,128)S(1)} custom-call(bf16[32,5120]{1,0:T(8,128)(2,1)} %pack.3.x_ref, bf16[160,5120]{1,0:T(8,128)(2,1)S(1)} %pack.4.y_ref), custom_call_target="tpu_custom_call" | custom-call | flops 52428800 | bytes 1966080 | tf_op jit(solution)/shard_map/gram/pallas_call | solution.py:66
  10.7 0.0 copy-start.7
  10.7 2.0 %gram.5 = f32[128,160]{1,0:T(8,128)S(1)} custom-call(bf16[128,5120]{1,0:T(8,128)(2,1)} %pack.5.x_ref, bf16[160,5120]{1,0:T(8,128)(2,1)S(1)} %pack.4.y_ref), custom_call_target="tpu_custom_call" | custom-call | flops 209715200 | bytes 2949120 | tf_op jit(solution)/shard_map/gram/pallas_call | solution.py:66
  12.7 0.7 pad_maximum_fusion
  13.4 0.1 copy.8
  13.5 1.6 %pad_maximum_fusion.1 = bf16[160,384]{1,0:T(8,128)(2,1)} fusion(bf16[160,24]{1,0:T(8,128)(2,1)S(1)} %broadcast_in_dim.6, bf16[160,40]{1,0:T(8,128)(2,1)S(1)} %bitcast.5, bf16[160,320]{1,0:T(8,128)(2,1)} %bitcast.3), kind=kLoop, calls=%fused_computation.4 | loop fusion | flops 368640 | bytes 245760 | tf_op jit(solution)/shard_map/concatenate | solution.py:191
  15.1 2.0 %collective-permute-start.8 = (bf16[160,384]{1,0:T(8,128)(2,1)}, bf16[160,384]{1,0:T(8,128)(2,1)}, u32[]{:S(2)}, u32[]{:S(2)}) collective-permute-start(bf16[160,384]{1,0:T(8,128)(2,1)} %pad_maximum_fusion.1), channel_id=1, source_target_pairs={{0,1},{1,0},{2,3},{3,2},{4,5},{5,4},{6,7},{7,6},{8,9},{9,8},{10,11... | collective-permute-start | bytes 368648 | tf_op jit(solution)/shard_map/ppermute | solution.py:158
  17.2 1.6 %fusion = f32[160,160]{1,0:T(8,128)} fusion(f32[160,160]{1,0:T(8,128)} %collective-permute-done.9, f32[32,160]{1,0:T(8,128)S(1)} %gram.6, f32[128,160]{1,0:T(8,128)S(1)} %gram.5), kind=kLoop, calls=%fused_computation.6 | loop fusion | flops 51200 | bytes 307200 | tf_op jit(solution)/shard_map/add | solution.py:163
  18.8 1.5 %collective-permute-start.10 = (f32[160,160]{1,0:T(8,128)}, f32[160,160]{1,0:T(8,128)}, u32[]{:S(2)}, u32[]{:S(2)}) collective-permute-start(f32[160,160]{1,0:T(8,128)} %fusion), channel_id=1, source_target_pairs={{0,4},{2,6},{4,0},{6,2},{8,12},{10,14},{12,8},{14,10},{16,20},{18,... | collective-permute-start | bytes 307208 | tf_op jit(solution)/shard_map/ppermute | solution.py:157
  20.3 0.8 pad.4.cyc_ref
  21.0 4.4 %collective-permute-done.10 = f32[160,160]{1,0:T(8,128)} collective-permute-done((f32[160,160]{1,0:T(8,128)}, f32[160,160]{1,0:T(8,128)}, u32[]{:S(2)}, u32[]{:S(2)}) %collective-permute-start.10) | collective-permute-done | bytes 102432 | tf_op jit(solution)/shard_map/ppermute | solution.py:157
  25.4 1.0 %add.53 = f32[160,160]{1,0:T(8,128)S(1)} add(f32[160,160]{1,0:T(8,128)} %fusion, f32[160,160]{1,0:T(8,128)} %collective-permute-done.10) | non-fusion elementwise | flops 25600 | bytes 307200 | tf_op jit(solution)/shard_map/add | solution.py:167
  26.4 3.7 %collective-permute-start.13 = (f32[160,160]{1,0:T(8,128)S(1)}, f32[160,160]{1,0:T(8,128)S(1)}, u32[]{:S(2)}, u32[]{:S(2)}) collective-permute-start(f32[160,160]{1,0:T(8,128)S(1)} %add.53), channel_id=1, source_target_pairs={{0,24},{2,26},{4,28},{6,30},{8,16},{10,18},{12,20},{14,22},{16,8},... | collective-permute-start | bytes 307208 | tf_op jit(solution)/shard_map/ppermute | solution.py:157
  30.1 0.0 collective-permute-start.12
  30.1 13.7 %collective-permute-done.x_ref.refs_1_ = bf16[32,5120]{1,0:T(8,128)(2,1)S(1)} collective-permute-done((bf16[32,5120]{1,0:T(8,128)(2,1)}, bf16[32,5120]{1,0:T(8,128)(2,1)S(1)}, u32[]{:S(2)}, u32[]{:S(2)}) %collective-permute-start) | collective-permute-done | bytes 327712 | tf_op jit(solution)/shard_map/ppermute | solution.py:158
  43.8 2.1 %collective-permute-start.11 = (f32[160,160]{1,0:T(8,128)S(1)}, f32[160,160]{1,0:T(8,128)S(1)}, u32[]{:S(2)}, u32[]{:S(2)}) collective-permute-start(f32[160,160]{1,0:T(8,128)S(1)} %add.53), channel_id=1, source_target_pairs={{0,8},{2,10},{4,12},{6,14},{8,0},{10,2},{12,4},{14,6},{16,24},{18,... | collective-permute-start | bytes 307208 | tf_op jit(solution)/shard_map/ppermute | solution.py:157
  45.9 0.6 gram.4
  46.5 0.0 collective-permute-done.8
  46.5 0.1 collective-permute-start.1
  46.6 1.1 %maximum_select_fusion.wl_ref = bf16[320,384]{1,0:T(8,128)(2,1)S(1)} fusion(bf16[160,384]{1,0:T(8,128)(2,1)} %collective-permute-done.8, bf16[160,24]{1,0:T(8,128)(2,1)S(1)} %broadcast_in_dim.6, bf16[160,40]{1,0:T(8,128)(2,1)S(1)} %bitcast.6, bf16[160,320]{1,0:T(8,128)(2,1)S(1)} %bitcast.4, pred[]{:T(512)S(6)} %eq.3), kind=kLoop, calls=%fused_computation | loop fusion | flops 2088960 | bytes 491521 | tf_op jit(solution)/shard_map/jit(_where)/select_n | solution.py:193
  47.7 0.1 collective-permute-done.1
  47.8 0.0 copy-start.3
  47.8 0.0 copy-start.5
  47.8 2.5 %collective-permute-start.3 = (f32[32,160]{1,0:T(8,128)S(1)}, f32[32,160]{1,0:T(8,128)S(1)}, u32[]{:S(2)}, u32[]{:S(2)}) collective-permute-start(f32[32,160]{1,0:T(8,128)S(1)} %add.47), channel_id=1, source_target_pairs={{0,5},{1,4},{2,7},{3,6},{4,1},{5,0},{6,3},{7,2},{8,13},{9,12},{10,... | collective-permute-start | bytes 61448 | tf_op jit(solution)/shard_map/ppermute | solution.py:158
  50.4 0.5 collective-permute-start.2
  50.9 0.6 gram.7
  51.6 0.1 collective-permute-start.14
  51.6 0.0 collective-permute-done.12
  51.7 1.0 %collective-permute-done.3 = f32[32,160]{1,0:T(8,128)S(1)} collective-permute-done((f32[32,160]{1,0:T(8,128)S(1)}, f32[32,160]{1,0:T(8,128)S(1)}, u32[]{:S(2)}, u32[]{:S(2)}) %collective-permute-start.3) | collective-permute-done | bytes 20512 | tf_op jit(solution)/shard_map/ppermute | solution.py:158
  52.7 1.6 %collective-permute-done.2 = f32[32,160]{1,0:T(8,128)S(1)} collective-permute-done((f32[32,160]{1,0:T(8,128)S(1)}, f32[32,160]{1,0:T(8,128)S(1)}, u32[]{:S(2)}, u32[]{:S(2)}) %collective-permute-start.2) | collective-permute-done | bytes 20512 | tf_op jit(solution)/shard_map/ppermute | solution.py:158
  54.3 2.9 %collective-permute-start.6 = (f32[32,160]{1,0:T(8,128)S(1)}, f32[32,160]{1,0:T(8,128)S(1)}, u32[]{:S(2)}, u32[]{:S(2)}) collective-permute-start(f32[32,160]{1,0:T(8,128)S(1)} %add.48), channel_id=1, source_target_pairs={{0,24},{2,26},{4,28},{6,30},{8,16},{10,18},{12,20},{14,22},{16,8},... | collective-permute-start | bytes 61448 | tf_op jit(solution)/shard_map/ppermute | solution.py:157
  57.2 1.4 %collective-permute-start.4 = (f32[32,160]{1,0:T(8,128)S(1)}, f32[32,160]{1,0:T(8,128)S(1)}, u32[]{:S(2)}, u32[]{:S(2)}) collective-permute-start(f32[32,160]{1,0:T(8,128)S(1)} %add.48), channel_id=1, source_target_pairs={{0,8},{2,10},{4,12},{6,14},{8,0},{10,2},{12,4},{14,6},{16,24},{18,... | collective-permute-start | bytes 61448 | tf_op jit(solution)/shard_map/ppermute | solution.py:157
  58.7 1.2 %collective-permute-start.16 = (f32[128,160]{1,0:T(8,128)S(1)}, f32[128,160]{1,0:T(8,128)S(1)}, u32[]{:S(2)}, u32[]{:S(2)}) collective-permute-start(f32[128,160]{1,0:T(8,128)S(1)} %add.57), channel_id=1, source_target_pairs={{0,5},{1,4},{2,7},{3,6},{4,1},{5,0},{6,3},{7,2},{8,13},{9,12},{10,... | collective-permute-start | bytes 245768 | tf_op jit(solution)/shard_map/ppermute | solution.py:158
  59.9 0.8 %collective-permute-start.15 = (f32[128,160]{1,0:T(8,128)S(1)}, f32[128,160]{1,0:T(8,128)S(1)}, u32[]{:S(2)}, u32[]{:S(2)}) collective-permute-start(f32[128,160]{1,0:T(8,128)S(1)} %add.57), channel_id=1, source_target_pairs={{0,1},{1,0},{2,3},{3,2},{4,5},{5,4},{6,7},{7,6},{8,9},{9,8},{10,11... | collective-permute-start | bytes 245768 | tf_op jit(solution)/shard_map/ppermute | solution.py:158
  60.7 5.3 %near.1.refs_2_ = f32[16,160,320]{2,1,0:T(8,128)S(1)} custom-call(s32[16]{0:T(128)S(1)} %copy-done.5, bf16[16,160,320]{2,1,0:T(8,128)(2,1)S(1)} %copy-done.1, bf16[16,160,320]{2,1,0:T(8,128)(2,1)S(1)} %copy-done.3, bf16[64,320]{1,0:T(8,128)(2,1)S(1)} %pad.4.cyc_ref, bf16[320,384]{1,0:T(8,128)(2,1)S(1)} %maximum_select_fusion.wl_ref, ...), custom_call_target="tpu_custom_call" | custom-call | flops 891289600 | bytes 6553600 | tf_op jit(solution)/shard_map/near/pallas_call | solution.py:96
  66.1 3.0 %collective-permute-start.19 = (f32[128,160]{1,0:T(8,128)S(1)}, f32[128,160]{1,0:T(8,128)S(1)}, u32[]{:S(2)}, u32[]{:S(2)}) collective-permute-start(f32[128,160]{1,0:T(8,128)S(1)} %add.58), channel_id=1, source_target_pairs={{0,24},{2,26},{4,28},{6,30},{8,16},{10,18},{12,20},{14,22},{16,8},... | collective-permute-start | bytes 245768 | tf_op jit(solution)/shard_map/ppermute | solution.py:157
  69.1 1.5 %collective-permute-start.17 = (f32[128,160]{1,0:T(8,128)S(1)}, f32[128,160]{1,0:T(8,128)S(1)}, u32[]{:S(2)}, u32[]{:S(2)}) collective-permute-start(f32[128,160]{1,0:T(8,128)S(1)} %add.58), channel_id=1, source_target_pairs={{0,8},{2,10},{4,12},{6,14},{8,0},{10,2},{12,4},{14,6},{16,24},{18,... | collective-permute-start | bytes 245768 | tf_op jit(solution)/shard_map/ppermute | solution.py:157
  70.6 3.6 %collective-permute-done.19 = f32[128,160]{1,0:T(8,128)S(1)} collective-permute-done((f32[128,160]{1,0:T(8,128)S(1)}, f32[128,160]{1,0:T(8,128)S(1)}, u32[]{:S(2)}, u32[]{:S(2)}) %collective-permute-start.19) | collective-permute-done | bytes 81952 | tf_op jit(solution)/shard_map/ppermute | solution.py:157
  74.2 4.1 %collective-permute-done.18 = f32[128,160]{1,0:T(8,128)S(1)} collective-permute-done((f32[128,160]{1,0:T(8,128)S(1)}, f32[128,160]{1,0:T(8,128)S(1)}, u32[]{:S(2)}, u32[]{:S(2)}) %collective-permute-start.18) | collective-permute-done | bytes 81952 | tf_op jit(solution)/shard_map/ppermute | solution.py:157
  78.4 2.0 %last.2.refs_3_ = bf16[16,160,320]{2,1,0:T(8,128)(2,1)} custom-call(bf16[128,160]{1,0:T(8,128)(2,1)S(1)} %multiply_convert_fusion.1.den_ref, bf16[128,5120]{1,0:T(8,128)(2,1)S(1)} %collective-permute-done.7.x_ref.refs_0_, bf16[32,5120]{1,0:T(8,128)(2,1)S(1)} %collective-permute-done.x_ref.refs_1_, f32[16,160,320]{2,1,0:T(8,128)S(1)} %near.1.refs_2_, ...), custom_call_target="tpu_custom_call" | custom-call | flops 209715200 | bytes 3932160 | tf_op jit(solution)/shard_map/last/pallas_call | solution.py:141
  80.3 1.2 %last.3 = bf16[16,160,320]{2,1,0:T(8,128)(2,1)} custom-call(bf16[32,160]{1,0:T(8,128)(2,1)S(1)} %multiply_convert_fusion.2.den_ref, bf16[128,5120]{1,0:T(8,128)(2,1)S(1)} %collective-permute-done.7.x_ref.refs_0_, bf16[32,5120]{1,0:T(8,128)(2,1)S(1)} %collective-permute-done.x_ref.refs_1_, ...), custom_call_target="tpu_custom_call", output_to_operand_aliasing={{}: (4, {})} | custom-call | flops 52428800 | bytes 983040 | tf_op jit(solution)/shard_map/last/pallas_call | solution.py:141
  (34 shorter events, 0.2 us)
Async XLA Ops:
  0.0 1.5 %copy-start = (bf16[16,160,320]{2,1,0:T(8,128)(2,1)S(1)}, bf16[16,160,320]{2,1,0:T(8,128)(2,1)}, u32[]{:S(2)}) copy-start(bf16[16,160,320]{2,1,0:T(8,128)(2,1)} %lam_ref.1) | copy-start | bytes 4915204
  1.5 0.7 copy-start.4
  4.0 4.3 %copy-start.2 = (bf16[16,160,320]{2,1,0:T(8,128)(2,1)S(1)}, bf16[16,160,320]{2,1,0:T(8,128)(2,1)}, u32[]{:S(2)}) copy-start(bf16[16,160,320]{2,1,0:T(8,128)(2,1)} %amp_ref.1) | copy-start | bytes 4915204
  4.0 46.4 %collective-permute-start.7 = (bf16[128,5120]{1,0:T(8,128)(2,1)}, bf16[128,5120]{1,0:T(8,128)(2,1)S(1)}, u32[]{:S(2)}, u32[]{:S(2)}) collective-permute-start(bf16[128,5120]{1,0:T(8,128)(2,1)} %pack.5.x_ref), channel_id=1, source_target_pairs={{0,1},{1,0},{2,3},{3,2},{4,5},{5,4},{6,7},{7,6},{8,9},{9,8},{10,11... | collective-permute-start | bytes 3932168 | tf_op jit(solution)/shard_map/ppermute | solution.py:158
  8.3 35.5 %collective-permute-start = (bf16[32,5120]{1,0:T(8,128)(2,1)}, bf16[32,5120]{1,0:T(8,128)(2,1)S(1)}, u32[]{:S(2)}, u32[]{:S(2)}) collective-permute-start(bf16[32,5120]{1,0:T(8,128)(2,1)} %pack.3.x_ref), channel_id=1, source_target_pairs={{0,1},{1,0},{2,3},{3,2},{4,5},{5,4},{6,7},{7,6},{8,9},{9,8},{10,11... | collective-permute-start | bytes 983048 | tf_op jit(solution)/shard_map/ppermute | solution.py:158
  10.7 2.7 %copy-start.7 = (bf16[40,160]{1,0:T(8,128)(2,1)S(1)}, bf16[40,160]{1,0:T(8,128)(2,1)}, u32[]{:S(2)}) copy-start(bf16[40,160]{1,0:T(8,128)(2,1)} %param.11) | copy-start | bytes 38404
  13.4 3.8 %collective-permute-start.9 = (f32[160,160]{1,0:T(8,128)}, f32[160,160]{1,0:T(8,128)}, u32[]{:S(2)}, u32[]{:S(2)}) collective-permute-start(f32[160,160]{1,0:T(8,128)} %pad_maximum_fusion), channel_id=1, source_target_pairs={{0,2},{2,0},{4,6},{6,4},{8,10},{10,8},{12,14},{14,12},{16,18},{18,... | collective-permute-start | bytes 307208 | tf_op jit(solution)/shard_map/ppermute | solution.py:157
  15.1 31.4 %collective-permute-start.8 = (bf16[160,384]{1,0:T(8,128)(2,1)}, bf16[160,384]{1,0:T(8,128)(2,1)}, u32[]{:S(2)}, u32[]{:S(2)}) collective-permute-start(bf16[160,384]{1,0:T(8,128)(2,1)} %pad_maximum_fusion.1), channel_id=1, source_target_pairs={{0,1},{1,0},{2,3},{3,2},{4,5},{5,4},{6,7},{7,6},{8,9},{9,8},{10,11... | collective-permute-start | bytes 368648 | tf_op jit(solution)/shard_map/ppermute | solution.py:158
  18.8 27.9 %copy-start.6 = (bf16[320,160]{0,1:T(8,128)(2,1)S(1)}, bf16[320,160]{0,1:T(8,128)(2,1)}, u32[]{:S(2)}) copy-start(bf16[320,160]{0,1:T(8,128)(2,1)} %param.9) | copy-start | bytes 307204
  18.8 6.6 %collective-permute-start.10 = (f32[160,160]{1,0:T(8,128)}, f32[160,160]{1,0:T(8,128)}, u32[]{:S(2)}, u32[]{:S(2)}) collective-permute-start(f32[160,160]{1,0:T(8,128)} %fusion), channel_id=1, source_target_pairs={{0,4},{2,6},{4,0},{6,2},{8,12},{10,14},{12,8},{14,10},{16,20},{18,... | collective-permute-start | bytes 307208 | tf_op jit(solution)/shard_map/ppermute | solution.py:157
  26.4 25.1 %collective-permute-start.13 = (f32[160,160]{1,0:T(8,128)S(1)}, f32[160,160]{1,0:T(8,128)S(1)}, u32[]{:S(2)}, u32[]{:S(2)}) collective-permute-start(f32[160,160]{1,0:T(8,128)S(1)} %add.53), channel_id=1, source_target_pairs={{0,24},{2,26},{4,28},{6,30},{8,16},{10,18},{12,20},{14,22},{16,8},... | collective-permute-start | bytes 307208 | tf_op jit(solution)/shard_map/ppermute | solution.py:157
  30.1 21.5 %collective-permute-start.12 = (f32[160,160]{1,0:T(8,128)S(1)}, f32[160,160]{1,0:T(8,128)S(1)}, u32[]{:S(2)}, u32[]{:S(2)}) collective-permute-start(f32[160,160]{1,0:T(8,128)S(1)} %add.53), channel_id=1, source_target_pairs={{0,16},{2,18},{4,20},{6,22},{8,24},{10,26},{12,28},{14,30},{16,0},... | collective-permute-start | bytes 307208 | tf_op jit(solution)/shard_map/ppermute | solution.py:157
  43.8 7.9 %collective-permute-start.11 = (f32[160,160]{1,0:T(8,128)S(1)}, f32[160,160]{1,0:T(8,128)S(1)}, u32[]{:S(2)}, u32[]{:S(2)}) collective-permute-start(f32[160,160]{1,0:T(8,128)S(1)} %add.53), channel_id=1, source_target_pairs={{0,8},{2,10},{4,12},{6,14},{8,0},{10,2},{12,4},{14,6},{16,24},{18,... | collective-permute-start | bytes 307208 | tf_op jit(solution)/shard_map/ppermute | solution.py:157
  46.5 1.3 %collective-permute-start.1 = (f32[32,160]{1,0:T(8,128)S(1)}, f32[32,160]{1,0:T(8,128)S(1)}, u32[]{:S(2)}, u32[]{:S(2)}) collective-permute-start(f32[32,160]{1,0:T(8,128)S(1)} %gram.4), channel_id=1, source_target_pairs={{0,2},{2,0},{4,6},{6,4},{8,10},{10,8},{12,14},{14,12},{16,18},{18,... | collective-permute-start | bytes 61448 | tf_op jit(solution)/shard_map/ppermute | solution.py:157
  47.8 12.9 %copy-start.1 = (bf16[16,160,320]{2,1,0:T(8,128)(2,1)S(1)}, bf16[16,160,320]{2,1,0:T(8,128)(2,1)}, u32[]{:S(2)}) copy-start(bf16[16,160,320]{2,1,0:T(8,128)(2,1)} %lam_ref.1) | copy-start | bytes 4915204
  47.8 12.9 %copy-start.3 = (bf16[16,160,320]{2,1,0:T(8,128)(2,1)S(1)}, bf16[16,160,320]{2,1,0:T(8,128)(2,1)}, u32[]{:S(2)}) copy-start(bf16[16,160,320]{2,1,0:T(8,128)(2,1)} %amp_ref.1) | copy-start | bytes 4915204
  47.8 12.9 %copy-start.5 = (s32[16]{0:T(128)S(1)}, s32[16]{0:T(128)}, u32[]{:S(2)}) copy-start(s32[16]{0:T(128)} %ext.7) | copy-start | bytes 196
  47.8 4.9 %collective-permute-start.3 = (f32[32,160]{1,0:T(8,128)S(1)}, f32[32,160]{1,0:T(8,128)S(1)}, u32[]{:S(2)}, u32[]{:S(2)}) collective-permute-start(f32[32,160]{1,0:T(8,128)S(1)} %add.47), channel_id=1, source_target_pairs={{0,5},{1,4},{2,7},{3,6},{4,1},{5,0},{6,3},{7,2},{8,13},{9,12},{10,... | collective-permute-start | bytes 61448 | tf_op jit(solution)/shard_map/ppermute | solution.py:158
  50.4 3.9 %collective-permute-start.2 = (f32[32,160]{1,0:T(8,128)S(1)}, f32[32,160]{1,0:T(8,128)S(1)}, u32[]{:S(2)}, u32[]{:S(2)}) collective-permute-start(f32[32,160]{1,0:T(8,128)S(1)} %add.47), channel_id=1, source_target_pairs={{0,1},{1,0},{2,3},{3,2},{4,5},{5,4},{6,7},{7,6},{8,9},{9,8},{10,11... | collective-permute-start | bytes 61448 | tf_op jit(solution)/shard_map/ppermute | solution.py:158
  51.6 7.1 %collective-permute-start.14 = (f32[128,160]{1,0:T(8,128)S(1)}, f32[128,160]{1,0:T(8,128)S(1)}, u32[]{:S(2)}, u32[]{:S(2)}) collective-permute-start(f32[128,160]{1,0:T(8,128)S(1)} %gram.7), channel_id=1, source_target_pairs={{0,2},{2,0},{4,6},{6,4},{8,10},{10,8},{12,14},{14,12},{16,18},{18,... | collective-permute-start | bytes 245768 | tf_op jit(solution)/shard_map/ppermute | solution.py:157
  54.3 14.8 %collective-permute-start.6 = (f32[32,160]{1,0:T(8,128)S(1)}, f32[32,160]{1,0:T(8,128)S(1)}, u32[]{:S(2)}, u32[]{:S(2)}) collective-permute-start(f32[32,160]{1,0:T(8,128)S(1)} %add.48), channel_id=1, source_target_pairs={{0,24},{2,26},{4,28},{6,30},{8,16},{10,18},{12,20},{14,22},{16,8},... | collective-permute-start | bytes 61448 | tf_op jit(solution)/shard_map/ppermute | solution.py:157
  57.2 13.3 %collective-permute-start.5 = (f32[32,160]{1,0:T(8,128)S(1)}, f32[32,160]{1,0:T(8,128)S(1)}, u32[]{:S(2)}, u32[]{:S(2)}) collective-permute-start(f32[32,160]{1,0:T(8,128)S(1)} %add.48), channel_id=1, source_target_pairs={{0,16},{2,18},{4,20},{6,22},{8,24},{10,26},{12,28},{14,30},{16,0},... | collective-permute-start | bytes 61448 | tf_op jit(solution)/shard_map/ppermute | solution.py:157
  57.2 13.3 %collective-permute-start.4 = (f32[32,160]{1,0:T(8,128)S(1)}, f32[32,160]{1,0:T(8,128)S(1)}, u32[]{:S(2)}, u32[]{:S(2)}) collective-permute-start(f32[32,160]{1,0:T(8,128)S(1)} %add.48), channel_id=1, source_target_pairs={{0,8},{2,10},{4,12},{6,14},{8,0},{10,2},{12,4},{14,6},{16,24},{18,... | collective-permute-start | bytes 61448 | tf_op jit(solution)/shard_map/ppermute | solution.py:157
  58.7 7.4 %collective-permute-start.16 = (f32[128,160]{1,0:T(8,128)S(1)}, f32[128,160]{1,0:T(8,128)S(1)}, u32[]{:S(2)}, u32[]{:S(2)}) collective-permute-start(f32[128,160]{1,0:T(8,128)S(1)} %add.57), channel_id=1, source_target_pairs={{0,5},{1,4},{2,7},{3,6},{4,1},{5,0},{6,3},{7,2},{8,13},{9,12},{10,... | collective-permute-start | bytes 245768 | tf_op jit(solution)/shard_map/ppermute | solution.py:158
  59.9 6.2 %collective-permute-start.15 = (f32[128,160]{1,0:T(8,128)S(1)}, f32[128,160]{1,0:T(8,128)S(1)}, u32[]{:S(2)}, u32[]{:S(2)}) collective-permute-start(f32[128,160]{1,0:T(8,128)S(1)} %add.57), channel_id=1, source_target_pairs={{0,1},{1,0},{2,3},{3,2},{4,5},{5,4},{6,7},{7,6},{8,9},{9,8},{10,11... | collective-permute-start | bytes 245768 | tf_op jit(solution)/shard_map/ppermute | solution.py:158
  66.1 8.1 %collective-permute-start.19 = (f32[128,160]{1,0:T(8,128)S(1)}, f32[128,160]{1,0:T(8,128)S(1)}, u32[]{:S(2)}, u32[]{:S(2)}) collective-permute-start(f32[128,160]{1,0:T(8,128)S(1)} %add.58), channel_id=1, source_target_pairs={{0,24},{2,26},{4,28},{6,30},{8,16},{10,18},{12,20},{14,22},{16,8},... | collective-permute-start | bytes 245768 | tf_op jit(solution)/shard_map/ppermute | solution.py:157
  69.1 9.2 %collective-permute-start.18 = (f32[128,160]{1,0:T(8,128)S(1)}, f32[128,160]{1,0:T(8,128)S(1)}, u32[]{:S(2)}, u32[]{:S(2)}) collective-permute-start(f32[128,160]{1,0:T(8,128)S(1)} %add.58), channel_id=1, source_target_pairs={{0,16},{2,18},{4,20},{6,22},{8,24},{10,26},{12,28},{14,30},{16,0},... | collective-permute-start | bytes 245768 | tf_op jit(solution)/shard_map/ppermute | solution.py:157
  69.1 9.2 %collective-permute-start.17 = (f32[128,160]{1,0:T(8,128)S(1)}, f32[128,160]{1,0:T(8,128)S(1)}, u32[]{:S(2)}, u32[]{:S(2)}) collective-permute-start(f32[128,160]{1,0:T(8,128)S(1)} %add.58), channel_id=1, source_target_pairs={{0,8},{2,10},{4,12},{6,14},{8,0},{10,2},{12,4},{14,6},{16,24},{18,... | collective-permute-start | bytes 245768 | tf_op jit(solution)/shard_map/ppermute | solution.py:157

commit v2 on v1

v2 whole, which is shorter than its diff:
```python
import functools

import jax
import jax.numpy as jnp
from jax import lax
from jax.experimental import pallas as pl
from jax.experimental.pallas import tpu as pltpu
from jax.sharding import PartitionSpec as P

F32, BF16 = jnp.float32, jnp.bfloat16
NT = (((1,), (1,)), ((), ()))
VMEM = functools.partial(pl.BlockSpec, memory_space=pltpu.VMEM)
SMEM = functools.partial(pl.BlockSpec, memory_space=pltpu.SMEM)
LATE = 64
EXTRA = 8


def params(mib, **kw):
    return pltpu.CompilerParams(vmem_limit_bytes=mib << 20, **kw)


def cost(flops, nbytes):
    return pl.CostEstimate(flops=flops, bytes_accessed=nbytes, transcendentals=0)


def whole(x):
    return pl.BlockSpec(x.shape, lambda i: (0,) * x.ndim)


def after(x, *others):
    return lax.optimization_barrier((x, *others))[0]


def pack_into(o_ref, x_ref, keep_ref=None):
    triples, _, width = x_ref.shape
    main = width // 128 * 128
    tail = width - main
    for t in range(0, triples, 2):
        pair = []
        for u in (t, t + 1):
            x = x_ref[u]
            if keep_ref is not None:
                x = x * keep_ref[u : u + 1, :].astype(BF16)
            o_ref[:, u * main : (u + 1) * main] = x[:, :main]
            pair.append(x[:, main:])
        at = triples * main + t * tail
        o_ref[:, at : at + 2 * tail] = jnp.concatenate(pair, axis=1)


def core_of():
    return lax.rem(lax.axis_index("occ"), 2)


def spread(x):
    return jnp.concatenate([x[i : i + EXTRA] for i in range(0, x.shape[0], EXTRA)], axis=1)


def gather_back(x, width):
    return jnp.concatenate([x[:, i : i + width] for i in range(0, x.shape[1], width)], axis=0)


def pack_kernel(x_ref, ladder_ref, doubles_ref, o_ref):
    rows = x_ref.shape[1]
    pack_into(o_ref.at[:rows], x_ref)
    half = ladder_ref.shape[0] // 2
    start = pl.multiple_of(core_of() * half, 16)
    parts = [spread(ladder_ref[pl.ds(start, half), :].astype(F32)), spread(doubles_ref[...].astype(F32))]
    used = sum(p.shape[1] for p in parts)
    parts.append(jnp.zeros((EXTRA, o_ref.shape[1] - used), F32))
    o_ref[rows:, :] = jnp.concatenate(parts, axis=1).astype(BF16)


def pack(x, ladder, doubles, start):
    triples, rows, width = x.shape
    rows = rows - start
    return pl.pallas_call(
        pack_kernel,
        grid=(1,),
        in_specs=[
            pl.BlockSpec((pl.Element(triples), pl.Element(rows), pl.Element(width)), lambda i: (0, start, 0)),
            whole(ladder),
            whole(doubles),
        ],
        out_specs=pl.BlockSpec((rows + EXTRA, triples * width), lambda i: (0, 0)),
        out_shape=jax.ShapeDtypeStruct((rows + EXTRA, triples * width), BF16),
        compiler_params=params(8),
        cost_estimate=cost(triples * rows * width * 2, triples * rows * width * 4),
        name="pack",
    )(x, ladder, doubles)


def fold(x):
    m = x.shape[0] // 4
    return jnp.concatenate([x[q * m : (q + 1) * m] for q in range(4)], axis=1)


def unfold(x):
    n = x.shape[1] // 4
    return jnp.concatenate([x[:, q * n : (q + 1) * n] for q in range(4)], axis=0)


def product_of(x, y):
    return lax.dot_general(x, y, NT, preferred_element_type=F32)


def prepare_kernel(lam_ref, early_ref, amp_ref, keep_ref, late_ref, all_ref, o_ref):
    pack_into(late_ref, lam_ref)
    pack_into(all_ref, amp_ref, keep_ref)
    y = all_ref[...]
    o_ref[...] = fold(jnp.concatenate([product_of(late_ref[...], y), product_of(early_ref[: y.shape[0] - LATE], y)]))


def prepare(lam, early, amp, keep):
    triples, rows, width = lam.shape
    size = triples * width
    return pl.pallas_call(
        prepare_kernel,
        grid=(1,),
        in_specs=[pl.BlockSpec((triples, LATE, width), lambda i: (0, 0, 0)), whole(early), whole(amp), whole(keep)],
        out_specs=[pl.BlockSpec(s, lambda i: (0, 0)) for s in ((LATE, size), (rows, size), (rows // 4, 4 * rows))],
        out_shape=[
            jax.ShapeDtypeStruct((LATE, size), BF16),
            jax.ShapeDtypeStruct((rows, size), BF16),
            jax.ShapeDtypeStruct((rows // 4, 4 * rows), F32),
        ],
        compiler_params=params(18),
        cost_estimate=cost(2 * rows * rows * size, 6 * rows * size),
        name="prepare",
    )(lam, early, amp, keep)


def gram_kernel(m, x_ref, y_ref, o_ref):
    o_ref[...] = fold(product_of(x_ref[:m], y_ref[...]))


def gram(x, y, m):
    n, k = y.shape
    return pl.pallas_call(
        functools.partial(gram_kernel, m),
        in_specs=[VMEM(), VMEM()],
        out_specs=VMEM(),
        out_shape=jax.ShapeDtypeStruct((m // 4, 4 * n), F32),
        compiler_params=params(8),
        cost_estimate=cost(2 * m * n * k, 2 * (m + n) * k),
        name="gram",
    )(x, y)


def near_kernel(
    step, norm, scale, keep_ref, lam_ref, amp_ref, cyc_ref, ladder_ref, doubles_ref, mine_ref, other_ref, den_ref, o_ref, w_ref, d_ref
):
    i = pl.program_id(0)
    half, width = ladder_ref.shape

    @pl.when(i == 0)
    def _():
        core, vir = core_of(), lax.axis_index("vir")
        size = half // 2 // EXTRA * width
        mine, other = mine_ref[...].astype(F32), other_ref[...].astype(F32)
        w_ref[pl.ds(pl.multiple_of(vir * half, 16), half), :] = ladder_ref[...]
        there = (1 - vir) * half
        for x, c in ((mine, core), (other, 1 - core)):
            at = pl.multiple_of(there + c * (half // 2), 16)
            w_ref[pl.ds(at, half // 2), :] = gather_back(x[:, :size], width).astype(BF16)
        own = doubles_ref[...].astype(F32)
        got = gather_back(mine[:, size : size + own.shape[0] // EXTRA * half], half)
        first = vir == 0
        d_ref[:, :half] = jnp.where(first, own, got).astype(BF16)
        d_ref[:, half:] = jnp.where(first, got, own).astype(BF16)

    den = (unfold(den_ref[...]) / norm).astype(BF16)
    for u in range(step):
        lam = lam_ref[u] * keep_ref[pl.ds(i * step + u, 1), :].astype(BF16)
        mid = product_of(amp_ref[u], cyc_ref[...]).astype(BF16)
        near = product_of(lam, w_ref[...]) + jnp.dot(mid, d_ref[...], preferred_element_type=F32)
        o_ref[u] = near + jnp.dot(den, lam, preferred_element_type=F32) * scale


def near_of(lam, amp, keep, cyc, ladder, doubles, mine, other, den, norm, scale, step=4):
    triples, rows, width = lam.shape
    block = pl.BlockSpec((step, rows, width), lambda i: (i, 0, 0))
    return pl.pallas_call(
        functools.partial(near_kernel, step, norm, scale),
        grid=(triples // step,),
        in_specs=[whole(keep), block, block, *map(whole, (cyc, ladder, doubles, mine, other, den))],
        out_specs=block,
        out_shape=jax.ShapeDtypeStruct(lam.shape, F32),
        scratch_shapes=[pltpu.VMEM((width, width), BF16), pltpu.VMEM((doubles.shape[0], width), BF16)],
        compiler_params=params(10),
        cost_estimate=cost(2 * triples * rows * width * (width + 64 + rows), triples * rows * width * 8),
        name="near",
    )(keep, lam, amp, cyc, ladder, doubles, mine, other, den)


def last_kernel(order, norm, scale, keep_ref, den_ref, *refs):
    *got, near_ref, _, o_ref = refs
    triples, rows, width = near_ref.shape
    got = [g[:n] for n, g in zip((LATE, den_ref.shape[1] // 4 - LATE), got)]
    main = width // 128 * 128
    tail = width - main
    den = unfold(den_ref[...].astype(F32))
    if norm is not None:
        den = den / norm
    den = den.astype(BF16)
    den = jnp.concatenate([den[:, s : s + g.shape[0]] for s, g in zip(order, got)], axis=1)
    all_got = jnp.concatenate(got, axis=0)

    def product(lo, size):
        return jnp.dot(den, all_got[:, lo : lo + size], preferred_element_type=F32) * scale

    for t in range(0, triples, 2):
        ends = product(triples * main + t * tail, 2 * tail)
        for u in (t, t + 1):
            s = (u - t) * tail
            keep = keep_ref[u : u + 1, :]
            o_ref[u, :, :main] = (near_ref[u, :, :main] + product(u * main, main) * keep[:, :main]).astype(BF16)
            o_ref[u, :, main:] = (near_ref[u, :, main:] + ends[:, s : s + tail] * keep[:, main:]).astype(BF16)


def last(keep, den, got, order, near, out, start, rows, norm, scale):
    triples, _, width = near.shape
    spec = pl.BlockSpec((pl.Element(triples), pl.Element(rows), pl.Element(width)), lambda i: (0, start, 0))
    if out is None:
        out, alias = jnp.zeros((8, 128), BF16), {}
    else:
        alias = {len(got) + 3: 0}
    return pl.pallas_call(
        functools.partial(last_kernel, order, norm, scale),
        in_specs=[whole(keep), whole(den), *map(whole, got), spec, pl.BlockSpec(memory_space=pl.ANY)],
        grid=(1,),
        out_specs=spec,
        out_shape=jax.ShapeDtypeStruct(near.shape, BF16),
        input_output_aliases=alias,
        compiler_params=params(14),
        cost_estimate=cost(2 * triples * rows * width * 160, triples * rows * width * 6),
        name="last",
    )(keep, den, *got, near, out)


def permute(x, flip, swap=0):
    n, v = lax.axis_size("occ"), lax.axis_size("vir")
    if not swap:
        return lax.ppermute(x, "occ", [(i, i ^ flip) for i in range(n)])
    return lax.ppermute(x, ("occ", "vir"), [(i * v + j, (i ^ flip) * v + (j ^ swap)) for i in range(n) for j in range(v)])


def far_sum(x):
    n = lax.axis_size("occ")
    bit = 4
    while bit < n:
        if 2 * bit < n:
            x = (x + permute(x, bit)) + (permute(x, 2 * bit) + permute(x, 3 * bit))
            bit *= 4
        else:
            x = x + permute(x, bit)
            bit *= 2
    return x


def near_sum(x):
    return (x + permute(x, 1)) + (permute(x, 2) + permute(x, 3))


def crossed_sum(x):
    x = x + permute(x, 1)
    return permute(x, 0, 1) + permute(x, 2, 1)


def on_device(lam, amp, ext, ladder, cycle, doubles):
    triples, rows, width = lam.shape
    all_triples = triples * lax.axis_size("occ")
    norm = float(all_triples * width) ** 0.5
    scale = 1.0 / float(width) ** 0.5
    early_rows = rows - LATE

    early_own = pack(lam, ladder.T, doubles, LATE)
    early_got = permute(early_own, 0, 1)
    keep = (lax.broadcasted_iota(jnp.int32, (triples, width), 1) < ext[:, None]).astype(F32)
    late_own, amp_all, own_den = prepare(lam, early_own, amp, keep)
    late_got = permute(late_own, 0, 1)

    own_den = near_sum(own_den)
    early_got = after(early_got, own_den)
    own_den = far_sum(own_den)

    early = near_sum(gram(early_got, amp_all, early_rows))
    mine = early_got[early_rows:]
    other = permute(mine, 1)
    near = near_of(lam, amp, keep, cycle.T, ladder.T, doubles, mine, other, after(own_den, early), norm, scale)

    early = far_sum(early)
    late_got = after(late_got, near)
    early = permute((early / norm).astype(BF16), 0, 1)
    late = crossed_sum(gram(late_got, amp_all, LATE))
    early = after(early, late)
    late = far_sum(late)

    order = (0, LATE)
    got = (late_got, early_got)
    out = last(keep, early, got, order, near, None, LATE, early_rows, None, scale)
    return last(keep, late, got, order, near, out, 0, LATE, norm, scale)


def solution(mesh):
    return jax.shard_map(
        on_device,
        mesh=mesh,
        in_specs=(
            P("occ", "vir", None),
            P("occ", "vir", None),
            P("occ"),
            P(None, "vir"),
            P(),
            P(None, "vir"),
        ),
        out_specs=P("occ", "vir", None),
        check_vma=False,
    )
```

time: 81.9 us -> 66.1 us (0.81)
  waiting for transfers between devices: 28.5 us -> 21.6 us
  other arithmetic: 6.19 us -> 0.19 us
  Pallas kernels: 17.2 us -> 11.8 us
  local copies, waits for them, and re-layouts: 3.15 us -> 4.78 us
    ppermute x7 -> x5, waiting for transfers between devices: 16.3 us -> 10.1 us  [permute(): lax.ppermute(x, ('occ', 'vir'), [(i * v + j, (i ^ flip) * v + (j ^ swap))...]
    pallas_call x10 -> x7, Pallas kernels: 17.2 us -> 11.8 us  [the longest x1 5.81 us: near_of(): pl.pallas_call(functools.partial(near_kernel, step, norm, scale), grid=(t...]
    ppermute x13 -> x17, starting transfers between devices: 16.3 us -> 19 us  [permute(): return lax.ppermute(x, 'occ', [(i, i ^ flip) for i in range(n)])]
    add x6, other arithmetic: 2.66 us -> 0.09 us  [the longest x2 0.04 us: near_sum(): return x + permute(x, 1) + (permute(x, 2) + permute(x, 3))]
    unnamed x17 -> x20, local copies, waits for them, and re-layouts: 2.37 us -> 4.77 us
    concatenate x2 -> x0, other arithmetic: 2.32 us -> none  [the longest x1 1.64 us: on_device(): wl_own = jnp.concatenate([ladder.T, doubles.T, pad], axis=1)]
    ppermute x7 -> x5, starting transfers between devices: 10.1 us -> 8.18 us  [permute(): lax.ppermute(x, ('occ', 'vir'), [(i * v + j, (i ^ flip) * v + (j ^ swap))...]
    select_n x1 -> x0, other arithmetic: 1.11 us -> none  [on_device(): jnp.where(vir == 0, jnp.concatenate([wl_own, wl_got]), jnp.concatenate([w...]
  transfers between devices with their start and end apart: 20 -> 22, of which waited for: 7 -> 9; matrix products, arithmetic and copies ran while one was open for 9% -> 0% of each run, Pallas kernels for 15% -> 15%
where the time goes in v2:
time: 66.1 us; the launch traced here: 65.8 us
  starting transfers between devices  27.2 us (41%)
  waiting for transfers between devices  21.6 us (33%)
  Pallas kernels  11.8 us (18%)
  local copies, waits for them, and re-layouts  4.78 us (7%)
    ppermute x17, starting transfers between devices, permute(): return lax.ppermute(x, 'occ', [(i, i ^ flip) for i in range(n)])  19 us
    ppermute x17, waiting for transfers between devices, permute(): return lax.ppermute(x, 'occ', [(i, i ^ flip) for i in range(n)])  11.5 us
    ppermute x5, waiting for transfers between devices, permute(): lax.ppermute(x, ('occ', 'vir'), [(i * v + j, (i ^ flip) * v + (j ^ swap))...  10.1 us
    ppermute x5, starting transfers between devices, permute(): lax.ppermute(x, ('occ', 'vir'), [(i * v + j, (i ^ flip) * v + (j ^ swap))...  8.18 us
    pallas_call x1, Pallas kernels, near_of(): pl.pallas_call(functools.partial(near_kernel, step, norm, scale), grid=(t...  5.81 us
    unnamed x20, local copies, waits for them, and re-layouts  4.77 us
    pallas_call x2, Pallas kernels, last(): pl.pallas_call(functools.partial(last_kernel, order, norm, scale), in_spe...  3.08 us
    pallas_call x2, Pallas kernels, gram(): pl.pallas_call(functools.partial(gram_kernel, m), in_specs=[VMEM(), VMEM(...  1.44 us
  transfers between devices with their start and end apart: 22, of which 9 were waited for; matrix products, arithmetic and copies ran while one was open for 0% of the time, Pallas kernels for 15%

profile of v2, /device:TPU:0, one launch (start us, length us, event | category | flops | bytes accessed | tf_op | source)
XLA Modules:
  0.0 65.8 jit_solution(2047431136086538804)
XLA Ops:
  0.0 1.6 %copy-done = bf16[16,160,320]{2,1,0:T(8,128)(2,1)S(1)} copy-done((bf16[16,160,320]{2,1,0:T(8,128)(2,1)S(1)}, bf16[16,160,320]{2,1,0:T(8,128)(2,1)}, u32[]{:S(2)}) %copy-start) | copy-done | bytes 1638424
  1.6 0.9 %copy-done.4 = bf16[320,160]{0,1:T(8,128)(2,1)S(1)} copy-done((bf16[320,160]{0,1:T(8,128)(2,1)S(1)}, bf16[320,160]{0,1:T(8,128)(2,1)}, u32[]{:S(2)}) %copy-start.4) | copy-done | bytes 102424
  2.5 0.7 %copy-done.6 = bf16[40,160]{1,0:T(8,128)(2,1)S(1)} copy-done((bf16[40,160]{1,0:T(8,128)(2,1)S(1)}, bf16[40,160]{1,0:T(8,128)(2,1)}, u32[]{:S(2)}) %copy-start.6) | copy-done | bytes 12824
  3.2 0.2 pack.1.early_ref
  3.4 3.0 %collective-permute-start.1 = (bf16[104,5120]{1,0:T(8,128)(2,1)S(1)}, bf16[104,5120]{1,0:T(8,128)(2,1)S(1)}, u32[]{:S(2)}, u32[]{:S(2)}) collective-permute-start(bf16[104,5120]{1,0:T(8,128)(2,1)S(1)} %pack.1.early_ref), channel_id=1, source_target_pairs={{0,1},{1,0},{2,3},{3,2},{4,5},{5,4},{6,7},{7,6},{8,9},{9,8},{10,11... | collective-permute-start | bytes 3194888 | tf_op jit(solution)/shard_map/ppermute | solution.py:244
  6.4 0.1 fusion.keep_ref
  6.5 1.5 %copy-done.2 = bf16[16,160,320]{2,1,0:T(8,128)(2,1)S(1)} copy-done((bf16[16,160,320]{2,1,0:T(8,128)(2,1)S(1)}, bf16[16,160,320]{2,1,0:T(8,128)(2,1)}, u32[]{:S(2)}) %copy-start.2) | copy-done | bytes 1638424
  8.0 1.3 %prepare.1 = (bf16[64,5120]{1,0:T(8,128)(2,1)S(1)}, bf16[160,5120]{1,0:T(8,128)(2,1)S(1)}, f32[40,640]{1,0:T(8,128)S(1)}) custom-call(bf16[16,160,320]{2,1,0:T(8,128)(2,1)S(1)} %copy-done.1, bf16[104,5120]{1,0:T(8,128)(2,1)S(1)} %pack.1.early_ref, bf16[16,160,320]{2,1,0:T(8,128)(2,1)S(1)} %copy-done.2, f32[16,320]{1,0:T(8,128)S(1)} %fusion.keep_ref), custom_call_target="tpu_custom_call" | custom-call | flops 262144000 | bytes 4915200 | tf_op jit(solution)/shard_map/prepare/pallas_call | solution.py:116
  9.4 0.7 %collective-permute-start.4 = (f32[40,640]{1,0:T(8,128)S(1)}, f32[40,640]{1,0:T(8,128)S(1)}, u32[]{:S(2)}, u32[]{:S(2)}) collective-permute-start(f32[40,640]{1,0:T(8,128)S(1)} %get-tuple-element.13), channel_id=1, source_target_pairs={{0,6},{2,4},{4,2},{6,0},{8,14},{10,12},{12,10},{14,8},{16,22},{18,... | collective-permute-start | bytes 307208 | tf_op jit(solution)/shard_map/ppermute | solution.py:243
  10.1 0.9 %collective-permute-start.3 = (f32[40,640]{1,0:T(8,128)S(1)}, f32[40,640]{1,0:T(8,128)S(1)}, u32[]{:S(2)}, u32[]{:S(2)}) collective-permute-start(f32[40,640]{1,0:T(8,128)S(1)} %get-tuple-element.13), channel_id=1, source_target_pairs={{0,4},{2,6},{4,0},{6,2},{8,12},{10,14},{12,8},{14,10},{16,20},{18,... | collective-permute-start | bytes 307208 | tf_op jit(solution)/shard_map/ppermute | solution.py:243
  11.0 0.3 collective-permute-start.2
  11.3 3.2 %collective-permute-done.4 = f32[40,640]{1,0:T(8,128)S(1)} collective-permute-done((f32[40,640]{1,0:T(8,128)S(1)}, f32[40,640]{1,0:T(8,128)S(1)}, u32[]{:S(2)}, u32[]{:S(2)}) %collective-permute-start.4) | collective-permute-done | bytes 102432 | tf_op jit(solution)/shard_map/ppermute | solution.py:243
  14.5 2.3 %collective-permute-done.3 = f32[40,640]{1,0:T(8,128)S(1)} collective-permute-done((f32[40,640]{1,0:T(8,128)S(1)}, f32[40,640]{1,0:T(8,128)S(1)}, u32[]{:S(2)}, u32[]{:S(2)}) %collective-permute-start.3) | collective-permute-done | bytes 102432 | tf_op jit(solution)/shard_map/ppermute | solution.py:243
  16.8 0.0 collective-permute-done.2
  16.8 0.0 copy-start.3
  16.9 0.0 copy-start.5
  16.9 0.0 copy-start.7
  16.9 0.0 copy-start.8
  16.9 3.7 %collective-permute-start.8 = (f32[40,640]{1,0:T(8,128)S(1)}, f32[40,640]{1,0:T(8,128)S(1)}, u32[]{:S(2)}, u32[]{:S(2)}) collective-permute-start(f32[40,640]{1,0:T(8,128)S(1)} %add_add_fusion.1), channel_id=1, source_target_pairs={{0,24},{2,26},{4,28},{6,30},{8,16},{10,18},{12,20},{14,22},{16,8},... | collective-permute-start | bytes 307208 | tf_op jit(solution)/shard_map/ppermute | solution.py:243
  20.6 0.8 %collective-permute-start.6 = (f32[40,640]{1,0:T(8,128)S(1)}, f32[40,640]{1,0:T(8,128)S(1)}, u32[]{:S(2)}, u32[]{:S(2)}) collective-permute-start(f32[40,640]{1,0:T(8,128)S(1)} %add_add_fusion.1), channel_id=1, source_target_pairs={{0,8},{2,10},{4,12},{6,14},{8,0},{10,2},{12,4},{14,6},{16,24},{18,... | collective-permute-start | bytes 307208 | tf_op jit(solution)/shard_map/ppermute | solution.py:243
  21.3 1.2 %collective-permute-start = (bf16[64,5120]{1,0:T(8,128)(2,1)S(1)}, bf16[64,5120]{1,0:T(8,128)(2,1)S(1)}, u32[]{:S(2)}, u32[]{:S(2)}) collective-permute-start(bf16[64,5120]{1,0:T(8,128)(2,1)S(1)} %get-tuple-element.12), channel_id=1, source_target_pairs={{0,1},{1,0},{2,3},{3,2},{4,5},{5,4},{6,7},{7,6},{8,9},{9,8},{10,11... | collective-permute-start | bytes 1966088 | tf_op jit(solution)/shard_map/ppermute | solution.py:244
  22.5 8.2 %collective-permute-done.1.x_ref.refs_1_ = bf16[104,5120]{1,0:T(8,128)(2,1)S(1)} collective-permute-done((bf16[104,5120]{1,0:T(8,128)(2,1)S(1)}, bf16[104,5120]{1,0:T(8,128)(2,1)S(1)}, u32[]{:S(2)}, u32[]{:S(2)}) %collective-permute-start.1) | collective-permute-done | bytes 1064992 | tf_op jit(solution)/shard_map/ppermute | solution.py:244
  30.7 0.7 %gram.2 = f32[24,640]{1,0:T(8,128)S(1)} custom-call(bf16[104,5120]{1,0:T(8,128)(2,1)S(1)} %collective-permute-done.1.x_ref.refs_1_, bf16[160,5120]{1,0:T(8,128)(2,1)S(1)} %get-tuple-element.15.y_ref), custom_call_target="tpu_custom_call" | custom-call | flops 157286400 | bytes 2621440 | tf_op jit(solution)/shard_map/gram/pallas_call | solution.py:138
  31.5 0.1 collective-permute-start.11
  31.5 0.0 collective-permute-done.8
  31.5 2.2 %collective-permute-start.10 = (f32[24,640]{1,0:T(8,128)S(1)}, f32[24,640]{1,0:T(8,128)S(1)}, u32[]{:S(2)}, u32[]{:S(2)}) collective-permute-start(f32[24,640]{1,0:T(8,128)S(1)} %gram.2), channel_id=1, source_target_pairs={{0,4},{2,6},{4,0},{6,2},{8,12},{10,14},{12,8},{14,10},{16,20},{18,... | collective-permute-start | bytes 184328 | tf_op jit(solution)/shard_map/ppermute | solution.py:243
  33.7 0.1 collective-permute-start.9
  33.8 0.5 collective-permute-start.5
  34.3 0.9 %collective-permute-done.11 = f32[24,640]{1,0:T(8,128)S(1)} collective-permute-done((f32[24,640]{1,0:T(8,128)S(1)}, f32[24,640]{1,0:T(8,128)S(1)}, u32[]{:S(2)}, u32[]{:S(2)}) %collective-permute-start.11) | collective-permute-done | bytes 61472 | tf_op jit(solution)/shard_map/ppermute | solution.py:243
  35.2 1.4 %collective-permute-done.10 = f32[24,640]{1,0:T(8,128)S(1)} collective-permute-done((f32[24,640]{1,0:T(8,128)S(1)}, f32[24,640]{1,0:T(8,128)S(1)}, u32[]{:S(2)}, u32[]{:S(2)}) %collective-permute-start.10) | collective-permute-done | bytes 61472 | tf_op jit(solution)/shard_map/ppermute | solution.py:243
  36.6 4.8 %collective-permute-start.20 = (f32[24,640]{1,0:T(8,128)S(1)}, f32[24,640]{1,0:T(8,128)S(1)}, u32[]{:S(2)}, u32[]{:S(2)}) collective-permute-start(f32[24,640]{1,0:T(8,128)S(1)} %add_add_fusion.2), channel_id=1, source_target_pairs={{0,24},{2,26},{4,28},{6,30},{8,16},{10,18},{12,20},{14,22},{16,8},... | collective-permute-start | bytes 184328 | tf_op jit(solution)/shard_map/ppermute | solution.py:243
  41.4 0.0 collective-permute-start.19
  41.4 0.6 collective-permute-start.18
  42.0 0.0 collective-permute-done.5.other_ref
  42.1 5.8 %near.1.refs_2_ = f32[16,160,320]{2,1,0:T(8,128)S(1)} custom-call(f32[16,320]{1,0:T(8,128)S(1)} %fusion.keep_ref, bf16[16,160,320]{2,1,0:T(8,128)(2,1)S(1)} %copy-done.1, bf16[16,160,320]{2,1,0:T(8,128)(2,1)S(1)} %copy-done.3, bf16[40,320]{1,0:T(8,128)(2,1)S(1)} %bitcast.4, bf16[160,320]{1,0:T(8,128)(2,1)S(1)} %bitcast.3, bf16[40,160]{1,0:T(8,128)(2,1)S(1)} %copy-done.7, ...), custom_call_target="tpu_custom_call" | custom-call | flops 891289600 | bytes 6553600 | tf_op jit(solution)/shard_map/near/pallas_call | solution.py:182
  47.9 0.7 %gram.3 = f32[16,640]{1,0:T(8,128)S(1)} custom-call(bf16[64,5120]{1,0:T(8,128)(2,1)S(1)} %collective-permute-done.x_ref.refs_0_, bf16[160,5120]{1,0:T(8,128)(2,1)S(1)} %get-tuple-element.15.y_ref), custom_call_target="tpu_custom_call" | custom-call | flops 104857600 | bytes 2293760 | tf_op jit(solution)/shard_map/gram/pallas_call | solution.py:138
  48.6 0.1 collective-permute-start.12
  48.7 1.2 %collective-permute-done.12 = f32[16,640]{1,0:T(8,128)S(1)} collective-permute-done((f32[16,640]{1,0:T(8,128)S(1)}, f32[16,640]{1,0:T(8,128)S(1)}, u32[]{:S(2)}, u32[]{:S(2)}) %collective-permute-start.12) | collective-permute-done | bytes 40992 | tf_op jit(solution)/shard_map/ppermute | solution.py:243
  49.9 1.9 %collective-permute-start.14 = (f32[16,640]{1,0:T(8,128)S(1)}, f32[16,640]{1,0:T(8,128)S(1)}, u32[]{:S(2)}, u32[]{:S(2)}) collective-permute-start(f32[16,640]{1,0:T(8,128)S(1)} %add.60), channel_id=1, source_target_pairs={{0,5},{1,4},{2,7},{3,6},{4,1},{5,0},{6,3},{7,2},{8,13},{9,12},{10,... | collective-permute-start | bytes 122888 | tf_op jit(solution)/shard_map/ppermute | solution.py:244
  51.8 0.5 collective-permute-start.13
  52.4 1.6 %collective-permute-start.21 = (bf16[24,640]{1,0:T(8,128)(2,1)S(1)}, bf16[24,640]{1,0:T(8,128)(2,1)S(1)}, u32[]{:S(2)}, u32[]{:S(2)}) collective-permute-start(bf16[24,640]{1,0:T(8,128)(2,1)S(1)} %multiply_convert_fusion), channel_id=1, source_target_pairs={{0,1},{1,0},{2,3},{3,2},{4,5},{5,4},{6,7},{7,6},{8,9},{9,8},{10,11... | collective-permute-start | bytes 92168 | tf_op jit(solution)/shard_map/ppermute | solution.py:244
  53.9 0.9 %collective-permute-done.14 = f32[16,640]{1,0:T(8,128)S(1)} collective-permute-done((f32[16,640]{1,0:T(8,128)S(1)}, f32[16,640]{1,0:T(8,128)S(1)}, u32[]{:S(2)}, u32[]{:S(2)}) %collective-permute-start.14) | collective-permute-done | bytes 40992 | tf_op jit(solution)/shard_map/ppermute | solution.py:244
  54.8 1.0 %collective-permute-done.13 = f32[16,640]{1,0:T(8,128)S(1)} collective-permute-done((f32[16,640]{1,0:T(8,128)S(1)}, f32[16,640]{1,0:T(8,128)S(1)}, u32[]{:S(2)}, u32[]{:S(2)}) %collective-permute-start.13) | collective-permute-done | bytes 40992 | tf_op jit(solution)/shard_map/ppermute | solution.py:244
  55.8 3.6 %collective-permute-start.17 = (f32[16,640]{1,0:T(8,128)S(1)}, f32[16,640]{1,0:T(8,128)S(1)}, u32[]{:S(2)}, u32[]{:S(2)}) collective-permute-start(f32[16,640]{1,0:T(8,128)S(1)} %add.61), channel_id=1, source_target_pairs={{0,24},{2,26},{4,28},{6,30},{8,16},{10,18},{12,20},{14,22},{16,8},... | collective-permute-start | bytes 122888 | tf_op jit(solution)/shard_map/ppermute | solution.py:243
  59.4 0.8 %collective-permute-start.15 = (f32[16,640]{1,0:T(8,128)S(1)}, f32[16,640]{1,0:T(8,128)S(1)}, u32[]{:S(2)}, u32[]{:S(2)}) collective-permute-start(f32[16,640]{1,0:T(8,128)S(1)} %add.61), channel_id=1, source_target_pairs={{0,8},{2,10},{4,12},{6,14},{8,0},{10,2},{12,4},{14,6},{16,24},{18,... | collective-permute-start | bytes 122888 | tf_op jit(solution)/shard_map/ppermute | solution.py:243
  60.2 1.6 %last.2.refs_3_ = bf16[16,160,320]{2,1,0:T(8,128)(2,1)} custom-call(f32[16,320]{1,0:T(8,128)S(1)} %fusion.keep_ref, bf16[24,640]{1,0:T(8,128)(2,1)S(1)} %collective-permute-done.21.den_ref, bf16[64,5120]{1,0:T(8,128)(2,1)S(1)} %collective-permute-done.x_ref.refs_0_, bf16[104,5120]{1,0:T(8,128)(2,1)S(1)} %collective-permute-done.1.x_ref.refs_1_, ...), custom_call_target="tpu_custom_call" | custom-call | flops 157286400 | bytes 2949120 | tf_op jit(solution)/shard_map/last/pallas_call | solution.py:227
  61.8 2.5 %collective-permute-done.16 = f32[16,640]{1,0:T(8,128)S(1)} collective-permute-done((f32[16,640]{1,0:T(8,128)S(1)}, f32[16,640]{1,0:T(8,128)S(1)}, u32[]{:S(2)}, u32[]{:S(2)}) %collective-permute-start.16) | collective-permute-done | bytes 40992 | tf_op jit(solution)/shard_map/ppermute | solution.py:243
  64.3 1.5 %last.3 = bf16[16,160,320]{2,1,0:T(8,128)(2,1)} custom-call(f32[16,320]{1,0:T(8,128)S(1)} %fusion.keep_ref, f32[16,640]{1,0:T(8,128)S(1)} %add_add_fusion.3.den_ref, bf16[64,5120]{1,0:T(8,128)(2,1)S(1)} %collective-permute-done.x_ref.refs_0_, bf16[104,5120]{1,0:T(8,128)(2,1)S(1)} %collective-permute-done.1.x_ref.refs_1_, ...), custom_call_target="tpu_custom_call", output_to_operand_aliasing={{}: (5, {})} | custom-call | flops 104857600 | bytes 1966080 | tf_op jit(solution)/shard_map/last/pallas_call | solution.py:227
  (33 shorter events, 0.2 us)
Async XLA Ops:
  0.0 6.4 %copy-start.9 = (s32[16]{0:T(128)S(1)}, s32[16]{0:T(128)}, u32[]{:S(2)}) copy-start(s32[16]{0:T(128)} %param.8) | copy-start | bytes 196
  0.0 1.6 %copy-start = (bf16[16,160,320]{2,1,0:T(8,128)(2,1)S(1)}, bf16[16,160,320]{2,1,0:T(8,128)(2,1)}, u32[]{:S(2)}) copy-start(bf16[16,160,320]{2,1,0:T(8,128)(2,1)} %lam_ref.3) | copy-start | bytes 4915204
  1.6 0.9 %copy-start.4 = (bf16[320,160]{0,1:T(8,128)(2,1)S(1)}, bf16[320,160]{0,1:T(8,128)(2,1)}, u32[]{:S(2)}) copy-start(bf16[320,160]{0,1:T(8,128)(2,1)} %param.9) | copy-start | bytes 307204
  2.5 0.7 %copy-start.6 = (bf16[40,160]{1,0:T(8,128)(2,1)S(1)}, bf16[40,160]{1,0:T(8,128)(2,1)}, u32[]{:S(2)}) copy-start(bf16[40,160]{1,0:T(8,128)(2,1)} %doubles_ref.3) | copy-start | bytes 38404
  3.2 3.3 %copy-start.1 = (bf16[16,160,320]{2,1,0:T(8,128)(2,1)S(1)}, bf16[16,160,320]{2,1,0:T(8,128)(2,1)}, u32[]{:S(2)}) copy-start(bf16[16,160,320]{2,1,0:T(8,128)(2,1)} %lam_ref.3) | copy-start | bytes 4915204
  3.4 27.3 %collective-permute-start.1 = (bf16[104,5120]{1,0:T(8,128)(2,1)S(1)}, bf16[104,5120]{1,0:T(8,128)(2,1)S(1)}, u32[]{:S(2)}, u32[]{:S(2)}) collective-permute-start(bf16[104,5120]{1,0:T(8,128)(2,1)S(1)} %pack.1.early_ref), channel_id=1, source_target_pairs={{0,1},{1,0},{2,3},{3,2},{4,5},{5,4},{6,7},{7,6},{8,9},{9,8},{10,11... | collective-permute-start | bytes 3194888 | tf_op jit(solution)/shard_map/ppermute | solution.py:244
  6.5 1.5 %copy-start.2 = (bf16[16,160,320]{2,1,0:T(8,128)(2,1)S(1)}, bf16[16,160,320]{2,1,0:T(8,128)(2,1)}, u32[]{:S(2)}) copy-start(bf16[16,160,320]{2,1,0:T(8,128)(2,1)} %amp_ref.3) | copy-start | bytes 4915204
  9.4 5.2 %collective-permute-start.4 = (f32[40,640]{1,0:T(8,128)S(1)}, f32[40,640]{1,0:T(8,128)S(1)}, u32[]{:S(2)}, u32[]{:S(2)}) collective-permute-start(f32[40,640]{1,0:T(8,128)S(1)} %get-tuple-element.13), channel_id=1, source_target_pairs={{0,6},{2,4},{4,2},{6,0},{8,14},{10,12},{12,10},{14,8},{16,22},{18,... | collective-permute-start | bytes 307208 | tf_op jit(solution)/shard_map/ppermute | solution.py:243
  10.1 6.7 %collective-permute-start.3 = (f32[40,640]{1,0:T(8,128)S(1)}, f32[40,640]{1,0:T(8,128)S(1)}, u32[]{:S(2)}, u32[]{:S(2)}) collective-permute-start(f32[40,640]{1,0:T(8,128)S(1)} %get-tuple-element.13), channel_id=1, source_target_pairs={{0,4},{2,6},{4,0},{6,2},{8,12},{10,14},{12,8},{14,10},{16,20},{18,... | collective-permute-start | bytes 307208 | tf_op jit(solution)/shard_map/ppermute | solution.py:243
  11.0 5.8 %collective-permute-start.2 = (f32[40,640]{1,0:T(8,128)S(1)}, f32[40,640]{1,0:T(8,128)S(1)}, u32[]{:S(2)}, u32[]{:S(2)}) collective-permute-start(f32[40,640]{1,0:T(8,128)S(1)} %get-tuple-element.13), channel_id=1, source_target_pairs={{0,2},{2,0},{4,6},{6,4},{8,10},{10,8},{12,14},{14,12},{16,18},{18,... | collective-permute-start | bytes 307208 | tf_op jit(solution)/shard_map/ppermute | solution.py:243
  16.8 25.2 %copy-start.3 = (bf16[16,160,320]{2,1,0:T(8,128)(2,1)S(1)}, bf16[16,160,320]{2,1,0:T(8,128)(2,1)}, u32[]{:S(2)}) copy-start(bf16[16,160,320]{2,1,0:T(8,128)(2,1)} %amp_ref.3) | copy-start | bytes 4915204
  16.9 25.2 %copy-start.5 = (bf16[320,160]{0,1:T(8,128)(2,1)S(1)}, bf16[320,160]{0,1:T(8,128)(2,1)}, u32[]{:S(2)}) copy-start(bf16[320,160]{0,1:T(8,128)(2,1)} %param.9) | copy-start | bytes 307204
  16.9 25.2 %copy-start.7 = (bf16[40,160]{1,0:T(8,128)(2,1)S(1)}, bf16[40,160]{1,0:T(8,128)(2,1)}, u32[]{:S(2)}) copy-start(bf16[40,160]{1,0:T(8,128)(2,1)} %doubles_ref.3) | copy-start | bytes 38404
  16.9 25.2 %copy-start.8 = (bf16[320,40]{0,1:T(8,128)(2,1)S(1)}, bf16[320,40]{0,1:T(8,128)(2,1)}, u32[]{:S(2)}) copy-start(bf16[320,40]{0,1:T(8,128)(2,1)} %param.10) | copy-start | bytes 76804
  16.9 14.6 %collective-permute-start.8 = (f32[40,640]{1,0:T(8,128)S(1)}, f32[40,640]{1,0:T(8,128)S(1)}, u32[]{:S(2)}, u32[]{:S(2)}) collective-permute-start(f32[40,640]{1,0:T(8,128)S(1)} %add_add_fusion.1), channel_id=1, source_target_pairs={{0,24},{2,26},{4,28},{6,30},{8,16},{10,18},{12,20},{14,22},{16,8},... | collective-permute-start | bytes 307208 | tf_op jit(solution)/shard_map/ppermute | solution.py:243
  20.6 13.1 %collective-permute-start.7 = (f32[40,640]{1,0:T(8,128)S(1)}, f32[40,640]{1,0:T(8,128)S(1)}, u32[]{:S(2)}, u32[]{:S(2)}) collective-permute-start(f32[40,640]{1,0:T(8,128)S(1)} %add_add_fusion.1), channel_id=1, source_target_pairs={{0,16},{2,18},{4,20},{6,22},{8,24},{10,26},{12,28},{14,30},{16,0},... | collective-permute-start | bytes 307208 | tf_op jit(solution)/shard_map/ppermute | solution.py:243
  20.6 13.2 %collective-permute-start.6 = (f32[40,640]{1,0:T(8,128)S(1)}, f32[40,640]{1,0:T(8,128)S(1)}, u32[]{:S(2)}, u32[]{:S(2)}) collective-permute-start(f32[40,640]{1,0:T(8,128)S(1)} %add_add_fusion.1), channel_id=1, source_target_pairs={{0,8},{2,10},{4,12},{6,14},{8,0},{10,2},{12,4},{14,6},{16,24},{18,... | collective-permute-start | bytes 307208 | tf_op jit(solution)/shard_map/ppermute | solution.py:243
  21.3 26.5 %collective-permute-start = (bf16[64,5120]{1,0:T(8,128)(2,1)S(1)}, bf16[64,5120]{1,0:T(8,128)(2,1)S(1)}, u32[]{:S(2)}, u32[]{:S(2)}) collective-permute-start(bf16[64,5120]{1,0:T(8,128)(2,1)S(1)} %get-tuple-element.12), channel_id=1, source_target_pairs={{0,1},{1,0},{2,3},{3,2},{4,5},{5,4},{6,7},{7,6},{8,9},{9,8},{10,11... | collective-permute-start | bytes 1966088 | tf_op jit(solution)/shard_map/ppermute | solution.py:244
  31.5 3.8 %collective-permute-start.11 = (f32[24,640]{1,0:T(8,128)S(1)}, f32[24,640]{1,0:T(8,128)S(1)}, u32[]{:S(2)}, u32[]{:S(2)}) collective-permute-start(f32[24,640]{1,0:T(8,128)S(1)} %gram.2), channel_id=1, source_target_pairs={{0,6},{2,4},{4,2},{6,0},{8,14},{10,12},{12,10},{14,8},{16,22},{18,... | collective-permute-start | bytes 184328 | tf_op jit(solution)/shard_map/ppermute | solution.py:243
  31.5 5.1 %collective-permute-start.10 = (f32[24,640]{1,0:T(8,128)S(1)}, f32[24,640]{1,0:T(8,128)S(1)}, u32[]{:S(2)}, u32[]{:S(2)}) collective-permute-start(f32[24,640]{1,0:T(8,128)S(1)} %gram.2), channel_id=1, source_target_pairs={{0,4},{2,6},{4,0},{6,2},{8,12},{10,14},{12,8},{14,10},{16,20},{18,... | collective-permute-start | bytes 184328 | tf_op jit(solution)/shard_map/ppermute | solution.py:243
  33.7 2.9 %collective-permute-start.9 = (f32[24,640]{1,0:T(8,128)S(1)}, f32[24,640]{1,0:T(8,128)S(1)}, u32[]{:S(2)}, u32[]{:S(2)}) collective-permute-start(f32[24,640]{1,0:T(8,128)S(1)} %gram.2), channel_id=1, source_target_pairs={{0,2},{2,0},{4,6},{6,4},{8,10},{10,8},{12,14},{14,12},{16,18},{18,... | collective-permute-start | bytes 184328 | tf_op jit(solution)/shard_map/ppermute | solution.py:243
  33.8 8.2 %collective-permute-start.5 = (bf16[8,5120]{1,0:T(8,128)(2,1)S(1)}, bf16[8,5120]{1,0:T(8,128)(2,1)S(1)}, u32[]{:S(2)}, u32[]{:S(2)}) collective-permute-start(bf16[8,5120]{1,0:T(8,128)(2,1)S(1)} %slice.3.mine_ref), channel_id=1, source_target_pairs={{0,2},{2,0},{4,6},{6,4},{8,10},{10,8},{12,14},{14,12},{16,18},{18,... | collective-permute-start | bytes 245768 | tf_op jit(solution)/shard_map/ppermute | solution.py:243
  36.6 15.7 %collective-permute-start.20 = (f32[24,640]{1,0:T(8,128)S(1)}, f32[24,640]{1,0:T(8,128)S(1)}, u32[]{:S(2)}, u32[]{:S(2)}) collective-permute-start(f32[24,640]{1,0:T(8,128)S(1)} %add_add_fusion.2), channel_id=1, source_target_pairs={{0,24},{2,26},{4,28},{6,30},{8,16},{10,18},{12,20},{14,22},{16,8},... | collective-permute-start | bytes 184328 | tf_op jit(solution)/shard_map/ppermute | solution.py:243
  41.4 11.0 %collective-permute-start.19 = (f32[24,640]{1,0:T(8,128)S(1)}, f32[24,640]{1,0:T(8,128)S(1)}, u32[]{:S(2)}, u32[]{:S(2)}) collective-permute-start(f32[24,640]{1,0:T(8,128)S(1)} %add_add_fusion.2), channel_id=1, source_target_pairs={{0,16},{2,18},{4,20},{6,22},{8,24},{10,26},{12,28},{14,30},{16,0},... | collective-permute-start | bytes 184328 | tf_op jit(solution)/shard_map/ppermute | solution.py:243
  41.4 11.0 %collective-permute-start.18 = (f32[24,640]{1,0:T(8,128)S(1)}, f32[24,640]{1,0:T(8,128)S(1)}, u32[]{:S(2)}, u32[]{:S(2)}) collective-permute-start(f32[24,640]{1,0:T(8,128)S(1)} %add_add_fusion.2), channel_id=1, source_target_pairs={{0,8},{2,10},{4,12},{6,14},{8,0},{10,2},{12,4},{14,6},{16,24},{18,... | collective-permute-start | bytes 184328 | tf_op jit(solution)/shard_map/ppermute | solution.py:243
  48.6 1.3 %collective-permute-start.12 = (f32[16,640]{1,0:T(8,128)S(1)}, f32[16,640]{1,0:T(8,128)S(1)}, u32[]{:S(2)}, u32[]{:S(2)}) collective-permute-start(f32[16,640]{1,0:T(8,128)S(1)} %gram.3), channel_id=1, source_target_pairs={{0,2},{2,0},{4,6},{6,4},{8,10},{10,8},{12,14},{14,12},{16,18},{18,... | collective-permute-start | bytes 122888 | tf_op jit(solution)/shard_map/ppermute | solution.py:243
  49.9 4.9 %collective-permute-start.14 = (f32[16,640]{1,0:T(8,128)S(1)}, f32[16,640]{1,0:T(8,128)S(1)}, u32[]{:S(2)}, u32[]{:S(2)}) collective-permute-start(f32[16,640]{1,0:T(8,128)S(1)} %add.60), channel_id=1, source_target_pairs={{0,5},{1,4},{2,7},{3,6},{4,1},{5,0},{6,3},{7,2},{8,13},{9,12},{10,... | collective-permute-start | bytes 122888 | tf_op jit(solution)/shard_map/ppermute | solution.py:244
  51.8 4.0 %collective-permute-start.13 = (f32[16,640]{1,0:T(8,128)S(1)}, f32[16,640]{1,0:T(8,128)S(1)}, u32[]{:S(2)}, u32[]{:S(2)}) collective-permute-start(f32[16,640]{1,0:T(8,128)S(1)} %add.60), channel_id=1, source_target_pairs={{0,1},{1,0},{2,3},{3,2},{4,5},{5,4},{6,7},{7,6},{8,9},{9,8},{10,11... | collective-permute-start | bytes 122888 | tf_op jit(solution)/shard_map/ppermute | solution.py:244
  52.4 7.8 %collective-permute-start.21 = (bf16[24,640]{1,0:T(8,128)(2,1)S(1)}, bf16[24,640]{1,0:T(8,128)(2,1)S(1)}, u32[]{:S(2)}, u32[]{:S(2)}) collective-permute-start(bf16[24,640]{1,0:T(8,128)(2,1)S(1)} %multiply_convert_fusion), channel_id=1, source_target_pairs={{0,1},{1,0},{2,3},{3,2},{4,5},{5,4},{6,7},{7,6},{8,9},{9,8},{10,11... | collective-permute-start | bytes 92168 | tf_op jit(solution)/shard_map/ppermute | solution.py:244
  55.8 6.0 %collective-permute-start.17 = (f32[16,640]{1,0:T(8,128)S(1)}, f32[16,640]{1,0:T(8,128)S(1)}, u32[]{:S(2)}, u32[]{:S(2)}) collective-permute-start(f32[16,640]{1,0:T(8,128)S(1)} %add.61), channel_id=1, source_target_pairs={{0,24},{2,26},{4,28},{6,30},{8,16},{10,18},{12,20},{14,22},{16,8},... | collective-permute-start | bytes 122888 | tf_op jit(solution)/shard_map/ppermute | solution.py:243
  59.4 4.9 %collective-permute-start.16 = (f32[16,640]{1,0:T(8,128)S(1)}, f32[16,640]{1,0:T(8,128)S(1)}, u32[]{:S(2)}, u32[]{:S(2)}) collective-permute-start(f32[16,640]{1,0:T(8,128)S(1)} %add.61), channel_id=1, source_target_pairs={{0,16},{2,18},{4,20},{6,22},{8,24},{10,26},{12,28},{14,30},{16,0},... | collective-permute-start | bytes 122888 | tf_op jit(solution)/shard_map/ppermute | solution.py:243
  59.4 4.9 %collective-permute-start.15 = (f32[16,640]{1,0:T(8,128)S(1)}, f32[16,640]{1,0:T(8,128)S(1)}, u32[]{:S(2)}, u32[]{:S(2)}) collective-permute-start(f32[16,640]{1,0:T(8,128)S(1)} %add.61), channel_id=1, source_target_pairs={{0,8},{2,10},{4,12},{6,14},{8,0},{10,2},{12,4},{14,6},{16,24},{18,... | collective-permute-start | bytes 122888 | tf_op jit(solution)/shard_map/ppermute | solution.py:243

commit v3 on v2

v3 whole, which is shorter than its diff:
```python
import functools

import jax
import jax.numpy as jnp
from jax import lax
from jax.experimental import pallas as pl
from jax.experimental.pallas import tpu as pltpu
from jax.sharding import PartitionSpec as P

F32, BF16 = jnp.float32, jnp.bfloat16
NT = (((1,), (1,)), ((), ()))
VMEM = functools.partial(pl.BlockSpec, memory_space=pltpu.VMEM)
SMEM = functools.partial(pl.BlockSpec, memory_space=pltpu.SMEM)
LATE = 64
FIRST = 32
PARTS = 4
EXTRA = 8


def params(mib, **kw):
    return pltpu.CompilerParams(vmem_limit_bytes=mib << 20, **kw)


def cost(flops, nbytes):
    return pl.CostEstimate(flops=flops, bytes_accessed=nbytes, transcendentals=0)


def whole(x):
    return pl.BlockSpec(x.shape, lambda i: (0,) * x.ndim)


def after(x, *others):
    return lax.optimization_barrier((x, *others))[0]


def pack_into(o_ref, x_ref, keep_ref=None):
    triples, _, width = x_ref.shape
    main = width // 128 * 128
    tail = width - main
    for t in range(0, triples, 2):
        pair = []
        for u in (t, t + 1):
            x = x_ref[u]
            if keep_ref is not None:
                x = x * keep_ref[u : u + 1, :].astype(BF16)
            o_ref[:, u * main : (u + 1) * main] = x[:, :main]
            pair.append(x[:, main:])
        at = triples * main + t * tail
        o_ref[:, at : at + 2 * tail] = jnp.concatenate(pair, axis=1)


def core_of():
    return lax.rem(lax.axis_index("occ"), 2)


def spread(x):
    return jnp.concatenate([x[i : i + EXTRA] for i in range(0, x.shape[0], EXTRA)], axis=1)


def gather_back(x, width):
    return jnp.concatenate([x[:, i : i + width] for i in range(0, x.shape[1], width)], axis=0)


def pack_kernel(start, x_ref, ladder_ref, doubles_ref, o_ref, p_ref, x_buf, l_buf, d_buf, sems):
    triples, rows, _ = x_buf.shape
    half = ladder_ref.shape[0] // 2
    n = triples // PARTS
    first = pl.multiple_of(core_of() * half, 16)
    copies = [(x_ref.at[pl.ds(k * n, n), pl.ds(start, rows)], x_buf.at[pl.ds(k * n, n)]) for k in range(PARTS)]
    copies += [(ladder_ref.at[pl.ds(first, half)], l_buf), (doubles_ref, d_buf)]
    copies = [pltpu.make_async_copy(src, dst, sems.at[k]) for k, (src, dst) in enumerate(copies)]
    for c in copies:
        c.start()
    for c in copies:
        c.wait()
    pack_into(o_ref.at[:FIRST], x_buf.at[:, :FIRST])
    pack_into(p_ref, x_buf.at[:, FIRST:])
    parts = [spread(l_buf[...].astype(F32)), spread(d_buf[...].astype(F32))]
    used = sum(p.shape[1] for p in parts)
    parts.append(jnp.zeros((EXTRA, o_ref.shape[1] - used), F32))
    o_ref[FIRST:, :] = jnp.concatenate(parts, axis=1).astype(BF16)


def pack(x, ladder, doubles, start):
    triples, rows, width = x.shape
    rows = rows - start
    shapes = [(FIRST + EXTRA, triples * width), (rows - FIRST, triples * width)]
    return pl.pallas_call(
        functools.partial(pack_kernel, start),
        in_specs=[pl.BlockSpec(memory_space=pltpu.HBM)] * 3,
        out_specs=[VMEM()] * 2,
        out_shape=[jax.ShapeDtypeStruct(s, BF16) for s in shapes],
        scratch_shapes=[
            pltpu.VMEM((triples, rows, width), BF16),
            pltpu.VMEM((ladder.shape[0] // 2, width), BF16),
            pltpu.VMEM(doubles.shape, BF16),
            pltpu.SemaphoreType.DMA((PARTS + 2,)),
        ],
        compiler_params=params(8),
        cost_estimate=cost(triples * rows * width * 2, triples * rows * width * 4),
        name="pack",
    )(*(pltpu.with_memory_space_constraint(y, pltpu.HBM) for y in (x, ladder, doubles)))


def fold_of(rows):
    return 5 if rows % 80 == 0 and rows < 160 else 4


def fold(x):
    q = fold_of(x.shape[0])
    m = x.shape[0] // q
    return jnp.concatenate([x[k * m : (k + 1) * m] for k in range(q)], axis=1)


def unfold(x, n):
    return jnp.concatenate([x[:, k : k + n] for k in range(0, x.shape[1], n)], axis=0)


def folded(m, n):
    q = fold_of(m)
    return jax.ShapeDtypeStruct((m // q, q * n), F32)


def product_of(x, y):
    return lax.dot_general(x, y, NT, preferred_element_type=F32)


def prepare_kernel(lam_ref, first_ref, early_ref, amp_ref, keep_ref, late_ref, all_ref, o_ref):
    pack_into(late_ref, lam_ref)
    pack_into(all_ref, amp_ref, keep_ref)
    y = all_ref[...]
    o_ref[...] = fold(jnp.concatenate([product_of(x, y) for x in (late_ref[...], first_ref[:FIRST], early_ref[...])]))


def prepare(lam, first, early, amp, keep):
    triples, rows, width = lam.shape
    size = triples * width
    return pl.pallas_call(
        prepare_kernel,
        grid=(1,),
        in_specs=[pl.BlockSpec((triples, LATE, width), lambda i: (0, 0, 0)), whole(first), whole(early), whole(amp), whole(keep)],
        out_specs=[pl.BlockSpec(s, lambda i: (0, 0)) for s in ((LATE, size), (rows, size), (rows // 4, 4 * rows))],
        out_shape=[
            jax.ShapeDtypeStruct((LATE, size), BF16),
            jax.ShapeDtypeStruct((rows, size), BF16),
            jax.ShapeDtypeStruct((rows // 4, 4 * rows), F32),
        ],
        compiler_params=params(18),
        cost_estimate=cost(2 * rows * rows * size, 6 * rows * size),
        name="prepare",
    )(lam, first, early, amp, keep)


def gram_kernel(*refs):
    *xs, y_ref, o_ref = refs
    y = y_ref[...]
    o_ref[...] = fold(jnp.concatenate([product_of(x[: x.shape[0] // 16 * 16], y) for x in xs]))


def gram(xs, y):
    m, (n, k) = sum(x.shape[0] // 16 * 16 for x in xs), y.shape
    return pl.pallas_call(
        gram_kernel,
        in_specs=[VMEM()] * (len(xs) + 1),
        out_specs=VMEM(),
        out_shape=folded(m, n),
        compiler_params=params(8),
        cost_estimate=cost(2 * m * n * k, 2 * (m + n) * k),
        name="gram",
    )(*xs, y)


def near_kernel(step, keep_ref, lam_ref, amp_ref, cyc_ref, ladder_ref, doubles_ref, mine_ref, other_ref, o_ref, w_ref, d_ref):
    i = pl.program_id(0)
    half, width = ladder_ref.shape
    rows = lam_ref.shape[1]

    @pl.when(i == 0)
    def _():
        core, vir = core_of(), lax.axis_index("vir")
        size = half // 2 // EXTRA * width
        mine, other = mine_ref[...].astype(F32), other_ref[...].astype(F32)
        w_ref[pl.ds(pl.multiple_of(vir * half, 16), half), :] = ladder_ref[...]
        there = (1 - vir) * half
        for x, c in ((mine, core), (other, 1 - core)):
            at = pl.multiple_of(there + c * (half // 2), 16)
            w_ref[pl.ds(at, half // 2), :] = gather_back(x[:, :size], width).astype(BF16)
        own = doubles_ref[...].astype(F32)
        got = gather_back(mine[:, size : size + own.shape[0] // EXTRA * half], half)
        d_ref[:, :half] = jnp.where(vir == 0, own, got).astype(BF16)
        d_ref[:, half:] = jnp.where(vir == 0, got, own).astype(BF16)

    keep = [keep_ref[pl.ds(i * step + u, 1), :].astype(BF16) for u in range(step)]
    lam = jnp.concatenate([lam_ref[u] * keep[u] for u in range(step)], axis=0)
    mid = product_of(amp_ref[...].reshape(step * rows, width), cyc_ref[...]).astype(BF16)
    near = product_of(lam, w_ref[...]) + jnp.dot(mid, d_ref[...], preferred_element_type=F32)
    o_ref[...] = near.reshape(step, rows, width)


def near_of(lam, amp, keep, cyc, ladder, doubles, mine, other, step=4):
    triples, rows, width = lam.shape
    block = pl.BlockSpec((step, rows, width), lambda i: (i, 0, 0))
    return pl.pallas_call(
        functools.partial(near_kernel, step),
        grid=(triples // step,),
        in_specs=[whole(keep), block, block, *map(whole, (cyc, ladder, doubles, mine, other))],
        out_specs=block,
        out_shape=jax.ShapeDtypeStruct(lam.shape, F32),
        scratch_shapes=[pltpu.VMEM((width, width), BF16), pltpu.VMEM((doubles.shape[0], width), BF16)],
        compiler_params=params(12),
        cost_estimate=cost(2 * triples * rows * width * (width + 64), triples * rows * width * 8),
        name="near",
    )(keep, lam, amp, cyc, ladder, doubles, mine, other)


def add_kernel(step, norm, scale, keep_ref, lam_ref, near_ref, den_ref, o_ref):
    i = pl.program_id(0)
    den = (unfold(den_ref[...], near_ref.shape[1]) / norm).astype(BF16)
    for u in range(step):
        keep = keep_ref[pl.ds(i * step + u, 1), :] * scale
        o_ref[u] = near_ref[u] + jnp.dot(den, lam_ref[u], preferred_element_type=F32) * keep


def add_own(keep, lam, near, den, norm, scale, step=4):
    triples, rows, width = lam.shape
    block = pl.BlockSpec((step, rows, width), lambda i: (i, 0, 0))
    return pl.pallas_call(
        functools.partial(add_kernel, step, norm, scale),
        grid=(triples // step,),
        in_specs=[whole(keep), block, block, whole(den)],
        out_specs=block,
        out_shape=jax.ShapeDtypeStruct(lam.shape, F32),
        input_output_aliases={2: 0},
        compiler_params=params(12),
        cost_estimate=cost(2 * triples * rows * width * rows, triples * rows * width * 10),
        name="add_own",
    )(keep, lam, near, den)


def last_kernel(norm, scale, keep_ref, den_ref, *refs):
    *got, near_ref, _, o_ref = refs
    triples, rows, width = near_ref.shape
    main = width // 128 * 128
    tail = width - main
    den = unfold(den_ref[...].astype(F32), sum(g.shape[0] // 16 * 16 for g in got))
    if norm is not None:
        den = den / norm
    den = den.astype(BF16)
    all_got = jnp.concatenate([g[: g.shape[0] // 16 * 16] for g in got], axis=0)

    def product(lo, size):
        return jnp.dot(den, all_got[:, lo : lo + size], preferred_element_type=F32) * scale

    for t in range(0, triples, 2):
        ends = product(triples * main + t * tail, 2 * tail)
        for u in (t, t + 1):
            s = (u - t) * tail
            keep = keep_ref[u : u + 1, :]
            o_ref[u, :, :main] = (near_ref[u, :, :main] + product(u * main, main) * keep[:, :main]).astype(BF16)
            o_ref[u, :, main:] = (near_ref[u, :, main:] + ends[:, s : s + tail] * keep[:, main:]).astype(BF16)


def last(keep, den, got, near, out, start, rows, norm, scale):
    triples, _, width = near.shape
    spec = pl.BlockSpec((pl.Element(triples), pl.Element(rows), pl.Element(width)), lambda i: (0, start, 0))
    if out is None:
        out, alias = jnp.zeros((8, 128), BF16), {}
    else:
        alias = {len(got) + 3: 0}
    return pl.pallas_call(
        functools.partial(last_kernel, norm, scale),
        in_specs=[whole(keep), whole(den), *map(whole, got), spec, pl.BlockSpec(memory_space=pl.ANY)],
        grid=(1,),
        out_specs=spec,
        out_shape=jax.ShapeDtypeStruct(near.shape, BF16),
        input_output_aliases=alias,
        compiler_params=params(14),
        cost_estimate=cost(2 * triples * rows * width * 160, triples * rows * width * 6),
        name="last",
    )(keep, den, *got, near, out)


def permute(x, flip, swap=0):
    n, v = lax.axis_size("occ"), lax.axis_size("vir")
    if not swap:
        return lax.ppermute(x, "occ", [(i, i ^ flip) for i in range(n)])
    return lax.ppermute(x, ("occ", "vir"), [(i * v + j, (i ^ flip) * v + (j ^ swap)) for i in range(n) for j in range(v)])


def far_sum(x):
    n = lax.axis_size("occ")
    bit = 4
    while bit < n:
        if 2 * bit < n:
            far, mid, close = permute(x, 3 * bit), permute(x, 2 * bit), permute(x, bit)
            x = (x + close) + (mid + far)
            bit *= 4
        else:
            x = x + permute(x, bit)
            bit *= 2
    return x


def near_sum(x):
    far, mid, close = permute(x, 3), permute(x, 2), permute(x, 1)
    return (x + close) + (mid + far)


def crossed_sum(x):
    x = x + permute(x, 1)
    far, close = permute(x, 2, 1), permute(x, 0, 1)
    return close + far


def on_device(lam, amp, ext, ladder, cycle, doubles):
    triples, rows, width = lam.shape
    all_triples = triples * lax.axis_size("occ")
    norm = float(all_triples * width) ** 0.5
    scale = 1.0 / float(width) ** 0.5
    early_rows = rows - LATE

    ladder = ladder.T
    first_own, early_own = pack(lam, ladder, doubles, LATE)
    first_got, early_got = permute(first_own, 0, 1), permute(early_own, 0, 1)
    keep = (lax.broadcasted_iota(jnp.int32, (triples, width), 1) < ext[:, None]).astype(F32)
    late_own, amp_all, own_den = prepare(lam, first_own, early_own, amp, keep)
    late_got = permute(late_own, 0, 1)

    own_den = near_sum(own_den)
    first_got = after(first_got, own_den)
    own_den = far_sum(own_den)
    mine = first_got[FIRST:]
    other = permute(mine, 1)
    near = near_of(lam, amp, keep, cycle.T, ladder, doubles, mine, other)

    early_got = after(early_got, near)
    early = near_sum(gram((first_got, early_got), amp_all))
    near = add_own(keep, lam, near, after(own_den, early), norm, scale)

    early = far_sum(early)
    late_got = after(late_got, near)
    early = permute((early / norm).astype(BF16), 0, 1)
    late = crossed_sum(gram((late_got,), amp_all))
    early = after(early, late)
    late = (far_sum(late) / norm).astype(BF16)

    got = (late_got, first_got, early_got)
    out = last(keep, early, got, near, None, LATE, early_rows, None, scale)
    return last(keep, late, got, near, out, 0, LATE, None, scale)


def solution(mesh):
    return jax.shard_map(
        on_device,
        mesh=mesh,
        in_specs=(
            P("occ", "vir", None),
            P("occ", "vir", None),
            P("occ"),
            P(None, "vir"),
            P(),
            P(None, "vir"),
        ),
        out_specs=P("occ", "vir", None),
        check_vma=False,
    )
```

time: 66.1 us -> 62.4 us (0.944)
  local copies, waits for them, and re-layouts: 4.78 us -> 1.58 us
  waiting for transfers between devices: 21.6 us -> 18.6 us
  Pallas kernels: 11.8 us -> 14 us
    ppermute x5 -> x6, waiting for transfers between devices: 10.1 us -> 4.37 us  [permute(): lax.ppermute(x, ('occ', 'vir'), [(i * v + j, (i ^ flip) * v + (j ^ swap))...]
    unnamed x20 -> x14, local copies, waits for them, and re-layouts: 4.77 us -> 1.57 us
    ppermute x17, waiting for transfers between devices: 11.5 us -> 14.3 us  [permute(): return lax.ppermute(x, 'occ', [(i, i ^ flip) for i in range(n)])]
    pallas_call x6 -> x7, Pallas kernels: 10.5 us -> 12.1 us  [the longest x1 4.04 us: near_of(): pl.pallas_call(functools.partial(near_kernel, step), grid=(triples // ste...]
    ppermute x5 -> x6, starting transfers between devices: 8.18 us -> 9.41 us  [permute(): lax.ppermute(x, ('occ', 'vir'), [(i * v + j, (i ^ flip) * v + (j ^ swap))...]
    ppermute x17, starting transfers between devices: 19 us -> 18.3 us  [permute(): return lax.ppermute(x, 'occ', [(i, i ^ flip) for i in range(n)])]
  transfers between devices with their start and end apart: 22 -> 23, of which waited for: 9 -> 9; matrix products, arithmetic and copies ran while one was open for 0% -> 0% of each run, Pallas kernels for 15% -> 18%
where the time goes in v3:
time: 62.4 us; the launch traced here: 62.3 us
  starting transfers between devices  27.7 us (44%)
  waiting for transfers between devices  18.6 us (30%)
  Pallas kernels  14 us (22%)
  local copies, waits for them, and re-layouts  1.58 us (3%)
    ppermute x17, starting transfers between devices, permute(): return lax.ppermute(x, 'occ', [(i, i ^ flip) for i in range(n)])  18.3 us
    ppermute x17, waiting for transfers between devices, permute(): return lax.ppermute(x, 'occ', [(i, i ^ flip) for i in range(n)])  14.3 us
    ppermute x6, starting transfers between devices, permute(): lax.ppermute(x, ('occ', 'vir'), [(i * v + j, (i ^ flip) * v + (j ^ swap))...  9.41 us
    ppermute x6, waiting for transfers between devices, permute(): lax.ppermute(x, ('occ', 'vir'), [(i * v + j, (i ^ flip) * v + (j ^ swap))...  4.37 us
    pallas_call x1, Pallas kernels, near_of(): pl.pallas_call(functools.partial(near_kernel, step), grid=(triples // ste...  4.04 us
    pallas_call x2, Pallas kernels, last(): pl.pallas_call(functools.partial(last_kernel, norm, scale), in_specs=[who...  3.04 us
    pallas_call x2, Pallas kernels, gram(): pl.pallas_call(gram_kernel, in_specs=[VMEM()] * (len(xs) + 1), out_specs=...  1.93 us
    pallas_call x1, Pallas kernels, prepare(): pl.pallas_call(prepare_kernel, grid=(1,), in_specs=[pl.BlockSpec((triples...  1.87 us
  transfers between devices with their start and end apart: 23, of which 9 were waited for; matrix products, arithmetic and copies ran while one was open for 0% of the time, Pallas kernels for 18%

profile of v3, /device:TPU:0, one launch (start us, length us, event | category | flops | bytes accessed | tf_op | source)
XLA Modules:
  0.0 62.3 jit_solution(5713050795442167430)
XLA Ops:
  0.0 1.6 %pack.1 = (bf16[40,5120]{1,0:T(8,128)(2,1)S(1)}, bf16[64,5120]{1,0:T(8,128)(2,1)S(1)}) custom-call(bf16[16,160,320]{2,1,0:T(8,128)(2,1)} %lam_ref.5, bf16[160,320]{1,0:T(8,128)(2,1)} %bitcast.2, bf16[40,160]{1,0:T(8,128)(2,1)} %doubles_ref.3), custom_call_target="tpu_custom_call" | custom-call | flops 983040 | bytes 1966080 | tf_op jit(solution)/shard_map/pack/pallas_call | solution.py:88
  1.6 3.0 %collective-permute-start.1 = (bf16[40,5120]{1,0:T(8,128)(2,1)S(1)}, bf16[40,5120]{1,0:T(8,128)(2,1)S(1)}, u32[]{:S(2)}, u32[]{:S(2)}) collective-permute-start(bf16[40,5120]{1,0:T(8,128)(2,1)S(1)} %get-tuple-element.15.first_ref), channel_id=1, source_target_pairs={{0,1},{1,0},{2,3},{3,2},{4,5},{5,4},{6,7},{7,6},{8,9},{9,8},{10,11... | collective-permute-start | bytes 1228808 | tf_op jit(solution)/shard_map/ppermute | solution.py:287
  4.6 0.1 collective-permute-start.9
  4.7 0.1 fusion.keep_ref
  4.8 1.5 %copy-done.1 = bf16[16,160,320]{2,1,0:T(8,128)(2,1)S(1)} copy-done((bf16[16,160,320]{2,1,0:T(8,128)(2,1)S(1)}, bf16[16,160,320]{2,1,0:T(8,128)(2,1)}, u32[]{:S(2)}) %copy-start.1) | copy-done | bytes 1638424
  6.4 1.9 %prepare.1 = (bf16[64,5120]{1,0:T(8,128)(2,1)S(1)}, bf16[160,5120]{1,0:T(8,128)(2,1)S(1)}, f32[40,640]{1,0:T(8,128)S(1)}) custom-call(bf16[16,160,320]{2,1,0:T(8,128)(2,1)S(1)} %copy-done, bf16[40,5120]{1,0:T(8,128)(2,1)S(1)} %get-tuple-element.15.first_ref, bf16[64,5120]{1,0:T(8,128)(2,1)S(1)} %get-tuple-element.16.early_ref, ...), custom_call_target="tpu_custom_call" | custom-call | flops 262144000 | bytes 4915200 | tf_op jit(solution)/shard_map/prepare/pallas_call | solution.py:138
  8.2 0.1 collective-permute-start.2
  8.3 2.0 %collective-permute-start.3 = (f32[40,640]{1,0:T(8,128)S(1)}, f32[40,640]{1,0:T(8,128)S(1)}, u32[]{:S(2)}, u32[]{:S(2)}) collective-permute-start(f32[40,640]{1,0:T(8,128)S(1)} %get-tuple-element.18), channel_id=1, source_target_pairs={{0,4},{2,6},{4,0},{6,2},{8,12},{10,14},{12,8},{14,10},{16,20},{18,... | collective-permute-start | bytes 307208 | tf_op jit(solution)/shard_map/ppermute | solution.py:286
  10.3 0.1 collective-permute-start.4
  10.4 3.7 %collective-permute-done.3 = f32[40,640]{1,0:T(8,128)S(1)} collective-permute-done((f32[40,640]{1,0:T(8,128)S(1)}, f32[40,640]{1,0:T(8,128)S(1)}, u32[]{:S(2)}, u32[]{:S(2)}) %collective-permute-start.3) | collective-permute-done | bytes 102432 | tf_op jit(solution)/shard_map/ppermute | solution.py:286
  14.1 1.6 %collective-permute-done.4 = f32[40,640]{1,0:T(8,128)S(1)} collective-permute-done((f32[40,640]{1,0:T(8,128)S(1)}, f32[40,640]{1,0:T(8,128)S(1)}, u32[]{:S(2)}, u32[]{:S(2)}) %collective-permute-start.4) | collective-permute-done | bytes 102432 | tf_op jit(solution)/shard_map/ppermute | solution.py:286
  15.8 0.5 collective-permute-start.5
  16.3 1.7 %collective-permute-start = (bf16[64,5120]{1,0:T(8,128)(2,1)S(1)}, bf16[64,5120]{1,0:T(8,128)(2,1)S(1)}, u32[]{:S(2)}, u32[]{:S(2)}) collective-permute-start(bf16[64,5120]{1,0:T(8,128)(2,1)S(1)} %get-tuple-element.17), channel_id=1, source_target_pairs={{0,1},{1,0},{2,3},{3,2},{4,5},{5,4},{6,7},{7,6},{8,9},{9,8},{10,11... | collective-permute-start | bytes 1966088 | tf_op jit(solution)/shard_map/ppermute | solution.py:287
  18.0 1.6 %collective-permute-start.6 = (f32[40,640]{1,0:T(8,128)S(1)}, f32[40,640]{1,0:T(8,128)S(1)}, u32[]{:S(2)}, u32[]{:S(2)}) collective-permute-start(f32[40,640]{1,0:T(8,128)S(1)} %add_add_fusion.1), channel_id=1, source_target_pairs={{0,8},{2,10},{4,12},{6,14},{8,0},{10,2},{12,4},{14,6},{16,24},{18,... | collective-permute-start | bytes 307208 | tf_op jit(solution)/shard_map/ppermute | solution.py:286
  19.6 2.6 %collective-permute-start.7 = (f32[40,640]{1,0:T(8,128)S(1)}, f32[40,640]{1,0:T(8,128)S(1)}, u32[]{:S(2)}, u32[]{:S(2)}) collective-permute-start(f32[40,640]{1,0:T(8,128)S(1)} %add_add_fusion.1), channel_id=1, source_target_pairs={{0,16},{2,18},{4,20},{6,22},{8,24},{10,26},{12,28},{14,30},{16,0},... | collective-permute-start | bytes 307208 | tf_op jit(solution)/shard_map/ppermute | solution.py:286
  22.2 0.0 collective-permute-done.5.other_ref
  22.2 0.2 collective-permute-start.8
  22.4 4.0 %near.1.near_ref = f32[16,160,320]{2,1,0:T(8,128)S(1)} custom-call(f32[16,320]{1,0:T(8,128)S(1)} %fusion.keep_ref, bf16[16,160,320]{2,1,0:T(8,128)(2,1)S(1)} %copy-done, bf16[16,160,320]{2,1,0:T(8,128)(2,1)S(1)} %copy-done.2, bf16[40,320]{1,0:T(8,128)(2,1)S(1)} %bitcast.4, bf16[160,320]{1,0:T(8,128)(2,1)S(1)} %bitcast.3, bf16[40,160]{1,0:T(8,128)(2,1)S(1)} %copy-done.4, ...), custom_call_target="tpu_custom_call" | custom-call | flops 629145600 | bytes 6553600 | tf_op jit(solution)/shard_map/near/pallas_call | solution.py:203
  26.4 2.5 %collective-permute-done.9.refs_1_.refs_2_ = bf16[64,5120]{1,0:T(8,128)(2,1)S(1)} collective-permute-done((bf16[64,5120]{1,0:T(8,128)(2,1)S(1)}, bf16[64,5120]{1,0:T(8,128)(2,1)S(1)}, u32[]{:S(2)}, u32[]{:S(2)}) %collective-permute-start.9) | collective-permute-done | bytes 655392 | tf_op jit(solution)/shard_map/ppermute | solution.py:287
  29.0 1.2 %gram.2 = f32[24,640]{1,0:T(8,128)S(1)} custom-call(bf16[40,5120]{1,0:T(8,128)(2,1)S(1)} %collective-permute-done.1.refs_0_.refs_1_, bf16[64,5120]{1,0:T(8,128)(2,1)S(1)} %collective-permute-done.9.refs_1_.refs_2_, bf16[160,5120]{1,0:T(8,128)(2,1)S(1)} %get-tuple-element.21.refs_2_.refs_1_), custom_call_target="tpu_custom_call" | custom-call | flops 157286400 | bytes 2621440 | tf_op jit(solution)/shard_map/gram/pallas_call | solution.py:162
  30.2 0.1 collective-permute-start.10
  30.3 2.1 %collective-permute-start.11 = (f32[24,640]{1,0:T(8,128)S(1)}, f32[24,640]{1,0:T(8,128)S(1)}, u32[]{:S(2)}, u32[]{:S(2)}) collective-permute-start(f32[24,640]{1,0:T(8,128)S(1)} %gram.2), channel_id=1, source_target_pairs={{0,4},{2,6},{4,0},{6,2},{8,12},{10,14},{12,8},{14,10},{16,20},{18,... | collective-permute-start | bytes 184328 | tf_op jit(solution)/shard_map/ppermute | solution.py:286
  32.4 0.0 collective-permute-done.7
  32.4 0.1 collective-permute-start.12
  32.6 0.0 collective-permute-done.8
  32.6 0.0 collective-permute-done.10
  32.6 2.4 %collective-permute-done.11 = f32[24,640]{1,0:T(8,128)S(1)} collective-permute-done((f32[24,640]{1,0:T(8,128)S(1)}, f32[24,640]{1,0:T(8,128)S(1)}, u32[]{:S(2)}, u32[]{:S(2)}) %collective-permute-start.11) | collective-permute-done | bytes 61472 | tf_op jit(solution)/shard_map/ppermute | solution.py:286
  35.0 1.4 %collective-permute-done.12 = f32[24,640]{1,0:T(8,128)S(1)} collective-permute-done((f32[24,640]{1,0:T(8,128)S(1)}, f32[24,640]{1,0:T(8,128)S(1)}, u32[]{:S(2)}, u32[]{:S(2)}) %collective-permute-start.12) | collective-permute-done | bytes 61472 | tf_op jit(solution)/shard_map/ppermute | solution.py:286
  36.4 1.6 %collective-permute-start.19 = (f32[24,640]{1,0:T(8,128)S(1)}, f32[24,640]{1,0:T(8,128)S(1)}, u32[]{:S(2)}, u32[]{:S(2)}) collective-permute-start(f32[24,640]{1,0:T(8,128)S(1)} %add_add_fusion.2), channel_id=1, source_target_pairs={{0,8},{2,10},{4,12},{6,14},{8,0},{10,2},{12,4},{14,6},{16,24},{18,... | collective-permute-start | bytes 184328 | tf_op jit(solution)/shard_map/ppermute | solution.py:286
  38.1 2.6 %collective-permute-start.20 = (f32[24,640]{1,0:T(8,128)S(1)}, f32[24,640]{1,0:T(8,128)S(1)}, u32[]{:S(2)}, u32[]{:S(2)}) collective-permute-start(f32[24,640]{1,0:T(8,128)S(1)} %add_add_fusion.2), channel_id=1, source_target_pairs={{0,16},{2,18},{4,20},{6,22},{8,24},{10,26},{12,28},{14,30},{16,0},... | collective-permute-start | bytes 184328 | tf_op jit(solution)/shard_map/ppermute | solution.py:286
  40.7 0.2 collective-permute-start.21
  40.9 1.5 %add_own.1.refs_3_ = f32[16,160,320]{2,1,0:T(8,128)S(1)} custom-call(f32[16,320]{1,0:T(8,128)S(1)} %fusion.keep_ref, bf16[16,160,320]{2,1,0:T(8,128)(2,1)S(1)} %copy-done, f32[16,160,320]{2,1,0:T(8,128)S(1)} %near.1.near_ref, f32[40,640]{1,0:T(8,128)S(1)} %add_add_fusion.den_ref), custom_call_target="tpu_custom_call", output_to_operand_aliasing={{}: (2, {})} | custom-call | flops 262144000 | bytes 8192000 | tf_op jit(solution)/shard_map/add_own/pallas_call | solution.py:227
  42.4 0.0 collective-permute-done.refs_0_
  42.4 0.7 %gram.3 = f32[16,640]{1,0:T(8,128)S(1)} custom-call(bf16[64,5120]{1,0:T(8,128)(2,1)S(1)} %collective-permute-done.refs_0_, bf16[160,5120]{1,0:T(8,128)(2,1)S(1)} %get-tuple-element.21.refs_2_.refs_1_), custom_call_target="tpu_custom_call" | custom-call | flops 104857600 | bytes 2293760 | tf_op jit(solution)/shard_map/gram/pallas_call | solution.py:162
  43.1 0.1 collective-permute-start.13
  43.2 1.2 %collective-permute-done.13 = f32[16,640]{1,0:T(8,128)S(1)} collective-permute-done((f32[16,640]{1,0:T(8,128)S(1)}, f32[16,640]{1,0:T(8,128)S(1)}, u32[]{:S(2)}, u32[]{:S(2)}) %collective-permute-start.13) | collective-permute-done | bytes 40992 | tf_op jit(solution)/shard_map/ppermute | solution.py:286
  44.4 1.6 %collective-permute-start.14 = (f32[16,640]{1,0:T(8,128)S(1)}, f32[16,640]{1,0:T(8,128)S(1)}, u32[]{:S(2)}, u32[]{:S(2)}) collective-permute-start(f32[16,640]{1,0:T(8,128)S(1)} %add.60), channel_id=1, source_target_pairs={{0,1},{1,0},{2,3},{3,2},{4,5},{5,4},{6,7},{7,6},{8,9},{9,8},{10,11... | collective-permute-start | bytes 122888 | tf_op jit(solution)/shard_map/ppermute | solution.py:287
  46.0 1.5 %collective-permute-start.15 = (f32[16,640]{1,0:T(8,128)S(1)}, f32[16,640]{1,0:T(8,128)S(1)}, u32[]{:S(2)}, u32[]{:S(2)}) collective-permute-start(f32[16,640]{1,0:T(8,128)S(1)} %add.60), channel_id=1, source_target_pairs={{0,5},{1,4},{2,7},{3,6},{4,1},{5,0},{6,3},{7,2},{8,13},{9,12},{10,... | collective-permute-start | bytes 122888 | tf_op jit(solution)/shard_map/ppermute | solution.py:287
  47.4 0.0 collective-permute-done.19
  47.5 1.6 %collective-permute-start.22 = (bf16[24,640]{1,0:T(8,128)(2,1)S(1)}, bf16[24,640]{1,0:T(8,128)(2,1)S(1)}, u32[]{:S(2)}, u32[]{:S(2)}) collective-permute-start(bf16[24,640]{1,0:T(8,128)(2,1)S(1)} %multiply_convert_fusion), channel_id=1, source_target_pairs={{0,1},{1,0},{2,3},{3,2},{4,5},{5,4},{6,7},{7,6},{8,9},{9,8},{10,11... | collective-permute-start | bytes 92168 | tf_op jit(solution)/shard_map/ppermute | solution.py:287
  49.0 1.8 %collective-permute-done.15 = f32[16,640]{1,0:T(8,128)S(1)} collective-permute-done((f32[16,640]{1,0:T(8,128)S(1)}, f32[16,640]{1,0:T(8,128)S(1)}, u32[]{:S(2)}, u32[]{:S(2)}) %collective-permute-start.15) | collective-permute-done | bytes 40992 | tf_op jit(solution)/shard_map/ppermute | solution.py:287
  50.9 1.6 %collective-permute-start.16 = (f32[16,640]{1,0:T(8,128)S(1)}, f32[16,640]{1,0:T(8,128)S(1)}, u32[]{:S(2)}, u32[]{:S(2)}) collective-permute-start(f32[16,640]{1,0:T(8,128)S(1)} %add.61), channel_id=1, source_target_pairs={{0,8},{2,10},{4,12},{6,14},{8,0},{10,2},{12,4},{14,6},{16,24},{18,... | collective-permute-start | bytes 122888 | tf_op jit(solution)/shard_map/ppermute | solution.py:286
  52.4 2.6 %collective-permute-start.17 = (f32[16,640]{1,0:T(8,128)S(1)}, f32[16,640]{1,0:T(8,128)S(1)}, u32[]{:S(2)}, u32[]{:S(2)}) collective-permute-start(f32[16,640]{1,0:T(8,128)S(1)} %add.61), channel_id=1, source_target_pairs={{0,16},{2,18},{4,20},{6,22},{8,24},{10,26},{12,28},{14,30},{16,0},... | collective-permute-start | bytes 122888 | tf_op jit(solution)/shard_map/ppermute | solution.py:286
  55.0 0.2 collective-permute-start.18
  55.3 1.6 %last.2.refs_4_ = bf16[16,160,320]{2,1,0:T(8,128)(2,1)} custom-call(f32[16,320]{1,0:T(8,128)S(1)} %fusion.keep_ref, bf16[24,640]{1,0:T(8,128)(2,1)S(1)} %collective-permute-done.22.den_ref, bf16[64,5120]{1,0:T(8,128)(2,1)S(1)} %collective-permute-done.refs_0_, bf16[40,5120]{1,0:T(8,128)(2,1)S(1)} %collective-permute-done.1.refs_0_.refs_1_, ...), custom_call_target="tpu_custom_call" | custom-call | flops 157286400 | bytes 2949120 | tf_op jit(solution)/shard_map/last/pallas_call | solution.py:270
  56.9 1.3 %collective-permute-done.17 = f32[16,640]{1,0:T(8,128)S(1)} collective-permute-done((f32[16,640]{1,0:T(8,128)S(1)}, f32[16,640]{1,0:T(8,128)S(1)}, u32[]{:S(2)}, u32[]{:S(2)}) %collective-permute-start.17) | collective-permute-done | bytes 40992 | tf_op jit(solution)/shard_map/ppermute | solution.py:286
  58.2 2.6 %collective-permute-done.18 = f32[16,640]{1,0:T(8,128)S(1)} collective-permute-done((f32[16,640]{1,0:T(8,128)S(1)}, f32[16,640]{1,0:T(8,128)S(1)}, u32[]{:S(2)}, u32[]{:S(2)}) %collective-permute-start.18) | collective-permute-done | bytes 40992 | tf_op jit(solution)/shard_map/ppermute | solution.py:286
  60.9 1.4 %last.3 = bf16[16,160,320]{2,1,0:T(8,128)(2,1)} custom-call(f32[16,320]{1,0:T(8,128)S(1)} %fusion.keep_ref, bf16[16,640]{1,0:T(8,128)(2,1)S(1)} %multiply_convert_fusion.1.den_ref, bf16[64,5120]{1,0:T(8,128)(2,1)S(1)} %collective-permute-done.refs_0_, bf16[40,5120]{1,0:T(8,128)(2,1)S(1)} %collective-permute-done.1.refs_0_.refs_1_, ...), custom_call_target="tpu_custom_call", output_to_operand_aliasing={{}: (6, {})} | custom-call | flops 104857600 | bytes 1966080 | tf_op jit(solution)/shard_map/last/pallas_call | solution.py:270
  (30 shorter events, 0.2 us)
Async XLA Ops:
  0.0 4.8 %copy-start = (bf16[16,160,320]{2,1,0:T(8,128)(2,1)S(1)}, bf16[16,160,320]{2,1,0:T(8,128)(2,1)}, u32[]{:S(2)}) copy-start(bf16[16,160,320]{2,1,0:T(8,128)(2,1)} %lam_ref.5) | copy-start | bytes 4915204
  0.0 4.7 %copy-start.6 = (s32[16]{0:T(128)S(1)}, s32[16]{0:T(128)}, u32[]{:S(2)}) copy-start(s32[16]{0:T(128)} %param.8) | copy-start | bytes 196
  1.6 14.1 %collective-permute-start.1 = (bf16[40,5120]{1,0:T(8,128)(2,1)S(1)}, bf16[40,5120]{1,0:T(8,128)(2,1)S(1)}, u32[]{:S(2)}, u32[]{:S(2)}) collective-permute-start(bf16[40,5120]{1,0:T(8,128)(2,1)S(1)} %get-tuple-element.15.first_ref), channel_id=1, source_target_pairs={{0,1},{1,0},{2,3},{3,2},{4,5},{5,4},{6,7},{7,6},{8,9},{9,8},{10,11... | collective-permute-start | bytes 1228808 | tf_op jit(solution)/shard_map/ppermute | solution.py:287
  4.6 24.3 %collective-permute-start.9 = (bf16[64,5120]{1,0:T(8,128)(2,1)S(1)}, bf16[64,5120]{1,0:T(8,128)(2,1)S(1)}, u32[]{:S(2)}, u32[]{:S(2)}) collective-permute-start(bf16[64,5120]{1,0:T(8,128)(2,1)S(1)} %get-tuple-element.16.early_ref), channel_id=1, source_target_pairs={{0,1},{1,0},{2,3},{3,2},{4,5},{5,4},{6,7},{7,6},{8,9},{9,8},{10,11... | collective-permute-start | bytes 1966088 | tf_op jit(solution)/shard_map/ppermute | solution.py:287
  4.8 1.5 %copy-start.1 = (bf16[16,160,320]{2,1,0:T(8,128)(2,1)S(1)}, bf16[16,160,320]{2,1,0:T(8,128)(2,1)}, u32[]{:S(2)}) copy-start(bf16[16,160,320]{2,1,0:T(8,128)(2,1)} %amp_ref.3) | copy-start | bytes 4915204
  6.3 16.0 %copy-start.2 = (bf16[16,160,320]{2,1,0:T(8,128)(2,1)S(1)}, bf16[16,160,320]{2,1,0:T(8,128)(2,1)}, u32[]{:S(2)}) copy-start(bf16[16,160,320]{2,1,0:T(8,128)(2,1)} %amp_ref.3) | copy-start | bytes 4915204
  6.3 16.0 %copy-start.3 = (bf16[320,160]{0,1:T(8,128)(2,1)S(1)}, bf16[320,160]{0,1:T(8,128)(2,1)}, u32[]{:S(2)}) copy-start(bf16[320,160]{0,1:T(8,128)(2,1)} %param.9) | copy-start | bytes 307204
  6.4 16.0 %copy-start.4 = (bf16[40,160]{1,0:T(8,128)(2,1)S(1)}, bf16[40,160]{1,0:T(8,128)(2,1)}, u32[]{:S(2)}) copy-start(bf16[40,160]{1,0:T(8,128)(2,1)} %doubles_ref.3) | copy-start | bytes 38404
  6.4 16.0 %copy-start.5 = (bf16[320,40]{0,1:T(8,128)(2,1)S(1)}, bf16[320,40]{0,1:T(8,128)(2,1)}, u32[]{:S(2)}) copy-start(bf16[320,40]{0,1:T(8,128)(2,1)} %param.10) | copy-start | bytes 76804
  8.2 2.2 %collective-permute-start.2 = (f32[40,640]{1,0:T(8,128)S(1)}, f32[40,640]{1,0:T(8,128)S(1)}, u32[]{:S(2)}, u32[]{:S(2)}) collective-permute-start(f32[40,640]{1,0:T(8,128)S(1)} %get-tuple-element.18), channel_id=1, source_target_pairs={{0,2},{2,0},{4,6},{6,4},{8,10},{10,8},{12,14},{14,12},{16,18},{18,... | collective-permute-start | bytes 307208 | tf_op jit(solution)/shard_map/ppermute | solution.py:286
  8.3 5.8 %collective-permute-start.3 = (f32[40,640]{1,0:T(8,128)S(1)}, f32[40,640]{1,0:T(8,128)S(1)}, u32[]{:S(2)}, u32[]{:S(2)}) collective-permute-start(f32[40,640]{1,0:T(8,128)S(1)} %get-tuple-element.18), channel_id=1, source_target_pairs={{0,4},{2,6},{4,0},{6,2},{8,12},{10,14},{12,8},{14,10},{16,20},{18,... | collective-permute-start | bytes 307208 | tf_op jit(solution)/shard_map/ppermute | solution.py:286
  10.3 5.4 %collective-permute-start.4 = (f32[40,640]{1,0:T(8,128)S(1)}, f32[40,640]{1,0:T(8,128)S(1)}, u32[]{:S(2)}, u32[]{:S(2)}) collective-permute-start(f32[40,640]{1,0:T(8,128)S(1)} %get-tuple-element.18), channel_id=1, source_target_pairs={{0,6},{2,4},{4,2},{6,0},{8,14},{10,12},{12,10},{14,8},{16,22},{18,... | collective-permute-start | bytes 307208 | tf_op jit(solution)/shard_map/ppermute | solution.py:286
  15.8 6.4 %collective-permute-start.5 = (bf16[8,5120]{1,0:T(8,128)(2,1)S(1)}, bf16[8,5120]{1,0:T(8,128)(2,1)S(1)}, u32[]{:S(2)}, u32[]{:S(2)}) collective-permute-start(bf16[8,5120]{1,0:T(8,128)(2,1)S(1)} %slice.3.mine_ref), channel_id=1, source_target_pairs={{0,2},{2,0},{4,6},{6,4},{8,10},{10,8},{12,14},{14,12},{16,18},{18,... | collective-permute-start | bytes 245768 | tf_op jit(solution)/shard_map/ppermute | solution.py:286
  16.3 26.1 %collective-permute-start = (bf16[64,5120]{1,0:T(8,128)(2,1)S(1)}, bf16[64,5120]{1,0:T(8,128)(2,1)S(1)}, u32[]{:S(2)}, u32[]{:S(2)}) collective-permute-start(bf16[64,5120]{1,0:T(8,128)(2,1)S(1)} %get-tuple-element.17), channel_id=1, source_target_pairs={{0,1},{1,0},{2,3},{3,2},{4,5},{5,4},{6,7},{7,6},{8,9},{9,8},{10,11... | collective-permute-start | bytes 1966088 | tf_op jit(solution)/shard_map/ppermute | solution.py:287
  18.0 12.3 %collective-permute-start.6 = (f32[40,640]{1,0:T(8,128)S(1)}, f32[40,640]{1,0:T(8,128)S(1)}, u32[]{:S(2)}, u32[]{:S(2)}) collective-permute-start(f32[40,640]{1,0:T(8,128)S(1)} %add_add_fusion.1), channel_id=1, source_target_pairs={{0,8},{2,10},{4,12},{6,14},{8,0},{10,2},{12,4},{14,6},{16,24},{18,... | collective-permute-start | bytes 307208 | tf_op jit(solution)/shard_map/ppermute | solution.py:286
  19.6 12.9 %collective-permute-start.7 = (f32[40,640]{1,0:T(8,128)S(1)}, f32[40,640]{1,0:T(8,128)S(1)}, u32[]{:S(2)}, u32[]{:S(2)}) collective-permute-start(f32[40,640]{1,0:T(8,128)S(1)} %add_add_fusion.1), channel_id=1, source_target_pairs={{0,16},{2,18},{4,20},{6,22},{8,24},{10,26},{12,28},{14,30},{16,0},... | collective-permute-start | bytes 307208 | tf_op jit(solution)/shard_map/ppermute | solution.py:286
  22.2 10.4 %collective-permute-start.8 = (f32[40,640]{1,0:T(8,128)S(1)}, f32[40,640]{1,0:T(8,128)S(1)}, u32[]{:S(2)}, u32[]{:S(2)}) collective-permute-start(f32[40,640]{1,0:T(8,128)S(1)} %add_add_fusion.1), channel_id=1, source_target_pairs={{0,24},{2,26},{4,28},{6,30},{8,16},{10,18},{12,20},{14,22},{16,8},... | collective-permute-start | bytes 307208 | tf_op jit(solution)/shard_map/ppermute | solution.py:286
  30.2 2.4 %collective-permute-start.10 = (f32[24,640]{1,0:T(8,128)S(1)}, f32[24,640]{1,0:T(8,128)S(1)}, u32[]{:S(2)}, u32[]{:S(2)}) collective-permute-start(f32[24,640]{1,0:T(8,128)S(1)} %gram.2), channel_id=1, source_target_pairs={{0,2},{2,0},{4,6},{6,4},{8,10},{10,8},{12,14},{14,12},{16,18},{18,... | collective-permute-start | bytes 184328 | tf_op jit(solution)/shard_map/ppermute | solution.py:286
  30.3 4.7 %collective-permute-start.11 = (f32[24,640]{1,0:T(8,128)S(1)}, f32[24,640]{1,0:T(8,128)S(1)}, u32[]{:S(2)}, u32[]{:S(2)}) collective-permute-start(f32[24,640]{1,0:T(8,128)S(1)} %gram.2), channel_id=1, source_target_pairs={{0,4},{2,6},{4,0},{6,2},{8,12},{10,14},{12,8},{14,10},{16,20},{18,... | collective-permute-start | bytes 184328 | tf_op jit(solution)/shard_map/ppermute | solution.py:286
  32.4 4.0 %collective-permute-start.12 = (f32[24,640]{1,0:T(8,128)S(1)}, f32[24,640]{1,0:T(8,128)S(1)}, u32[]{:S(2)}, u32[]{:S(2)}) collective-permute-start(f32[24,640]{1,0:T(8,128)S(1)} %gram.2), channel_id=1, source_target_pairs={{0,6},{2,4},{4,2},{6,0},{8,14},{10,12},{12,10},{14,8},{16,22},{18,... | collective-permute-start | bytes 184328 | tf_op jit(solution)/shard_map/ppermute | solution.py:286
  36.4 11.0 %collective-permute-start.19 = (f32[24,640]{1,0:T(8,128)S(1)}, f32[24,640]{1,0:T(8,128)S(1)}, u32[]{:S(2)}, u32[]{:S(2)}) collective-permute-start(f32[24,640]{1,0:T(8,128)S(1)} %add_add_fusion.2), channel_id=1, source_target_pairs={{0,8},{2,10},{4,12},{6,14},{8,0},{10,2},{12,4},{14,6},{16,24},{18,... | collective-permute-start | bytes 184328 | tf_op jit(solution)/shard_map/ppermute | solution.py:286
  38.1 9.4 %collective-permute-start.20 = (f32[24,640]{1,0:T(8,128)S(1)}, f32[24,640]{1,0:T(8,128)S(1)}, u32[]{:S(2)}, u32[]{:S(2)}) collective-permute-start(f32[24,640]{1,0:T(8,128)S(1)} %add_add_fusion.2), channel_id=1, source_target_pairs={{0,16},{2,18},{4,20},{6,22},{8,24},{10,26},{12,28},{14,30},{16,0},... | collective-permute-start | bytes 184328 | tf_op jit(solution)/shard_map/ppermute | solution.py:286
  40.7 6.8 %collective-permute-start.21 = (f32[24,640]{1,0:T(8,128)S(1)}, f32[24,640]{1,0:T(8,128)S(1)}, u32[]{:S(2)}, u32[]{:S(2)}) collective-permute-start(f32[24,640]{1,0:T(8,128)S(1)} %add_add_fusion.2), channel_id=1, source_target_pairs={{0,24},{2,26},{4,28},{6,30},{8,16},{10,18},{12,20},{14,22},{16,8},... | collective-permute-start | bytes 184328 | tf_op jit(solution)/shard_map/ppermute | solution.py:286
  43.1 1.3 %collective-permute-start.13 = (f32[16,640]{1,0:T(8,128)S(1)}, f32[16,640]{1,0:T(8,128)S(1)}, u32[]{:S(2)}, u32[]{:S(2)}) collective-permute-start(f32[16,640]{1,0:T(8,128)S(1)} %gram.3), channel_id=1, source_target_pairs={{0,2},{2,0},{4,6},{6,4},{8,10},{10,8},{12,14},{14,12},{16,18},{18,... | collective-permute-start | bytes 122888 | tf_op jit(solution)/shard_map/ppermute | solution.py:286
  44.4 4.6 %collective-permute-start.14 = (f32[16,640]{1,0:T(8,128)S(1)}, f32[16,640]{1,0:T(8,128)S(1)}, u32[]{:S(2)}, u32[]{:S(2)}) collective-permute-start(f32[16,640]{1,0:T(8,128)S(1)} %add.60), channel_id=1, source_target_pairs={{0,1},{1,0},{2,3},{3,2},{4,5},{5,4},{6,7},{7,6},{8,9},{9,8},{10,11... | collective-permute-start | bytes 122888 | tf_op jit(solution)/shard_map/ppermute | solution.py:287
  46.0 4.9 %collective-permute-start.15 = (f32[16,640]{1,0:T(8,128)S(1)}, f32[16,640]{1,0:T(8,128)S(1)}, u32[]{:S(2)}, u32[]{:S(2)}) collective-permute-start(f32[16,640]{1,0:T(8,128)S(1)} %add.60), channel_id=1, source_target_pairs={{0,5},{1,4},{2,7},{3,6},{4,1},{5,0},{6,3},{7,2},{8,13},{9,12},{10,... | collective-permute-start | bytes 122888 | tf_op jit(solution)/shard_map/ppermute | solution.py:287
  47.5 7.8 %collective-permute-start.22 = (bf16[24,640]{1,0:T(8,128)(2,1)S(1)}, bf16[24,640]{1,0:T(8,128)(2,1)S(1)}, u32[]{:S(2)}, u32[]{:S(2)}) collective-permute-start(bf16[24,640]{1,0:T(8,128)(2,1)S(1)} %multiply_convert_fusion), channel_id=1, source_target_pairs={{0,1},{1,0},{2,3},{3,2},{4,5},{5,4},{6,7},{7,6},{8,9},{9,8},{10,11... | collective-permute-start | bytes 92168 | tf_op jit(solution)/shard_map/ppermute | solution.py:287
  50.9 6.0 %collective-permute-start.16 = (f32[16,640]{1,0:T(8,128)S(1)}, f32[16,640]{1,0:T(8,128)S(1)}, u32[]{:S(2)}, u32[]{:S(2)}) collective-permute-start(f32[16,640]{1,0:T(8,128)S(1)} %add.61), channel_id=1, source_target_pairs={{0,8},{2,10},{4,12},{6,14},{8,0},{10,2},{12,4},{14,6},{16,24},{18,... | collective-permute-start | bytes 122888 | tf_op jit(solution)/shard_map/ppermute | solution.py:286
  52.4 5.8 %collective-permute-start.17 = (f32[16,640]{1,0:T(8,128)S(1)}, f32[16,640]{1,0:T(8,128)S(1)}, u32[]{:S(2)}, u32[]{:S(2)}) collective-permute-start(f32[16,640]{1,0:T(8,128)S(1)} %add.61), channel_id=1, source_target_pairs={{0,16},{2,18},{4,20},{6,22},{8,24},{10,26},{12,28},{14,30},{16,0},... | collective-permute-start | bytes 122888 | tf_op jit(solution)/shard_map/ppermute | solution.py:286
  55.0 5.8 %collective-permute-start.18 = (f32[16,640]{1,0:T(8,128)S(1)}, f32[16,640]{1,0:T(8,128)S(1)}, u32[]{:S(2)}, u32[]{:S(2)}) collective-permute-start(f32[16,640]{1,0:T(8,128)S(1)} %add.61), channel_id=1, source_target_pairs={{0,24},{2,26},{4,28},{6,30},{8,16},{10,18},{12,20},{14,22},{16,8},... | collective-permute-start | bytes 122888 | tf_op jit(solution)/shard_map/ppermute | solution.py:286

commit v4 on v3

--- a/solution.py
+++ b/solution.py
@@ -237,47 +237,78 @@
     )(keep, lam, near, den)
 
 
-def last_kernel(norm, scale, keep_ref, den_ref, *refs):
-    *got, near_ref, _, o_ref = refs
-    triples, rows, width = near_ref.shape
+def add_product(o_ref, near_ref, keep_ref, den, got, scale, first):
+    triples, _, width = o_ref.shape
     main = width // 128 * 128
     tail = width - main
-    den = unfold(den_ref[...].astype(F32), sum(g.shape[0] // 16 * 16 for g in got))
-    if norm is not None:
-        den = den / norm
-    den = den.astype(BF16)
-    all_got = jnp.concatenate([g[: g.shape[0] // 16 * 16] for g in got], axis=0)
+    ends_at = got.shape[1] - got.shape[1] // width * tail
 
     def product(lo, size):
-        return jnp.dot(den, all_got[:, lo : lo + size], preferred_element_type=F32) * scale
+        return jnp.dot(den, got[:, lo : lo + size], preferred_element_type=F32) * scale
 
     for t in range(0, triples, 2):
-        ends = product(triples * main + t * tail, 2 * tail)
+        ends = product(ends_at + (first + t) * tail, 2 * tail)
         for u in (t, t + 1):
             s = (u - t) * tail
-            keep = keep_ref[u : u + 1, :]
-            o_ref[u, :, :main] = (near_ref[u, :, :main] + product(u * main, main) * keep[:, :main]).astype(BF16)
+            keep = keep_ref[first + u : first + u + 1, :]
+            o_ref[u, :, :main] = (near_ref[u, :, :main] + product((first + u) * main, main) * keep[:, :main]).astype(BF16)
             o_ref[u, :, main:] = (near_ref[u, :, main:] + ends[:, s : s + tail] * keep[:, main:]).astype(BF16)
 
 
-def last(keep, den, got, near, out, start, rows, norm, scale):
-    triples, _, width = near.shape
-    spec = pl.BlockSpec((pl.Element(triples), pl.Element(rows), pl.Element(width)), lambda i: (0, start, 0))
-    if out is None:
-        out, alias = jnp.zeros((8, 128), BF16), {}
-    else:
-        alias = {len(got) + 3: 0}
-    return pl.pallas_call(
-        functools.partial(last_kernel, norm, scale),
-        in_specs=[whole(keep), whole(den), *map(whole, got), spec, pl.BlockSpec(memory_space=pl.ANY)],
+def early_kernel(scale, keep_ref, den_ref, *refs):
+    *got, near_ref, o_ref, all_ref = refs
+    at = 0
+    for g in got:
+        n = g.shape[0] // 16 * 16
+        all_ref[at : at + n, :] = g[:n]
+        at += n
+    den = unfold(den_ref[...].astype(F32), at).astype(BF16)
+    add_product(o_ref, near_ref, keep_ref, den, all_ref, scale, 0)
+
+
+def early_output(keep, den, got, near, start, scale):
+    triples, rows, width = near.shape
+    spec = pl.BlockSpec((pl.Element(triples), pl.Element(rows - start), pl.Element(width)), lambda i: (0, start, 0))
+    all_got = jax.ShapeDtypeStruct((rows, triples * width), BF16)
+    return pl.pallas_call(
+        functools.partial(early_kernel, scale),
         grid=(1,),
-        out_specs=spec,
-        out_shape=jax.ShapeDtypeStruct(near.shape, BF16),
-        input_output_aliases=alias,
+        in_specs=[whole(keep), whole(den), *map(whole, got), spec],
+        out_specs=[spec, whole(all_got)],
+        out_shape=[jax.ShapeDtypeStruct(near.shape, BF16), all_got],
         compiler_params=params(14),
         cost_estimate=cost(2 * triples * rows * width * 160, triples * rows * width * 6),
-        name="last",
-    )(keep, den, *got, near, out)
+        name="early",
+    )(keep, den, *got, near)
+
+
+def late_kernel(scale, keep_ref, den_ref, got_ref, near_ref, _, o_ref, buf, sems):
+    triples, rows, _ = buf.shape
+    n = triples // PARTS
+    den = unfold(den_ref[...].astype(F32), got_ref.shape[0]).astype(BF16)
+    copies = []
+    for k in range(PARTS):
+        part = buf.at[k * n : (k + 1) * n]
+        add_product(part, near_ref.at[k * n : (k + 1) * n, :rows], keep_ref, den, got_ref, scale, k * n)
+        copies.append(pltpu.make_async_copy(part, o_ref.at[k * n : (k + 1) * n, :rows], sems.at[k]))
+        copies[-1].start()
+    for c in copies:
+        c.wait()
+
+
+def late_output(keep, den, got, near, out, rows, scale):
+    triples, _, width = near.shape
+    return pl.pallas_call(
+        functools.partial(late_kernel, scale),
+        in_specs=[VMEM()] * 4 + [pl.BlockSpec(memory_space=pl.ANY)],
+        out_specs=pl.BlockSpec(memory_space=pl.ANY),
+        out_shape=jax.ShapeDtypeStruct(near.shape, BF16),
+        scratch_shapes=[pltpu.VMEM((triples, rows, width), BF16), pltpu.SemaphoreType.DMA((PARTS,))],
+        input_output_aliases={4: 0},
+        compiler_params=params(8),
+        cost_estimate=cost(2 * triples * rows * width * 160, triples * rows * width * 6),
+        name="late",
+    )(keep, den, got, near, out)
 
 
 def permute(x, flip, swap=0):
@@ -293,7 +324,7 @@
     while bit < n:
         if 2 * bit < n:
             far, mid, close = permute(x, 3 * bit), permute(x, 2 * bit), permute(x, bit)
-            x = (x + close) + (mid + far)
+            x = (far + mid) + (close + x)
             bit *= 4
         else:
             x = x + permute(x, bit)
@@ -345,8 +376,8 @@
     late = (far_sum(late) / norm).astype(BF16)
 
     got = (late_got, first_got, early_got)
-    out = last(keep, early, got, near, None, LATE, early_rows, None, scale)
-    return last(keep, late, got, near, out, 0, LATE, None, scale)
+    out, all_got = early_output(keep, early, got, near, LATE, scale)
+    return late_output(keep, late, all_got, near, out, LATE, scale)
 
 
 def solution(mesh):

time: 62.4 us -> 60.8 us (0.974)
  waiting for transfers between devices: 18.6 us -> 17.2 us
    ppermute x17, waiting for transfers between devices: 14.3 us -> 12.8 us  [permute(): return lax.ppermute(x, 'occ', [(i, i ^ flip) for i in range(n)])]
  transfers between devices with their start and end apart: 23 -> 23, of which waited for: 9 -> 8; matrix products, arithmetic and copies ran while one was open for 0% -> 0% of each run, Pallas kernels for 18% -> 18%
where the time goes in v4:
time: 60.8 us; the launch traced here: 60.7 us
  starting transfers between devices  27.7 us (46%)
  waiting for transfers between devices  17.2 us (28%)
  Pallas kernels  13.8 us (23%)
  local copies, waits for them, and re-layouts  1.58 us (3%)
    ppermute x17, starting transfers between devices, permute(): return lax.ppermute(x, 'occ', [(i, i ^ flip) for i in range(n)])  18.3 us
    ppermute x17, waiting for transfers between devices, permute(): return lax.ppermute(x, 'occ', [(i, i ^ flip) for i in range(n)])  12.8 us
    ppermute x6, starting transfers between devices, permute(): lax.ppermute(x, ('occ', 'vir'), [(i * v + j, (i ^ flip) * v + (j ^ swap))...  9.41 us
    ppermute x6, waiting for transfers between devices, permute(): lax.ppermute(x, ('occ', 'vir'), [(i * v + j, (i ^ flip) * v + (j ^ swap))...  4.39 us
    pallas_call x1, Pallas kernels, near_of(): pl.pallas_call(functools.partial(near_kernel, step), grid=(triples // ste...  4.03 us
    pallas_call x2, Pallas kernels, gram(): pl.pallas_call(gram_kernel, in_specs=[VMEM()] * (len(xs) + 1), out_specs=...  1.93 us
    pallas_call x1, Pallas kernels, prepare(): pl.pallas_call(prepare_kernel, grid=(1,), in_specs=[pl.BlockSpec((triples...  1.84 us
    pallas_call x1, Pallas kernels, early_output(): pl.pallas_call(functools.partial(early_kernel, scale), grid=(1,), in_spec...  1.66 us
  transfers between devices with their start and end apart: 23, of which 8 were waited for; matrix products, arithmetic and copies ran while one was open for 0% of the time, Pallas kernels for 18%

profile of v4, /device:TPU:0, one launch (start us, length us, event | category | flops | bytes accessed | tf_op | source)
XLA Modules:
  0.0 60.7 jit_solution(2486900390418485282)
XLA Ops:
  0.0 1.6 %pack.1 = (bf16[40,5120]{1,0:T(8,128)(2,1)S(1)}, bf16[64,5120]{1,0:T(8,128)(2,1)S(1)}) custom-call(bf16[16,160,320]{2,1,0:T(8,128)(2,1)} %lam_ref.5, bf16[160,320]{1,0:T(8,128)(2,1)} %bitcast.2, bf16[40,160]{1,0:T(8,128)(2,1)} %doubles_ref.3), custom_call_target="tpu_custom_call" | custom-call | flops 983040 | bytes 1966080 | tf_op jit(solution)/shard_map/pack/pallas_call | solution.py:88
  1.6 3.0 %collective-permute-start.1 = (bf16[40,5120]{1,0:T(8,128)(2,1)S(1)}, bf16[40,5120]{1,0:T(8,128)(2,1)S(1)}, u32[]{:S(2)}, u32[]{:S(2)}) collective-permute-start(bf16[40,5120]{1,0:T(8,128)(2,1)S(1)} %get-tuple-element.17.first_ref), channel_id=1, source_target_pairs={{0,1},{1,0},{2,3},{3,2},{4,5},{5,4},{6,7},{7,6},{8,9},{9,8},{10,11... | collective-permute-start | bytes 1228808 | tf_op jit(solution)/shard_map/ppermute | solution.py:318
  4.6 0.1 collective-permute-start.9
  4.7 0.1 fusion.keep_ref
  4.8 1.5 %copy-done.1 = bf16[16,160,320]{2,1,0:T(8,128)(2,1)S(1)} copy-done((bf16[16,160,320]{2,1,0:T(8,128)(2,1)S(1)}, bf16[16,160,320]{2,1,0:T(8,128)(2,1)}, u32[]{:S(2)}) %copy-start.1) | copy-done | bytes 1638424
  6.4 1.8 %prepare.1 = (bf16[64,5120]{1,0:T(8,128)(2,1)S(1)}, bf16[160,5120]{1,0:T(8,128)(2,1)S(1)}, f32[40,640]{1,0:T(8,128)S(1)}) custom-call(bf16[16,160,320]{2,1,0:T(8,128)(2,1)S(1)} %copy-done, bf16[40,5120]{1,0:T(8,128)(2,1)S(1)} %get-tuple-element.17.first_ref, bf16[64,5120]{1,0:T(8,128)(2,1)S(1)} %get-tuple-element.18.early_ref, ...), custom_call_target="tpu_custom_call" | custom-call | flops 262144000 | bytes 4915200 | tf_op jit(solution)/shard_map/prepare/pallas_call | solution.py:138
  8.2 0.1 collective-permute-start.2
  8.3 2.0 %collective-permute-start.3 = (f32[40,640]{1,0:T(8,128)S(1)}, f32[40,640]{1,0:T(8,128)S(1)}, u32[]{:S(2)}, u32[]{:S(2)}) collective-permute-start(f32[40,640]{1,0:T(8,128)S(1)} %get-tuple-element.20), channel_id=1, source_target_pairs={{0,4},{2,6},{4,0},{6,2},{8,12},{10,14},{12,8},{14,10},{16,20},{18,... | collective-permute-start | bytes 307208 | tf_op jit(solution)/shard_map/ppermute | solution.py:317
  10.3 0.1 collective-permute-start.4
  10.4 0.0 collective-permute-done.2
  10.4 3.7 %collective-permute-done.3 = f32[40,640]{1,0:T(8,128)S(1)} collective-permute-done((f32[40,640]{1,0:T(8,128)S(1)}, f32[40,640]{1,0:T(8,128)S(1)}, u32[]{:S(2)}, u32[]{:S(2)}) %collective-permute-start.3) | collective-permute-done | bytes 102432 | tf_op jit(solution)/shard_map/ppermute | solution.py:317
  14.1 1.6 %collective-permute-done.4 = f32[40,640]{1,0:T(8,128)S(1)} collective-permute-done((f32[40,640]{1,0:T(8,128)S(1)}, f32[40,640]{1,0:T(8,128)S(1)}, u32[]{:S(2)}, u32[]{:S(2)}) %collective-permute-start.4) | collective-permute-done | bytes 102432 | tf_op jit(solution)/shard_map/ppermute | solution.py:317
  15.7 0.0 collective-permute-done.1.refs_0_.refs_1_
  15.8 0.5 collective-permute-start.5
  16.2 1.7 %collective-permute-start = (bf16[64,5120]{1,0:T(8,128)(2,1)S(1)}, bf16[64,5120]{1,0:T(8,128)(2,1)S(1)}, u32[]{:S(2)}, u32[]{:S(2)}) collective-permute-start(bf16[64,5120]{1,0:T(8,128)(2,1)S(1)} %get-tuple-element.19), channel_id=1, source_target_pairs={{0,1},{1,0},{2,3},{3,2},{4,5},{5,4},{6,7},{7,6},{8,9},{9,8},{10,11... | collective-permute-start | bytes 1966088 | tf_op jit(solution)/shard_map/ppermute | solution.py:318
  18.0 3.6 %collective-permute-start.6 = (f32[40,640]{1,0:T(8,128)S(1)}, f32[40,640]{1,0:T(8,128)S(1)}, u32[]{:S(2)}, u32[]{:S(2)}) collective-permute-start(f32[40,640]{1,0:T(8,128)S(1)} %add_add_fusion.1), channel_id=1, source_target_pairs={{0,24},{2,26},{4,28},{6,30},{8,16},{10,18},{12,20},{14,22},{16,8},... | collective-permute-start | bytes 307208 | tf_op jit(solution)/shard_map/ppermute | solution.py:317
  21.6 0.0 collective-permute-done.5.other_ref
  21.6 0.8 %collective-permute-start.8 = (f32[40,640]{1,0:T(8,128)S(1)}, f32[40,640]{1,0:T(8,128)S(1)}, u32[]{:S(2)}, u32[]{:S(2)}) collective-permute-start(f32[40,640]{1,0:T(8,128)S(1)} %add_add_fusion.1), channel_id=1, source_target_pairs={{0,8},{2,10},{4,12},{6,14},{8,0},{10,2},{12,4},{14,6},{16,24},{18,... | collective-permute-start | bytes 307208 | tf_op jit(solution)/shard_map/ppermute | solution.py:317
  22.4 4.0 %near.1.near_ref = f32[16,160,320]{2,1,0:T(8,128)S(1)} custom-call(f32[16,320]{1,0:T(8,128)S(1)} %fusion.keep_ref, bf16[16,160,320]{2,1,0:T(8,128)(2,1)S(1)} %copy-done, bf16[16,160,320]{2,1,0:T(8,128)(2,1)S(1)} %copy-done.2, bf16[40,320]{1,0:T(8,128)(2,1)S(1)} %bitcast.4, bf16[160,320]{1,0:T(8,128)(2,1)S(1)} %bitcast.3, bf16[40,160]{1,0:T(8,128)(2,1)S(1)} %copy-done.4, ...), custom_call_target="tpu_custom_call" | custom-call | flops 629145600 | bytes 6553600 | tf_op jit(solution)/shard_map/near/pallas_call | solution.py:203
  26.4 2.6 %collective-permute-done.9.refs_1_.refs_2_ = bf16[64,5120]{1,0:T(8,128)(2,1)S(1)} collective-permute-done((bf16[64,5120]{1,0:T(8,128)(2,1)S(1)}, bf16[64,5120]{1,0:T(8,128)(2,1)S(1)}, u32[]{:S(2)}, u32[]{:S(2)}) %collective-permute-start.9) | collective-permute-done | bytes 655392 | tf_op jit(solution)/shard_map/ppermute | solution.py:318
  29.0 1.2 %gram.2 = f32[24,640]{1,0:T(8,128)S(1)} custom-call(bf16[40,5120]{1,0:T(8,128)(2,1)S(1)} %collective-permute-done.1.refs_0_.refs_1_, bf16[64,5120]{1,0:T(8,128)(2,1)S(1)} %collective-permute-done.9.refs_1_.refs_2_, bf16[160,5120]{1,0:T(8,128)(2,1)S(1)} %get-tuple-element.23.refs_2_.refs_1_), custom_call_target="tpu_custom_call" | custom-call | flops 157286400 | bytes 2621440 | tf_op jit(solution)/shard_map/gram/pallas_call | solution.py:162
  30.2 0.1 collective-permute-start.10
  30.3 0.0 collective-permute-done.6
  30.3 2.1 %collective-permute-start.11 = (f32[24,640]{1,0:T(8,128)S(1)}, f32[24,640]{1,0:T(8,128)S(1)}, u32[]{:S(2)}, u32[]{:S(2)}) collective-permute-start(f32[24,640]{1,0:T(8,128)S(1)} %gram.2), channel_id=1, source_target_pairs={{0,4},{2,6},{4,0},{6,2},{8,12},{10,14},{12,8},{14,10},{16,20},{18,... | collective-permute-start | bytes 184328 | tf_op jit(solution)/shard_map/ppermute | solution.py:317
  32.4 0.1 collective-permute-start.12
  32.6 2.4 %collective-permute-done.11 = f32[24,640]{1,0:T(8,128)S(1)} collective-permute-done((f32[24,640]{1,0:T(8,128)S(1)}, f32[24,640]{1,0:T(8,128)S(1)}, u32[]{:S(2)}, u32[]{:S(2)}) %collective-permute-start.11) | collective-permute-done | bytes 61472 | tf_op jit(solution)/shard_map/ppermute | solution.py:317
  35.0 1.4 %collective-permute-done.12 = f32[24,640]{1,0:T(8,128)S(1)} collective-permute-done((f32[24,640]{1,0:T(8,128)S(1)}, f32[24,640]{1,0:T(8,128)S(1)}, u32[]{:S(2)}, u32[]{:S(2)}) %collective-permute-start.12) | collective-permute-done | bytes 61472 | tf_op jit(solution)/shard_map/ppermute | solution.py:317
  36.4 3.7 %collective-permute-start.19 = (f32[24,640]{1,0:T(8,128)S(1)}, f32[24,640]{1,0:T(8,128)S(1)}, u32[]{:S(2)}, u32[]{:S(2)}) collective-permute-start(f32[24,640]{1,0:T(8,128)S(1)} %add_add_fusion.2), channel_id=1, source_target_pairs={{0,24},{2,26},{4,28},{6,30},{8,16},{10,18},{12,20},{14,22},{16,8},... | collective-permute-start | bytes 184328 | tf_op jit(solution)/shard_map/ppermute | solution.py:317
  40.1 0.0 collective-permute-start.20
  40.1 0.8 %collective-permute-start.21 = (f32[24,640]{1,0:T(8,128)S(1)}, f32[24,640]{1,0:T(8,128)S(1)}, u32[]{:S(2)}, u32[]{:S(2)}) collective-permute-start(f32[24,640]{1,0:T(8,128)S(1)} %add_add_fusion.2), channel_id=1, source_target_pairs={{0,8},{2,10},{4,12},{6,14},{8,0},{10,2},{12,4},{14,6},{16,24},{18,... | collective-permute-start | bytes 184328 | tf_op jit(solution)/shard_map/ppermute | solution.py:317
  40.9 1.5 %add_own.1.refs_3_.near_ref = f32[16,160,320]{2,1,0:T(8,128)S(1)} custom-call(f32[16,320]{1,0:T(8,128)S(1)} %fusion.keep_ref, bf16[16,160,320]{2,1,0:T(8,128)(2,1)S(1)} %copy-done, f32[16,160,320]{2,1,0:T(8,128)S(1)} %near.1.near_ref, f32[40,640]{1,0:T(8,128)S(1)} %add_add_fusion.den_ref), custom_call_target="tpu_custom_call", output_to_operand_aliasing={{}: (2, {})} | custom-call | flops 262144000 | bytes 8192000 | tf_op jit(solution)/shard_map/add_own/pallas_call | solution.py:227
  42.4 0.0 collective-permute-done.refs_0_
  42.4 0.7 %gram.3 = f32[16,640]{1,0:T(8,128)S(1)} custom-call(bf16[64,5120]{1,0:T(8,128)(2,1)S(1)} %collective-permute-done.refs_0_, bf16[160,5120]{1,0:T(8,128)(2,1)S(1)} %get-tuple-element.23.refs_2_.refs_1_), custom_call_target="tpu_custom_call" | custom-call | flops 104857600 | bytes 2293760 | tf_op jit(solution)/shard_map/gram/pallas_call | solution.py:162
  43.1 0.1 collective-permute-start.13
  43.2 1.2 %collective-permute-done.13 = f32[16,640]{1,0:T(8,128)S(1)} collective-permute-done((f32[16,640]{1,0:T(8,128)S(1)}, f32[16,640]{1,0:T(8,128)S(1)}, u32[]{:S(2)}, u32[]{:S(2)}) %collective-permute-start.13) | collective-permute-done | bytes 40992 | tf_op jit(solution)/shard_map/ppermute | solution.py:317
  44.4 1.5 %collective-permute-start.14 = (f32[16,640]{1,0:T(8,128)S(1)}, f32[16,640]{1,0:T(8,128)S(1)}, u32[]{:S(2)}, u32[]{:S(2)}) collective-permute-start(f32[16,640]{1,0:T(8,128)S(1)} %add.60), channel_id=1, source_target_pairs={{0,1},{1,0},{2,3},{3,2},{4,5},{5,4},{6,7},{7,6},{8,9},{9,8},{10,11... | collective-permute-start | bytes 122888 | tf_op jit(solution)/shard_map/ppermute | solution.py:318
  46.0 1.5 %collective-permute-start.15 = (f32[16,640]{1,0:T(8,128)S(1)}, f32[16,640]{1,0:T(8,128)S(1)}, u32[]{:S(2)}, u32[]{:S(2)}) collective-permute-start(f32[16,640]{1,0:T(8,128)S(1)} %add.60), channel_id=1, source_target_pairs={{0,5},{1,4},{2,7},{3,6},{4,1},{5,0},{6,3},{7,2},{8,13},{9,12},{10,... | collective-permute-start | bytes 122888 | tf_op jit(solution)/shard_map/ppermute | solution.py:318
  47.5 0.0 collective-permute-done.20
  47.5 0.0 collective-permute-done.21
  47.5 1.6 %collective-permute-start.22 = (bf16[24,640]{1,0:T(8,128)(2,1)S(1)}, bf16[24,640]{1,0:T(8,128)(2,1)S(1)}, u32[]{:S(2)}, u32[]{:S(2)}) collective-permute-start(bf16[24,640]{1,0:T(8,128)(2,1)S(1)} %multiply_convert_fusion), channel_id=1, source_target_pairs={{0,1},{1,0},{2,3},{3,2},{4,5},{5,4},{6,7},{7,6},{8,9},{9,8},{10,11... | collective-permute-start | bytes 92168 | tf_op jit(solution)/shard_map/ppermute | solution.py:318
  49.1 0.0 collective-permute-done.14
  49.1 1.8 %collective-permute-done.15 = f32[16,640]{1,0:T(8,128)S(1)} collective-permute-done((f32[16,640]{1,0:T(8,128)S(1)}, f32[16,640]{1,0:T(8,128)S(1)}, u32[]{:S(2)}, u32[]{:S(2)}) %collective-permute-start.15) | collective-permute-done | bytes 40992 | tf_op jit(solution)/shard_map/ppermute | solution.py:318
  50.9 3.6 %collective-permute-start.16 = (f32[16,640]{1,0:T(8,128)S(1)}, f32[16,640]{1,0:T(8,128)S(1)}, u32[]{:S(2)}, u32[]{:S(2)}) collective-permute-start(f32[16,640]{1,0:T(8,128)S(1)} %add.61), channel_id=1, source_target_pairs={{0,24},{2,26},{4,28},{6,30},{8,16},{10,18},{12,20},{14,22},{16,8},... | collective-permute-start | bytes 122888 | tf_op jit(solution)/shard_map/ppermute | solution.py:317
  54.5 0.0 collective-permute-start.17
  54.5 0.8 %collective-permute-start.18 = (f32[16,640]{1,0:T(8,128)S(1)}, f32[16,640]{1,0:T(8,128)S(1)}, u32[]{:S(2)}, u32[]{:S(2)}) collective-permute-start(f32[16,640]{1,0:T(8,128)S(1)} %add.61), channel_id=1, source_target_pairs={{0,8},{2,10},{4,12},{6,14},{8,0},{10,2},{12,4},{14,6},{16,24},{18,... | collective-permute-start | bytes 122888 | tf_op jit(solution)/shard_map/ppermute | solution.py:317
  55.3 1.7 %early.1 = (bf16[16,160,320]{2,1,0:T(8,128)(2,1)}, bf16[160,5120]{1,0:T(8,128)(2,1)S(1)}) custom-call(f32[16,320]{1,0:T(8,128)S(1)} %fusion.keep_ref, bf16[24,640]{1,0:T(8,128)(2,1)S(1)} %collective-permute-done.22.den_ref, bf16[64,5120]{1,0:T(8,128)(2,1)S(1)} %collective-permute-done.refs_0_, bf16[40,5120]{1,0:T(8,128)(2,1)S(1)} %collective-permute-done.1.refs_0_.refs_1_, ...), custom_call_target="tpu_custom_call" | custom-call | flops 262144000 | bytes 4915200 | tf_op jit(solution)/shard_map/early/pallas_call | solution.py:273
  56.9 2.4 %collective-permute-done.17 = f32[16,640]{1,0:T(8,128)S(1)} collective-permute-done((f32[16,640]{1,0:T(8,128)S(1)}, f32[16,640]{1,0:T(8,128)S(1)}, u32[]{:S(2)}, u32[]{:S(2)}) %collective-permute-start.17) | collective-permute-done | bytes 40992 | tf_op jit(solution)/shard_map/ppermute | solution.py:317
  59.4 1.3 %late.1 = bf16[16,160,320]{2,1,0:T(8,128)(2,1)} custom-call(f32[16,320]{1,0:T(8,128)S(1)} %fusion.keep_ref, bf16[16,640]{1,0:T(8,128)(2,1)S(1)} %multiply_convert_fusion.1.den_ref, bf16[160,5120]{1,0:T(8,128)(2,1)S(1)} %get-tuple-element.27.got_ref, f32[16,160,320]{2,1,0:T(8,128)S(1)} %add_own.1.refs_3_.near_ref, ...), custom_call_target="tpu_custom_call", output_to_operand_aliasing={{}: (4, {})} | custom-call | flops 104857600 | bytes 1966080 | tf_op jit(solution)/shard_map/late/pallas_call | solution.py:301
  (29 shorter events, 0.2 us)
Async XLA Ops:
  0.0 4.8 %copy-start = (bf16[16,160,320]{2,1,0:T(8,128)(2,1)S(1)}, bf16[16,160,320]{2,1,0:T(8,128)(2,1)}, u32[]{:S(2)}) copy-start(bf16[16,160,320]{2,1,0:T(8,128)(2,1)} %lam_ref.5) | copy-start | bytes 4915204
  0.0 4.7 %copy-start.6 = (s32[16]{0:T(128)S(1)}, s32[16]{0:T(128)}, u32[]{:S(2)}) copy-start(s32[16]{0:T(128)} %param.8) | copy-start | bytes 196
  1.6 14.1 %collective-permute-start.1 = (bf16[40,5120]{1,0:T(8,128)(2,1)S(1)}, bf16[40,5120]{1,0:T(8,128)(2,1)S(1)}, u32[]{:S(2)}, u32[]{:S(2)}) collective-permute-start(bf16[40,5120]{1,0:T(8,128)(2,1)S(1)} %get-tuple-element.17.first_ref), channel_id=1, source_target_pairs={{0,1},{1,0},{2,3},{3,2},{4,5},{5,4},{6,7},{7,6},{8,9},{9,8},{10,11... | collective-permute-start | bytes 1228808 | tf_op jit(solution)/shard_map/ppermute | solution.py:318
  4.6 24.3 %collective-permute-start.9 = (bf16[64,5120]{1,0:T(8,128)(2,1)S(1)}, bf16[64,5120]{1,0:T(8,128)(2,1)S(1)}, u32[]{:S(2)}, u32[]{:S(2)}) collective-permute-start(bf16[64,5120]{1,0:T(8,128)(2,1)S(1)} %get-tuple-element.18.early_ref), channel_id=1, source_target_pairs={{0,1},{1,0},{2,3},{3,2},{4,5},{5,4},{6,7},{7,6},{8,9},{9,8},{10,11... | collective-permute-start | bytes 1966088 | tf_op jit(solution)/shard_map/ppermute | solution.py:318
  4.8 1.5 %copy-start.1 = (bf16[16,160,320]{2,1,0:T(8,128)(2,1)S(1)}, bf16[16,160,320]{2,1,0:T(8,128)(2,1)}, u32[]{:S(2)}) copy-start(bf16[16,160,320]{2,1,0:T(8,128)(2,1)} %amp_ref.3) | copy-start | bytes 4915204
  6.3 16.0 %copy-start.2 = (bf16[16,160,320]{2,1,0:T(8,128)(2,1)S(1)}, bf16[16,160,320]{2,1,0:T(8,128)(2,1)}, u32[]{:S(2)}) copy-start(bf16[16,160,320]{2,1,0:T(8,128)(2,1)} %amp_ref.3) | copy-start | bytes 4915204
  6.3 16.0 %copy-start.3 = (bf16[320,160]{0,1:T(8,128)(2,1)S(1)}, bf16[320,160]{0,1:T(8,128)(2,1)}, u32[]{:S(2)}) copy-start(bf16[320,160]{0,1:T(8,128)(2,1)} %param.9) | copy-start | bytes 307204
  6.4 16.0 %copy-start.4 = (bf16[40,160]{1,0:T(8,128)(2,1)S(1)}, bf16[40,160]{1,0:T(8,128)(2,1)}, u32[]{:S(2)}) copy-start(bf16[40,160]{1,0:T(8,128)(2,1)} %doubles_ref.3) | copy-start | bytes 38404
  6.4 16.0 %copy-start.5 = (bf16[320,40]{0,1:T(8,128)(2,1)S(1)}, bf16[320,40]{0,1:T(8,128)(2,1)}, u32[]{:S(2)}) copy-start(bf16[320,40]{0,1:T(8,128)(2,1)} %param.10) | copy-start | bytes 76804
  8.2 2.2 %collective-permute-start.2 = (f32[40,640]{1,0:T(8,128)S(1)}, f32[40,640]{1,0:T(8,128)S(1)}, u32[]{:S(2)}, u32[]{:S(2)}) collective-permute-start(f32[40,640]{1,0:T(8,128)S(1)} %get-tuple-element.20), channel_id=1, source_target_pairs={{0,2},{2,0},{4,6},{6,4},{8,10},{10,8},{12,14},{14,12},{16,18},{18,... | collective-permute-start | bytes 307208 | tf_op jit(solution)/shard_map/ppermute | solution.py:317
  8.3 5.8 %collective-permute-start.3 = (f32[40,640]{1,0:T(8,128)S(1)}, f32[40,640]{1,0:T(8,128)S(1)}, u32[]{:S(2)}, u32[]{:S(2)}) collective-permute-start(f32[40,640]{1,0:T(8,128)S(1)} %get-tuple-element.20), channel_id=1, source_target_pairs={{0,4},{2,6},{4,0},{6,2},{8,12},{10,14},{12,8},{14,10},{16,20},{18,... | collective-permute-start | bytes 307208 | tf_op jit(solution)/shard_map/ppermute | solution.py:317
  10.3 5.4 %collective-permute-start.4 = (f32[40,640]{1,0:T(8,128)S(1)}, f32[40,640]{1,0:T(8,128)S(1)}, u32[]{:S(2)}, u32[]{:S(2)}) collective-permute-start(f32[40,640]{1,0:T(8,128)S(1)} %get-tuple-element.20), channel_id=1, source_target_pairs={{0,6},{2,4},{4,2},{6,0},{8,14},{10,12},{12,10},{14,8},{16,22},{18,... | collective-permute-start | bytes 307208 | tf_op jit(solution)/shard_map/ppermute | solution.py:317
  15.8 5.8 %collective-permute-start.5 = (bf16[8,5120]{1,0:T(8,128)(2,1)S(1)}, bf16[8,5120]{1,0:T(8,128)(2,1)S(1)}, u32[]{:S(2)}, u32[]{:S(2)}) collective-permute-start(bf16[8,5120]{1,0:T(8,128)(2,1)S(1)} %slice.3.mine_ref), channel_id=1, source_target_pairs={{0,2},{2,0},{4,6},{6,4},{8,10},{10,8},{12,14},{14,12},{16,18},{18,... | collective-permute-start | bytes 245768 | tf_op jit(solution)/shard_map/ppermute | solution.py:317
  16.2 26.1 %collective-permute-start = (bf16[64,5120]{1,0:T(8,128)(2,1)S(1)}, bf16[64,5120]{1,0:T(8,128)(2,1)S(1)}, u32[]{:S(2)}, u32[]{:S(2)}) collective-permute-start(bf16[64,5120]{1,0:T(8,128)(2,1)S(1)} %get-tuple-element.19), channel_id=1, source_target_pairs={{0,1},{1,0},{2,3},{3,2},{4,5},{5,4},{6,7},{7,6},{8,9},{9,8},{10,11... | collective-permute-start | bytes 1966088 | tf_op jit(solution)/shard_map/ppermute | solution.py:318
  18.0 12.3 %collective-permute-start.6 = (f32[40,640]{1,0:T(8,128)S(1)}, f32[40,640]{1,0:T(8,128)S(1)}, u32[]{:S(2)}, u32[]{:S(2)}) collective-permute-start(f32[40,640]{1,0:T(8,128)S(1)} %add_add_fusion.1), channel_id=1, source_target_pairs={{0,24},{2,26},{4,28},{6,30},{8,16},{10,18},{12,20},{14,22},{16,8},... | collective-permute-start | bytes 307208 | tf_op jit(solution)/shard_map/ppermute | solution.py:317
  21.6 10.9 %collective-permute-start.7 = (f32[40,640]{1,0:T(8,128)S(1)}, f32[40,640]{1,0:T(8,128)S(1)}, u32[]{:S(2)}, u32[]{:S(2)}) collective-permute-start(f32[40,640]{1,0:T(8,128)S(1)} %add_add_fusion.1), channel_id=1, source_target_pairs={{0,16},{2,18},{4,20},{6,22},{8,24},{10,26},{12,28},{14,30},{16,0},... | collective-permute-start | bytes 307208 | tf_op jit(solution)/shard_map/ppermute | solution.py:317
  21.6 11.0 %collective-permute-start.8 = (f32[40,640]{1,0:T(8,128)S(1)}, f32[40,640]{1,0:T(8,128)S(1)}, u32[]{:S(2)}, u32[]{:S(2)}) collective-permute-start(f32[40,640]{1,0:T(8,128)S(1)} %add_add_fusion.1), channel_id=1, source_target_pairs={{0,8},{2,10},{4,12},{6,14},{8,0},{10,2},{12,4},{14,6},{16,24},{18,... | collective-permute-start | bytes 307208 | tf_op jit(solution)/shard_map/ppermute | solution.py:317
  30.2 2.4 %collective-permute-start.10 = (f32[24,640]{1,0:T(8,128)S(1)}, f32[24,640]{1,0:T(8,128)S(1)}, u32[]{:S(2)}, u32[]{:S(2)}) collective-permute-start(f32[24,640]{1,0:T(8,128)S(1)} %gram.2), channel_id=1, source_target_pairs={{0,2},{2,0},{4,6},{6,4},{8,10},{10,8},{12,14},{14,12},{16,18},{18,... | collective-permute-start | bytes 184328 | tf_op jit(solution)/shard_map/ppermute | solution.py:317
  30.3 4.7 %collective-permute-start.11 = (f32[24,640]{1,0:T(8,128)S(1)}, f32[24,640]{1,0:T(8,128)S(1)}, u32[]{:S(2)}, u32[]{:S(2)}) collective-permute-start(f32[24,640]{1,0:T(8,128)S(1)} %gram.2), channel_id=1, source_target_pairs={{0,4},{2,6},{4,0},{6,2},{8,12},{10,14},{12,8},{14,10},{16,20},{18,... | collective-permute-start | bytes 184328 | tf_op jit(solution)/shard_map/ppermute | solution.py:317
  32.4 4.0 %collective-permute-start.12 = (f32[24,640]{1,0:T(8,128)S(1)}, f32[24,640]{1,0:T(8,128)S(1)}, u32[]{:S(2)}, u32[]{:S(2)}) collective-permute-start(f32[24,640]{1,0:T(8,128)S(1)} %gram.2), channel_id=1, source_target_pairs={{0,6},{2,4},{4,2},{6,0},{8,14},{10,12},{12,10},{14,8},{16,22},{18,... | collective-permute-start | bytes 184328 | tf_op jit(solution)/shard_map/ppermute | solution.py:317
  36.4 11.0 %collective-permute-start.19 = (f32[24,640]{1,0:T(8,128)S(1)}, f32[24,640]{1,0:T(8,128)S(1)}, u32[]{:S(2)}, u32[]{:S(2)}) collective-permute-start(f32[24,640]{1,0:T(8,128)S(1)} %add_add_fusion.2), channel_id=1, source_target_pairs={{0,24},{2,26},{4,28},{6,30},{8,16},{10,18},{12,20},{14,22},{16,8},... | collective-permute-start | bytes 184328 | tf_op jit(solution)/shard_map/ppermute | solution.py:317
  40.1 7.4 %collective-permute-start.20 = (f32[24,640]{1,0:T(8,128)S(1)}, f32[24,640]{1,0:T(8,128)S(1)}, u32[]{:S(2)}, u32[]{:S(2)}) collective-permute-start(f32[24,640]{1,0:T(8,128)S(1)} %add_add_fusion.2), channel_id=1, source_target_pairs={{0,16},{2,18},{4,20},{6,22},{8,24},{10,26},{12,28},{14,30},{16,0},... | collective-permute-start | bytes 184328 | tf_op jit(solution)/shard_map/ppermute | solution.py:317
  40.1 7.4 %collective-permute-start.21 = (f32[24,640]{1,0:T(8,128)S(1)}, f32[24,640]{1,0:T(8,128)S(1)}, u32[]{:S(2)}, u32[]{:S(2)}) collective-permute-start(f32[24,640]{1,0:T(8,128)S(1)} %add_add_fusion.2), channel_id=1, source_target_pairs={{0,8},{2,10},{4,12},{6,14},{8,0},{10,2},{12,4},{14,6},{16,24},{18,... | collective-permute-start | bytes 184328 | tf_op jit(solution)/shard_map/ppermute | solution.py:317
  43.1 1.3 %collective-permute-start.13 = (f32[16,640]{1,0:T(8,128)S(1)}, f32[16,640]{1,0:T(8,128)S(1)}, u32[]{:S(2)}, u32[]{:S(2)}) collective-permute-start(f32[16,640]{1,0:T(8,128)S(1)} %gram.3), channel_id=1, source_target_pairs={{0,2},{2,0},{4,6},{6,4},{8,10},{10,8},{12,14},{14,12},{16,18},{18,... | collective-permute-start | bytes 122888 | tf_op jit(solution)/shard_map/ppermute | solution.py:317
  44.4 4.6 %collective-permute-start.14 = (f32[16,640]{1,0:T(8,128)S(1)}, f32[16,640]{1,0:T(8,128)S(1)}, u32[]{:S(2)}, u32[]{:S(2)}) collective-permute-start(f32[16,640]{1,0:T(8,128)S(1)} %add.60), channel_id=1, source_target_pairs={{0,1},{1,0},{2,3},{3,2},{4,5},{5,4},{6,7},{7,6},{8,9},{9,8},{10,11... | collective-permute-start | bytes 122888 | tf_op jit(solution)/shard_map/ppermute | solution.py:318
  46.0 4.9 %collective-permute-start.15 = (f32[16,640]{1,0:T(8,128)S(1)}, f32[16,640]{1,0:T(8,128)S(1)}, u32[]{:S(2)}, u32[]{:S(2)}) collective-permute-start(f32[16,640]{1,0:T(8,128)S(1)} %add.60), channel_id=1, source_target_pairs={{0,5},{1,4},{2,7},{3,6},{4,1},{5,0},{6,3},{7,2},{8,13},{9,12},{10,... | collective-permute-start | bytes 122888 | tf_op jit(solution)/shard_map/ppermute | solution.py:318
  47.5 7.8 %collective-permute-start.22 = (bf16[24,640]{1,0:T(8,128)(2,1)S(1)}, bf16[24,640]{1,0:T(8,128)(2,1)S(1)}, u32[]{:S(2)}, u32[]{:S(2)}) collective-permute-start(bf16[24,640]{1,0:T(8,128)(2,1)S(1)} %multiply_convert_fusion), channel_id=1, source_target_pairs={{0,1},{1,0},{2,3},{3,2},{4,5},{5,4},{6,7},{7,6},{8,9},{9,8},{10,11... | collective-permute-start | bytes 92168 | tf_op jit(solution)/shard_map/ppermute | solution.py:318
  50.9 6.1 %collective-permute-start.16 = (f32[16,640]{1,0:T(8,128)S(1)}, f32[16,640]{1,0:T(8,128)S(1)}, u32[]{:S(2)}, u32[]{:S(2)}) collective-permute-start(f32[16,640]{1,0:T(8,128)S(1)} %add.61), channel_id=1, source_target_pairs={{0,24},{2,26},{4,28},{6,30},{8,16},{10,18},{12,20},{14,22},{16,8},... | collective-permute-start | bytes 122888 | tf_op jit(solution)/shard_map/ppermute | solution.py:317
  54.5 4.9 %collective-permute-start.17 = (f32[16,640]{1,0:T(8,128)S(1)}, f32[16,640]{1,0:T(8,128)S(1)}, u32[]{:S(2)}, u32[]{:S(2)}) collective-permute-start(f32[16,640]{1,0:T(8,128)S(1)} %add.61), channel_id=1, source_target_pairs={{0,16},{2,18},{4,20},{6,22},{8,24},{10,26},{12,28},{14,30},{16,0},... | collective-permute-start | bytes 122888 | tf_op jit(solution)/shard_map/ppermute | solution.py:317
  54.5 4.9 %collective-permute-start.18 = (f32[16,640]{1,0:T(8,128)S(1)}, f32[16,640]{1,0:T(8,128)S(1)}, u32[]{:S(2)}, u32[]{:S(2)}) collective-permute-start(f32[16,640]{1,0:T(8,128)S(1)} %add.61), channel_id=1, source_target_pairs={{0,8},{2,10},{4,12},{6,14},{8,0},{10,2},{12,4},{14,6},{16,24},{18,... | collective-permute-start | bytes 122888 | tf_op jit(solution)/shard_map/ppermute | solution.py:317

commit v5 on v4

--- a/solution.py
+++ b/solution.py
@@ -12,7 +12,7 @@
 VMEM = functools.partial(pl.BlockSpec, memory_space=pltpu.VMEM)
 SMEM = functools.partial(pl.BlockSpec, memory_space=pltpu.SMEM)
 LATE = 64
-FIRST = 32
+FIRST = 48
 PARTS = 4
 EXTRA = 8
 
@@ -61,7 +61,7 @@
     return jnp.concatenate([x[:, i : i + width] for i in range(0, x.shape[1], width)], axis=0)
 
 
-def pack_kernel(start, x_ref, ladder_ref, doubles_ref, o_ref, p_ref, x_buf, l_buf, d_buf, sems):
+def pack_kernel(start, x_ref, ladder_ref, doubles_ref, o_ref, x_buf, l_buf, d_buf, sems):
     triples, rows, _ = x_buf.shape
     half = ladder_ref.shape[0] // 2
     n = triples // PARTS
@@ -73,8 +73,7 @@
         c.start()
     for c in copies:
         c.wait()
-    pack_into(o_ref.at[:FIRST], x_buf.at[:, :FIRST])
-    pack_into(p_ref, x_buf.at[:, FIRST:])
+    pack_into(o_ref.at[:FIRST], x_buf)
     parts = [spread(l_buf[...].astype(F32)), spread(d_buf[...].astype(F32))]
     used = sum(p.shape[1] for p in parts)
     parts.append(jnp.zeros((EXTRA, o_ref.shape[1] - used), F32))
@@ -83,13 +82,12 @@
 
 def pack(x, ladder, doubles, start):
     triples, rows, width = x.shape
-    rows = rows - start
-    shapes = [(FIRST + EXTRA, triples * width), (rows - FIRST, triples * width)]
+    rows = FIRST
     return pl.pallas_call(
         functools.partial(pack_kernel, start),
         in_specs=[pl.BlockSpec(memory_space=pltpu.HBM)] * 3,
-        out_specs=[VMEM()] * 2,
-        out_shape=[jax.ShapeDtypeStruct(s, BF16) for s in shapes],
+        out_specs=VMEM(),
+        out_shape=jax.ShapeDtypeStruct((FIRST + EXTRA, triples * width), BF16),
         scratch_shapes=[
             pltpu.VMEM((triples, rows, width), BF16),
             pltpu.VMEM((ladder.shape[0] // 2, width), BF16),
@@ -125,30 +123,33 @@
     return lax.dot_general(x, y, NT, preferred_element_type=F32)
 
 
-def prepare_kernel(lam_ref, first_ref, early_ref, amp_ref, keep_ref, late_ref, all_ref, o_ref):
-    pack_into(late_ref, lam_ref)
+def prepare_kernel(lam_ref, first_ref, amp_ref, keep_ref, early_ref, late_ref, all_ref, o_ref):
+    pack_into(early_ref, lam_ref.at[:, LATE + FIRST :])
+    pack_into(late_ref, lam_ref.at[:, :LATE])
     pack_into(all_ref, amp_ref, keep_ref)
     y = all_ref[...]
     o_ref[...] = fold(jnp.concatenate([product_of(x, y) for x in (late_ref[...], first_ref[:FIRST], early_ref[...])]))
 
 
-def prepare(lam, first, early, amp, keep):
+def prepare(lam, first, amp, keep):
     triples, rows, width = lam.shape
     size = triples * width
+    shapes = [
+        jax.ShapeDtypeStruct((rows - LATE - FIRST, size), BF16),
+        jax.ShapeDtypeStruct((LATE, size), BF16),
+        jax.ShapeDtypeStruct((rows, size), BF16),
+        jax.ShapeDtypeStruct((rows // 4, 4 * rows), F32),
+    ]
     return pl.pallas_call(
         prepare_kernel,
         grid=(1,),
-        in_specs=[pl.BlockSpec((triples, LATE, width), lambda i: (0, 0, 0)), whole(first), whole(early), whole(amp), whole(keep)],
-        out_specs=[pl.BlockSpec(s, lambda i: (0, 0)) for s in ((LATE, size), (rows, size), (rows // 4, 4 * rows))],
-        out_shape=[
-            jax.ShapeDtypeStruct((LATE, size), BF16),
-            jax.ShapeDtypeStruct((rows, size), BF16),
-            jax.ShapeDtypeStruct((rows // 4, 4 * rows), F32),
-        ],
-        compiler_params=params(18),
+        in_specs=[whole(lam), whole(first), whole(amp), whole(keep)],
+        out_specs=[whole(s) for s in shapes],
+        out_shape=shapes,
+        compiler_params=params(20),
         cost_estimate=cost(2 * rows * rows * size, 6 * rows * size),
         name="prepare",
-    )(lam, first, early, amp, keep)
+    )(lam, first, amp, keep)
 
 
 def gram_kernel(*refs):
@@ -324,7 +325,7 @@
     while bit < n:
         if 2 * bit < n:
             far, mid, close = permute(x, 3 * bit), permute(x, 2 * bit), permute(x, bit)
-            x = (far + mid) + (close + x)
+            x = (mid + far) + (close + x)
             bit *= 4
         else:
             x = x + permute(x, bit)
@@ -337,10 +338,9 @@
     return (x + close) + (mid + far)
 
 
-def crossed_sum(x):
-    x = x + permute(x, 1)
+def crossed(x):
     far, close = permute(x, 2, 1), permute(x, 0, 1)
-    return close + far
+    return far + close
 
 
 def on_device(lam, amp, ext, ladder, cycle, doubles):
@@ -351,11 +351,11 @@
     early_rows = rows - LATE
 
     ladder = ladder.T
-    first_own, early_own = pack(lam, ladder, doubles, LATE)
-    first_got, early_got = permute(first_own, 0, 1), permute(early_own, 0, 1)
+    first_own = pack(lam, ladder, doubles, LATE)
+    first_got = permute(first_own, 0, 1)
     keep = (lax.broadcasted_iota(jnp.int32, (triples, width), 1) < ext[:, None]).astype(F32)
-    late_own, amp_all, own_den = prepare(lam, first_own, early_own, amp, keep)
-    late_got = permute(late_own, 0, 1)
+    early_own, late_own, amp_all, own_den = prepare(lam, first_own, amp, keep)
+    early_got, late_got = permute(early_own, 0, 1), permute(late_own, 0, 1)
 
     own_den = near_sum(own_den)
     first_got = after(first_got, own_den)
@@ -371,9 +371,10 @@
     early = far_sum(early)
     late_got = after(late_got, near)
     early = permute((early / norm).astype(BF16), 0, 1)
-    late = crossed_sum(gram((late_got,), amp_all))
+    late = gram((late_got,), amp_all)
+    late = far_sum(late + permute(late, 1))
     early = after(early, late)
-    late = (far_sum(late) / norm).astype(BF16)
+    late = (crossed(late) / norm).astype(BF16)
 
     got = (late_got, first_got, early_got)
     out, all_got = early_output(keep, early, got, near, LATE, scale)

time: 60.8 us -> 60.7 us (level)
  starting transfers between devices: 27.7 us -> 25.7 us
  waiting for transfers between devices: 17.2 us -> 19.2 us
    ppermute x17, starting transfers between devices: 18.3 us -> 15.7 us  [permute(): return lax.ppermute(x, 'occ', [(i, i ^ flip) for i in range(n)])]
    ppermute x17, waiting for transfers between devices: 12.8 us -> 14.8 us  [permute(): return lax.ppermute(x, 'occ', [(i, i ^ flip) for i in range(n)])]
    ppermute x6, starting transfers between devices: 9.41 us -> 10.1 us  [permute(): lax.ppermute(x, ('occ', 'vir'), [(i * v + j, (i ^ flip) * v + (j ^ swap))...]
  transfers between devices with their start and end apart: 23 -> 23, of which waited for: 8 -> 12; matrix products, arithmetic and copies ran while one was open for 0% -> 0% of each run, Pallas kernels for 18% -> 18%
where the time goes in v5:
time: 60.7 us; the launch traced here: 60.5 us
  starting transfers between devices  25.7 us (42%)
  waiting for transfers between devices  19.2 us (32%)
  Pallas kernels  13.7 us (23%)
  local copies, waits for them, and re-layouts  1.57 us (3%)
    ppermute x17, starting transfers between devices, permute(): return lax.ppermute(x, 'occ', [(i, i ^ flip) for i in range(n)])  15.7 us
    ppermute x17, waiting for transfers between devices, permute(): return lax.ppermute(x, 'occ', [(i, i ^ flip) for i in range(n)])  14.8 us
    ppermute x6, starting transfers between devices, permute(): lax.ppermute(x, ('occ', 'vir'), [(i * v + j, (i ^ flip) * v + (j ^ swap))...  10.1 us
    ppermute x6, waiting for transfers between devices, permute(): lax.ppermute(x, ('occ', 'vir'), [(i * v + j, (i ^ flip) * v + (j ^ swap))...  4.44 us
    pallas_call x1, Pallas kernels, near_of(): pl.pallas_call(functools.partial(near_kernel, step), grid=(triples // ste...  4.04 us
    pallas_call x2, Pallas kernels, gram(): pl.pallas_call(gram_kernel, in_specs=[VMEM()] * (len(xs) + 1), out_specs=...  1.89 us
    pallas_call x1, Pallas kernels, prepare(): pl.pallas_call(prepare_kernel, grid=(1,), in_specs=[whole(lam), whole(fir...  1.85 us
    pallas_call x1, Pallas kernels, early_output(): pl.pallas_call(functools.partial(early_kernel, scale), grid=(1,), in_spec...  1.66 us
  transfers between devices with their start and end apart: 23, of which 12 were waited for; matrix products, arithmetic and copies ran while one was open for 0% of the time, Pallas kernels for 18%

profile of v5, /device:TPU:0, one launch (start us, length us, event | category | flops | bytes accessed | tf_op | source)
XLA Modules:
  0.0 60.5 jit_solution(5490680016595514327)
XLA Ops:
  0.0 1.5 %pack.1.first_ref = bf16[56,5120]{1,0:T(8,128)(2,1)S(1)} custom-call(bf16[16,160,320]{2,1,0:T(8,128)(2,1)} %lam_ref.5, bf16[160,320]{1,0:T(8,128)(2,1)} %bitcast.2, bf16[40,160]{1,0:T(8,128)(2,1)} %doubles_ref.3), custom_call_target="tpu_custom_call" | custom-call | flops 491520 | bytes 983040 | tf_op jit(solution)/shard_map/pack/pallas_call | solution.py:86
  1.5 3.0 %collective-permute-start.1 = (bf16[56,5120]{1,0:T(8,128)(2,1)S(1)}, bf16[56,5120]{1,0:T(8,128)(2,1)S(1)}, u32[]{:S(2)}, u32[]{:S(2)}) collective-permute-start(bf16[56,5120]{1,0:T(8,128)(2,1)S(1)} %pack.1.first_ref), channel_id=1, source_target_pairs={{0,1},{1,0},{2,3},{3,2},{4,5},{5,4},{6,7},{7,6},{8,9},{9,8},{10,11... | collective-permute-start | bytes 1720328 | tf_op jit(solution)/shard_map/ppermute | solution.py:319
  4.5 0.1 fusion.keep_ref
  4.6 1.5 %copy-done.1 = bf16[16,160,320]{2,1,0:T(8,128)(2,1)S(1)} copy-done((bf16[16,160,320]{2,1,0:T(8,128)(2,1)S(1)}, bf16[16,160,320]{2,1,0:T(8,128)(2,1)}, u32[]{:S(2)}) %copy-start.1) | copy-done | bytes 1638424
  6.1 1.9 %prepare.1 = (bf16[48,5120]{1,0:T(8,128)(2,1)S(1)}, bf16[64,5120]{1,0:T(8,128)(2,1)S(1)}, bf16[160,5120]{1,0:T(8,128)(2,1)S(1)}, f32[40,640]{1,0:T(8,128)S(1)}) custom-call(bf16[16,160,320]{2,1,0:T(8,128)(2,1)S(1)} %copy-done, bf16[56,5120]{1,0:T(8,128)(2,1)S(1)} %pack.1.first_ref, bf16[16,160,320]{2,1,0:T(8,128)(2,1)S(1)} %copy-done.1, ...), custom_call_target="tpu_custom_call" | custom-call | flops 262144000 | bytes 4915200 | tf_op jit(solution)/shard_map/prepare/pallas_call | solution.py:143
  8.0 0.1 collective-permute-start.2
  8.1 1.6 %collective-permute-start.3 = (f32[40,640]{1,0:T(8,128)S(1)}, f32[40,640]{1,0:T(8,128)S(1)}, u32[]{:S(2)}, u32[]{:S(2)}) collective-permute-start(f32[40,640]{1,0:T(8,128)S(1)} %get-tuple-element.17), channel_id=1, source_target_pairs={{0,4},{2,6},{4,0},{6,2},{8,12},{10,14},{12,8},{14,10},{16,20},{18,... | collective-permute-start | bytes 307208 | tf_op jit(solution)/shard_map/ppermute | solution.py:318
  9.6 0.3 collective-permute-start.4
  9.9 0.3 collective-permute-start.9
  10.3 3.6 %collective-permute-done.3 = f32[40,640]{1,0:T(8,128)S(1)} collective-permute-done((f32[40,640]{1,0:T(8,128)S(1)}, f32[40,640]{1,0:T(8,128)S(1)}, u32[]{:S(2)}, u32[]{:S(2)}) %collective-permute-start.3) | collective-permute-done | bytes 102432 | tf_op jit(solution)/shard_map/ppermute | solution.py:318
  13.8 1.3 %collective-permute-done.4 = f32[40,640]{1,0:T(8,128)S(1)} collective-permute-done((f32[40,640]{1,0:T(8,128)S(1)}, f32[40,640]{1,0:T(8,128)S(1)}, u32[]{:S(2)}, u32[]{:S(2)}) %collective-permute-start.4) | collective-permute-done | bytes 102432 | tf_op jit(solution)/shard_map/ppermute | solution.py:318
  15.1 3.2 %collective-permute-done.1.refs_0_.refs_1_ = bf16[56,5120]{1,0:T(8,128)(2,1)S(1)} collective-permute-done((bf16[56,5120]{1,0:T(8,128)(2,1)S(1)}, bf16[56,5120]{1,0:T(8,128)(2,1)S(1)}, u32[]{:S(2)}, u32[]{:S(2)}) %collective-permute-start.1) | collective-permute-done | bytes 573472 | tf_op jit(solution)/shard_map/ppermute | solution.py:319
  18.3 0.0 collective-permute-start.5
  18.3 2.1 %collective-permute-start = (bf16[64,5120]{1,0:T(8,128)(2,1)S(1)}, bf16[64,5120]{1,0:T(8,128)(2,1)S(1)}, u32[]{:S(2)}, u32[]{:S(2)}) collective-permute-start(bf16[64,5120]{1,0:T(8,128)(2,1)S(1)} %get-tuple-element.16), channel_id=1, source_target_pairs={{0,1},{1,0},{2,3},{3,2},{4,5},{5,4},{6,7},{7,6},{8,9},{9,8},{10,11... | collective-permute-start | bytes 1966088 | tf_op jit(solution)/shard_map/ppermute | solution.py:319
  20.4 2.6 %collective-permute-start.6 = (f32[40,640]{1,0:T(8,128)S(1)}, f32[40,640]{1,0:T(8,128)S(1)}, u32[]{:S(2)}, u32[]{:S(2)}) collective-permute-start(f32[40,640]{1,0:T(8,128)S(1)} %add_add_fusion.1), channel_id=1, source_target_pairs={{0,16},{2,18},{4,20},{6,22},{8,24},{10,26},{12,28},{14,30},{16,0},... | collective-permute-start | bytes 307208 | tf_op jit(solution)/shard_map/ppermute | solution.py:318
  23.0 1.3 %collective-permute-start.7 = (f32[40,640]{1,0:T(8,128)S(1)}, f32[40,640]{1,0:T(8,128)S(1)}, u32[]{:S(2)}, u32[]{:S(2)}) collective-permute-start(f32[40,640]{1,0:T(8,128)S(1)} %add_add_fusion.1), channel_id=1, source_target_pairs={{0,24},{2,26},{4,28},{6,30},{8,16},{10,18},{12,20},{14,22},{16,8},... | collective-permute-start | bytes 307208 | tf_op jit(solution)/shard_map/ppermute | solution.py:318
  24.4 0.2 collective-permute-start.8
  24.6 4.0 %near.1.near_ref = f32[16,160,320]{2,1,0:T(8,128)S(1)} custom-call(f32[16,320]{1,0:T(8,128)S(1)} %fusion.keep_ref, bf16[16,160,320]{2,1,0:T(8,128)(2,1)S(1)} %copy-done, bf16[16,160,320]{2,1,0:T(8,128)(2,1)S(1)} %copy-done.2, bf16[40,320]{1,0:T(8,128)(2,1)S(1)} %bitcast.4, bf16[160,320]{1,0:T(8,128)(2,1)S(1)} %bitcast.3, bf16[40,160]{1,0:T(8,128)(2,1)S(1)} %copy-done.4, ...), custom_call_target="tpu_custom_call" | custom-call | flops 629145600 | bytes 6553600 | tf_op jit(solution)/shard_map/near/pallas_call | solution.py:204
  28.7 0.2 collective-permute-done.9.refs_1_.refs_2_
  28.8 1.2 %gram.2 = f32[24,640]{1,0:T(8,128)S(1)} custom-call(bf16[56,5120]{1,0:T(8,128)(2,1)S(1)} %collective-permute-done.1.refs_0_.refs_1_, bf16[48,5120]{1,0:T(8,128)(2,1)S(1)} %collective-permute-done.9.refs_1_.refs_2_, bf16[160,5120]{1,0:T(8,128)(2,1)S(1)} %get-tuple-element.21.refs_2_.refs_1_), custom_call_target="tpu_custom_call" | custom-call | flops 157286400 | bytes 2621440 | tf_op jit(solution)/shard_map/gram/pallas_call | solution.py:163
  30.0 0.1 collective-permute-start.10
  30.1 1.4 %collective-permute-done.6 = f32[40,640]{1,0:T(8,128)S(1)} collective-permute-done((f32[40,640]{1,0:T(8,128)S(1)}, f32[40,640]{1,0:T(8,128)S(1)}, u32[]{:S(2)}, u32[]{:S(2)}) %collective-permute-start.6) | collective-permute-done | bytes 102432 | tf_op jit(solution)/shard_map/ppermute | solution.py:318
  31.5 1.5 %collective-permute-start.11 = (f32[24,640]{1,0:T(8,128)S(1)}, f32[24,640]{1,0:T(8,128)S(1)}, u32[]{:S(2)}, u32[]{:S(2)}) collective-permute-start(f32[24,640]{1,0:T(8,128)S(1)} %gram.2), channel_id=1, source_target_pairs={{0,4},{2,6},{4,0},{6,2},{8,12},{10,14},{12,8},{14,10},{16,20},{18,... | collective-permute-start | bytes 184328 | tf_op jit(solution)/shard_map/ppermute | solution.py:318
  33.1 2.6 %collective-permute-done.11 = f32[24,640]{1,0:T(8,128)S(1)} collective-permute-done((f32[24,640]{1,0:T(8,128)S(1)}, f32[24,640]{1,0:T(8,128)S(1)}, u32[]{:S(2)}, u32[]{:S(2)}) %collective-permute-start.11) | collective-permute-done | bytes 61472 | tf_op jit(solution)/shard_map/ppermute | solution.py:318
  35.7 1.3 %collective-permute-done.12 = f32[24,640]{1,0:T(8,128)S(1)} collective-permute-done((f32[24,640]{1,0:T(8,128)S(1)}, f32[24,640]{1,0:T(8,128)S(1)}, u32[]{:S(2)}, u32[]{:S(2)}) %collective-permute-start.12) | collective-permute-done | bytes 61472 | tf_op jit(solution)/shard_map/ppermute | solution.py:318
  37.0 2.6 %collective-permute-start.19 = (f32[24,640]{1,0:T(8,128)S(1)}, f32[24,640]{1,0:T(8,128)S(1)}, u32[]{:S(2)}, u32[]{:S(2)}) collective-permute-start(f32[24,640]{1,0:T(8,128)S(1)} %add_add_fusion.2), channel_id=1, source_target_pairs={{0,16},{2,18},{4,20},{6,22},{8,24},{10,26},{12,28},{14,30},{16,0},... | collective-permute-start | bytes 184328 | tf_op jit(solution)/shard_map/ppermute | solution.py:318
  39.7 0.6 collective-permute-start.20
  40.2 0.4 collective-permute-start.21
  40.6 1.5 %add_own.1.refs_3_.near_ref = f32[16,160,320]{2,1,0:T(8,128)S(1)} custom-call(f32[16,320]{1,0:T(8,128)S(1)} %fusion.keep_ref, bf16[16,160,320]{2,1,0:T(8,128)(2,1)S(1)} %copy-done, f32[16,160,320]{2,1,0:T(8,128)S(1)} %near.1.near_ref, f32[40,640]{1,0:T(8,128)S(1)} %add_add_fusion.den_ref), custom_call_target="tpu_custom_call", output_to_operand_aliasing={{}: (2, {})} | custom-call | flops 262144000 | bytes 8192000 | tf_op jit(solution)/shard_map/add_own/pallas_call | solution.py:228
  42.1 0.7 %gram.3 = f32[16,640]{1,0:T(8,128)S(1)} custom-call(bf16[64,5120]{1,0:T(8,128)(2,1)S(1)} %collective-permute-done.refs_0_, bf16[160,5120]{1,0:T(8,128)(2,1)S(1)} %get-tuple-element.21.refs_2_.refs_1_), custom_call_target="tpu_custom_call" | custom-call | flops 104857600 | bytes 2293760 | tf_op jit(solution)/shard_map/gram/pallas_call | solution.py:163
  42.8 0.1 collective-permute-start.13
  42.9 1.2 %collective-permute-done.13 = f32[16,640]{1,0:T(8,128)S(1)} collective-permute-done((f32[16,640]{1,0:T(8,128)S(1)}, f32[16,640]{1,0:T(8,128)S(1)}, u32[]{:S(2)}, u32[]{:S(2)}) %collective-permute-start.13) | collective-permute-done | bytes 40992 | tf_op jit(solution)/shard_map/ppermute | solution.py:318
  44.1 3.4 %collective-permute-start.14 = (f32[16,640]{1,0:T(8,128)S(1)}, f32[16,640]{1,0:T(8,128)S(1)}, u32[]{:S(2)}, u32[]{:S(2)}) collective-permute-start(f32[16,640]{1,0:T(8,128)S(1)} %add.60), channel_id=1, source_target_pairs={{0,16},{2,18},{4,20},{6,22},{8,24},{10,26},{12,28},{14,30},{16,0},... | collective-permute-start | bytes 122888 | tf_op jit(solution)/shard_map/ppermute | solution.py:318
  47.6 0.7 %collective-permute-start.15 = (f32[16,640]{1,0:T(8,128)S(1)}, f32[16,640]{1,0:T(8,128)S(1)}, u32[]{:S(2)}, u32[]{:S(2)}) collective-permute-start(f32[16,640]{1,0:T(8,128)S(1)} %add.60), channel_id=1, source_target_pairs={{0,24},{2,26},{4,28},{6,30},{8,16},{10,18},{12,20},{14,22},{16,8},... | collective-permute-start | bytes 122888 | tf_op jit(solution)/shard_map/ppermute | solution.py:318
  48.2 0.0 collective-permute-done.19
  48.3 0.2 collective-permute-start.16
  48.5 0.0 collective-permute-done.20
  48.5 0.0 collective-permute-done.21
  48.5 1.6 %collective-permute-start.22 = (bf16[24,640]{1,0:T(8,128)(2,1)S(1)}, bf16[24,640]{1,0:T(8,128)(2,1)S(1)}, u32[]{:S(2)}, u32[]{:S(2)}) collective-permute-start(bf16[24,640]{1,0:T(8,128)(2,1)S(1)} %multiply_convert_fusion), channel_id=1, source_target_pairs={{0,1},{1,0},{2,3},{3,2},{4,5},{5,4},{6,7},{7,6},{8,9},{9,8},{10,11... | collective-permute-start | bytes 92168 | tf_op jit(solution)/shard_map/ppermute | solution.py:319
  50.1 0.3 collective-permute-done.14
  50.3 3.0 %collective-permute-done.15 = f32[16,640]{1,0:T(8,128)S(1)} collective-permute-done((f32[16,640]{1,0:T(8,128)S(1)}, f32[16,640]{1,0:T(8,128)S(1)}, u32[]{:S(2)}, u32[]{:S(2)}) %collective-permute-start.15) | collective-permute-done | bytes 40992 | tf_op jit(solution)/shard_map/ppermute | solution.py:318
  53.4 0.0 collective-permute-done.16
  53.4 1.8 %collective-permute-start.17 = (f32[16,640]{1,0:T(8,128)S(1)}, f32[16,640]{1,0:T(8,128)S(1)}, u32[]{:S(2)}, u32[]{:S(2)}) collective-permute-start(f32[16,640]{1,0:T(8,128)S(1)} %add_add_fusion.3), channel_id=1, source_target_pairs={{0,5},{1,4},{2,7},{3,6},{4,1},{5,0},{6,3},{7,2},{8,13},{9,12},{10,... | collective-permute-start | bytes 122888 | tf_op jit(solution)/shard_map/ppermute | solution.py:319
  55.2 1.2 %collective-permute-start.18 = (f32[16,640]{1,0:T(8,128)S(1)}, f32[16,640]{1,0:T(8,128)S(1)}, u32[]{:S(2)}, u32[]{:S(2)}) collective-permute-start(f32[16,640]{1,0:T(8,128)S(1)} %add_add_fusion.3), channel_id=1, source_target_pairs={{0,1},{1,0},{2,3},{3,2},{4,5},{5,4},{6,7},{7,6},{8,9},{9,8},{10,11... | collective-permute-start | bytes 122888 | tf_op jit(solution)/shard_map/ppermute | solution.py:319
  56.4 1.7 %early.1 = (bf16[16,160,320]{2,1,0:T(8,128)(2,1)}, bf16[160,5120]{1,0:T(8,128)(2,1)S(1)}) custom-call(f32[16,320]{1,0:T(8,128)S(1)} %fusion.keep_ref, bf16[24,640]{1,0:T(8,128)(2,1)S(1)} %collective-permute-done.22.den_ref, bf16[64,5120]{1,0:T(8,128)(2,1)S(1)} %collective-permute-done.refs_0_, bf16[56,5120]{1,0:T(8,128)(2,1)S(1)} %collective-permute-done.1.refs_0_.refs_1_, ...), custom_call_target="tpu_custom_call" | custom-call | flops 262144000 | bytes 4915200 | tf_op jit(solution)/shard_map/early/pallas_call | solution.py:274
  58.1 0.3 collective-permute-done.17
  58.4 0.9 %collective-permute-done.18 = f32[16,640]{1,0:T(8,128)S(1)} collective-permute-done((f32[16,640]{1,0:T(8,128)S(1)}, f32[16,640]{1,0:T(8,128)S(1)}, u32[]{:S(2)}, u32[]{:S(2)}) %collective-permute-start.18) | collective-permute-done | bytes 40992 | tf_op jit(solution)/shard_map/ppermute | solution.py:319
  59.2 1.3 %late.1 = bf16[16,160,320]{2,1,0:T(8,128)(2,1)} custom-call(f32[16,320]{1,0:T(8,128)S(1)} %fusion.keep_ref, bf16[16,640]{1,0:T(8,128)(2,1)S(1)} %multiply_convert_fusion.1.den_ref, bf16[160,5120]{1,0:T(8,128)(2,1)S(1)} %get-tuple-element.25.got_ref, f32[16,160,320]{2,1,0:T(8,128)S(1)} %add_own.1.refs_3_.near_ref, ...), custom_call_target="tpu_custom_call", output_to_operand_aliasing={{}: (4, {})} | custom-call | flops 104857600 | bytes 1966080 | tf_op jit(solution)/shard_map/late/pallas_call | solution.py:302
  (29 shorter events, 0.2 us)
Async XLA Ops:
  0.0 4.6 %copy-start = (bf16[16,160,320]{2,1,0:T(8,128)(2,1)S(1)}, bf16[16,160,320]{2,1,0:T(8,128)(2,1)}, u32[]{:S(2)}) copy-start(bf16[16,160,320]{2,1,0:T(8,128)(2,1)} %lam_ref.5) | copy-start | bytes 4915204
  0.0 4.5 %copy-start.6 = (s32[16]{0:T(128)S(1)}, s32[16]{0:T(128)}, u32[]{:S(2)}) copy-start(s32[16]{0:T(128)} %param.8) | copy-start | bytes 196
  1.5 16.8 %collective-permute-start.1 = (bf16[56,5120]{1,0:T(8,128)(2,1)S(1)}, bf16[56,5120]{1,0:T(8,128)(2,1)S(1)}, u32[]{:S(2)}, u32[]{:S(2)}) collective-permute-start(bf16[56,5120]{1,0:T(8,128)(2,1)S(1)} %pack.1.first_ref), channel_id=1, source_target_pairs={{0,1},{1,0},{2,3},{3,2},{4,5},{5,4},{6,7},{7,6},{8,9},{9,8},{10,11... | collective-permute-start | bytes 1720328 | tf_op jit(solution)/shard_map/ppermute | solution.py:319
  4.6 1.5 %copy-start.1 = (bf16[16,160,320]{2,1,0:T(8,128)(2,1)S(1)}, bf16[16,160,320]{2,1,0:T(8,128)(2,1)}, u32[]{:S(2)}) copy-start(bf16[16,160,320]{2,1,0:T(8,128)(2,1)} %amp_ref.3) | copy-start | bytes 4915204
  6.1 18.5 %copy-start.2 = (bf16[16,160,320]{2,1,0:T(8,128)(2,1)S(1)}, bf16[16,160,320]{2,1,0:T(8,128)(2,1)}, u32[]{:S(2)}) copy-start(bf16[16,160,320]{2,1,0:T(8,128)(2,1)} %amp_ref.3) | copy-start | bytes 4915204
  6.1 18.5 %copy-start.3 = (bf16[320,160]{0,1:T(8,128)(2,1)S(1)}, bf16[320,160]{0,1:T(8,128)(2,1)}, u32[]{:S(2)}) copy-start(bf16[320,160]{0,1:T(8,128)(2,1)} %param.9) | copy-start | bytes 307204
  6.1 18.5 %copy-start.4 = (bf16[40,160]{1,0:T(8,128)(2,1)S(1)}, bf16[40,160]{1,0:T(8,128)(2,1)}, u32[]{:S(2)}) copy-start(bf16[40,160]{1,0:T(8,128)(2,1)} %doubles_ref.3) | copy-start | bytes 38404
  6.1 18.5 %copy-start.5 = (bf16[320,40]{0,1:T(8,128)(2,1)S(1)}, bf16[320,40]{0,1:T(8,128)(2,1)}, u32[]{:S(2)}) copy-start(bf16[320,40]{0,1:T(8,128)(2,1)} %param.10) | copy-start | bytes 76804
  8.0 2.3 %collective-permute-start.2 = (f32[40,640]{1,0:T(8,128)S(1)}, f32[40,640]{1,0:T(8,128)S(1)}, u32[]{:S(2)}, u32[]{:S(2)}) collective-permute-start(f32[40,640]{1,0:T(8,128)S(1)} %get-tuple-element.17), channel_id=1, source_target_pairs={{0,2},{2,0},{4,6},{6,4},{8,10},{10,8},{12,14},{14,12},{16,18},{18,... | collective-permute-start | bytes 307208 | tf_op jit(solution)/shard_map/ppermute | solution.py:318
  8.1 5.7 %collective-permute-start.3 = (f32[40,640]{1,0:T(8,128)S(1)}, f32[40,640]{1,0:T(8,128)S(1)}, u32[]{:S(2)}, u32[]{:S(2)}) collective-permute-start(f32[40,640]{1,0:T(8,128)S(1)} %get-tuple-element.17), channel_id=1, source_target_pairs={{0,4},{2,6},{4,0},{6,2},{8,12},{10,14},{12,8},{14,10},{16,20},{18,... | collective-permute-start | bytes 307208 | tf_op jit(solution)/shard_map/ppermute | solution.py:318
  9.6 5.5 %collective-permute-start.4 = (f32[40,640]{1,0:T(8,128)S(1)}, f32[40,640]{1,0:T(8,128)S(1)}, u32[]{:S(2)}, u32[]{:S(2)}) collective-permute-start(f32[40,640]{1,0:T(8,128)S(1)} %get-tuple-element.17), channel_id=1, source_target_pairs={{0,6},{2,4},{4,2},{6,0},{8,14},{10,12},{12,10},{14,8},{16,22},{18,... | collective-permute-start | bytes 307208 | tf_op jit(solution)/shard_map/ppermute | solution.py:318
  9.9 18.9 %collective-permute-start.9 = (bf16[48,5120]{1,0:T(8,128)(2,1)S(1)}, bf16[48,5120]{1,0:T(8,128)(2,1)S(1)}, u32[]{:S(2)}, u32[]{:S(2)}) collective-permute-start(bf16[48,5120]{1,0:T(8,128)(2,1)S(1)} %get-tuple-element.19), channel_id=1, source_target_pairs={{0,1},{1,0},{2,3},{3,2},{4,5},{5,4},{6,7},{7,6},{8,9},{9,8},{10,11... | collective-permute-start | bytes 1474568 | tf_op jit(solution)/shard_map/ppermute | solution.py:319
  18.3 6.1 %collective-permute-start.5 = (bf16[8,5120]{1,0:T(8,128)(2,1)S(1)}, bf16[8,5120]{1,0:T(8,128)(2,1)S(1)}, u32[]{:S(2)}, u32[]{:S(2)}) collective-permute-start(bf16[8,5120]{1,0:T(8,128)(2,1)S(1)} %slice.3.mine_ref), channel_id=1, source_target_pairs={{0,2},{2,0},{4,6},{6,4},{8,10},{10,8},{12,14},{14,12},{16,18},{18,... | collective-permute-start | bytes 245768 | tf_op jit(solution)/shard_map/ppermute | solution.py:318
  18.3 23.8 %collective-permute-start = (bf16[64,5120]{1,0:T(8,128)(2,1)S(1)}, bf16[64,5120]{1,0:T(8,128)(2,1)S(1)}, u32[]{:S(2)}, u32[]{:S(2)}) collective-permute-start(bf16[64,5120]{1,0:T(8,128)(2,1)S(1)} %get-tuple-element.16), channel_id=1, source_target_pairs={{0,1},{1,0},{2,3},{3,2},{4,5},{5,4},{6,7},{7,6},{8,9},{9,8},{10,11... | collective-permute-start | bytes 1966088 | tf_op jit(solution)/shard_map/ppermute | solution.py:319
  20.4 11.1 %collective-permute-start.6 = (f32[40,640]{1,0:T(8,128)S(1)}, f32[40,640]{1,0:T(8,128)S(1)}, u32[]{:S(2)}, u32[]{:S(2)}) collective-permute-start(f32[40,640]{1,0:T(8,128)S(1)} %add_add_fusion.1), channel_id=1, source_target_pairs={{0,16},{2,18},{4,20},{6,22},{8,24},{10,26},{12,28},{14,30},{16,0},... | collective-permute-start | bytes 307208 | tf_op jit(solution)/shard_map/ppermute | solution.py:318
  23.0 10.0 %collective-permute-start.7 = (f32[40,640]{1,0:T(8,128)S(1)}, f32[40,640]{1,0:T(8,128)S(1)}, u32[]{:S(2)}, u32[]{:S(2)}) collective-permute-start(f32[40,640]{1,0:T(8,128)S(1)} %add_add_fusion.1), channel_id=1, source_target_pairs={{0,24},{2,26},{4,28},{6,30},{8,16},{10,18},{12,20},{14,22},{16,8},... | collective-permute-start | bytes 307208 | tf_op jit(solution)/shard_map/ppermute | solution.py:318
  24.4 8.7 %collective-permute-start.8 = (f32[40,640]{1,0:T(8,128)S(1)}, f32[40,640]{1,0:T(8,128)S(1)}, u32[]{:S(2)}, u32[]{:S(2)}) collective-permute-start(f32[40,640]{1,0:T(8,128)S(1)} %add_add_fusion.1), channel_id=1, source_target_pairs={{0,8},{2,10},{4,12},{6,14},{8,0},{10,2},{12,4},{14,6},{16,24},{18,... | collective-permute-start | bytes 307208 | tf_op jit(solution)/shard_map/ppermute | solution.py:318
  30.0 3.1 %collective-permute-start.10 = (f32[24,640]{1,0:T(8,128)S(1)}, f32[24,640]{1,0:T(8,128)S(1)}, u32[]{:S(2)}, u32[]{:S(2)}) collective-permute-start(f32[24,640]{1,0:T(8,128)S(1)} %gram.2), channel_id=1, source_target_pairs={{0,2},{2,0},{4,6},{6,4},{8,10},{10,8},{12,14},{14,12},{16,18},{18,... | collective-permute-start | bytes 184328 | tf_op jit(solution)/shard_map/ppermute | solution.py:318
  31.5 4.2 %collective-permute-start.11 = (f32[24,640]{1,0:T(8,128)S(1)}, f32[24,640]{1,0:T(8,128)S(1)}, u32[]{:S(2)}, u32[]{:S(2)}) collective-permute-start(f32[24,640]{1,0:T(8,128)S(1)} %gram.2), channel_id=1, source_target_pairs={{0,4},{2,6},{4,0},{6,2},{8,12},{10,14},{12,8},{14,10},{16,20},{18,... | collective-permute-start | bytes 184328 | tf_op jit(solution)/shard_map/ppermute | solution.py:318
  33.0 4.0 %collective-permute-start.12 = (f32[24,640]{1,0:T(8,128)S(1)}, f32[24,640]{1,0:T(8,128)S(1)}, u32[]{:S(2)}, u32[]{:S(2)}) collective-permute-start(f32[24,640]{1,0:T(8,128)S(1)} %gram.2), channel_id=1, source_target_pairs={{0,6},{2,4},{4,2},{6,0},{8,14},{10,12},{12,10},{14,8},{16,22},{18,... | collective-permute-start | bytes 184328 | tf_op jit(solution)/shard_map/ppermute | solution.py:318
  37.0 11.2 %collective-permute-start.19 = (f32[24,640]{1,0:T(8,128)S(1)}, f32[24,640]{1,0:T(8,128)S(1)}, u32[]{:S(2)}, u32[]{:S(2)}) collective-permute-start(f32[24,640]{1,0:T(8,128)S(1)} %add_add_fusion.2), channel_id=1, source_target_pairs={{0,16},{2,18},{4,20},{6,22},{8,24},{10,26},{12,28},{14,30},{16,0},... | collective-permute-start | bytes 184328 | tf_op jit(solution)/shard_map/ppermute | solution.py:318
  39.7 8.8 %collective-permute-start.20 = (f32[24,640]{1,0:T(8,128)S(1)}, f32[24,640]{1,0:T(8,128)S(1)}, u32[]{:S(2)}, u32[]{:S(2)}) collective-permute-start(f32[24,640]{1,0:T(8,128)S(1)} %add_add_fusion.2), channel_id=1, source_target_pairs={{0,24},{2,26},{4,28},{6,30},{8,16},{10,18},{12,20},{14,22},{16,8},... | collective-permute-start | bytes 184328 | tf_op jit(solution)/shard_map/ppermute | solution.py:318
  40.2 8.3 %collective-permute-start.21 = (f32[24,640]{1,0:T(8,128)S(1)}, f32[24,640]{1,0:T(8,128)S(1)}, u32[]{:S(2)}, u32[]{:S(2)}) collective-permute-start(f32[24,640]{1,0:T(8,128)S(1)} %add_add_fusion.2), channel_id=1, source_target_pairs={{0,8},{2,10},{4,12},{6,14},{8,0},{10,2},{12,4},{14,6},{16,24},{18,... | collective-permute-start | bytes 184328 | tf_op jit(solution)/shard_map/ppermute | solution.py:318
  42.8 1.3 %collective-permute-start.13 = (f32[16,640]{1,0:T(8,128)S(1)}, f32[16,640]{1,0:T(8,128)S(1)}, u32[]{:S(2)}, u32[]{:S(2)}) collective-permute-start(f32[16,640]{1,0:T(8,128)S(1)} %gram.3), channel_id=1, source_target_pairs={{0,2},{2,0},{4,6},{6,4},{8,10},{10,8},{12,14},{14,12},{16,18},{18,... | collective-permute-start | bytes 122888 | tf_op jit(solution)/shard_map/ppermute | solution.py:318
  44.1 6.2 %collective-permute-start.14 = (f32[16,640]{1,0:T(8,128)S(1)}, f32[16,640]{1,0:T(8,128)S(1)}, u32[]{:S(2)}, u32[]{:S(2)}) collective-permute-start(f32[16,640]{1,0:T(8,128)S(1)} %add.60), channel_id=1, source_target_pairs={{0,16},{2,18},{4,20},{6,22},{8,24},{10,26},{12,28},{14,30},{16,0},... | collective-permute-start | bytes 122888 | tf_op jit(solution)/shard_map/ppermute | solution.py:318
  47.6 5.8 %collective-permute-start.15 = (f32[16,640]{1,0:T(8,128)S(1)}, f32[16,640]{1,0:T(8,128)S(1)}, u32[]{:S(2)}, u32[]{:S(2)}) collective-permute-start(f32[16,640]{1,0:T(8,128)S(1)} %add.60), channel_id=1, source_target_pairs={{0,24},{2,26},{4,28},{6,30},{8,16},{10,18},{12,20},{14,22},{16,8},... | collective-permute-start | bytes 122888 | tf_op jit(solution)/shard_map/ppermute | solution.py:318
  48.3 5.1 %collective-permute-start.16 = (f32[16,640]{1,0:T(8,128)S(1)}, f32[16,640]{1,0:T(8,128)S(1)}, u32[]{:S(2)}, u32[]{:S(2)}) collective-permute-start(f32[16,640]{1,0:T(8,128)S(1)} %add.60), channel_id=1, source_target_pairs={{0,8},{2,10},{4,12},{6,14},{8,0},{10,2},{12,4},{14,6},{16,24},{18,... | collective-permute-start | bytes 122888 | tf_op jit(solution)/shard_map/ppermute | solution.py:318
  48.5 7.9 %collective-permute-start.22 = (bf16[24,640]{1,0:T(8,128)(2,1)S(1)}, bf16[24,640]{1,0:T(8,128)(2,1)S(1)}, u32[]{:S(2)}, u32[]{:S(2)}) collective-permute-start(bf16[24,640]{1,0:T(8,128)(2,1)S(1)} %multiply_convert_fusion), channel_id=1, source_target_pairs={{0,1},{1,0},{2,3},{3,2},{4,5},{5,4},{6,7},{7,6},{8,9},{9,8},{10,11... | collective-permute-start | bytes 92168 | tf_op jit(solution)/shard_map/ppermute | solution.py:319
  53.4 5.0 %collective-permute-start.17 = (f32[16,640]{1,0:T(8,128)S(1)}, f32[16,640]{1,0:T(8,128)S(1)}, u32[]{:S(2)}, u32[]{:S(2)}) collective-permute-start(f32[16,640]{1,0:T(8,128)S(1)} %add_add_fusion.3), channel_id=1, source_target_pairs={{0,5},{1,4},{2,7},{3,6},{4,1},{5,0},{6,3},{7,2},{8,13},{9,12},{10,... | collective-permute-start | bytes 122888 | tf_op jit(solution)/shard_map/ppermute | solution.py:319
  55.2 4.0 %collective-permute-start.18 = (f32[16,640]{1,0:T(8,128)S(1)}, f32[16,640]{1,0:T(8,128)S(1)}, u32[]{:S(2)}, u32[]{:S(2)}) collective-permute-start(f32[16,640]{1,0:T(8,128)S(1)} %add_add_fusion.3), channel_id=1, source_target_pairs={{0,1},{1,0},{2,3},{3,2},{4,5},{5,4},{6,7},{7,6},{8,9},{9,8},{10,11... | collective-permute-start | bytes 122888 | tf_op jit(solution)/shard_map/ppermute | solution.py:319

commit v6 on v5

--- a/solution.py
+++ b/solution.py
@@ -333,6 +333,11 @@
     return x
 
 
+def two_step_sum(x):
+    x = x + permute(x, 1)
+    return x + permute(x, 2)
+
+
 def near_sum(x):
     far, mid, close = permute(x, 3), permute(x, 2), permute(x, 1)
     return (x + close) + (mid + far)
@@ -365,7 +370,7 @@
     near = near_of(lam, amp, keep, cycle.T, ladder, doubles, mine, other)
 
     early_got = after(early_got, near)
-    early = near_sum(gram((first_got, early_got), amp_all))
+    early = two_step_sum(gram((first_got, early_got), amp_all))
     near = add_own(keep, lam, near, after(own_den, early), norm, scale)
 
     early = far_sum(early)

time: 60.7 us -> 60.7 us (level)
  starting transfers between devices: 25.7 us -> 27.7 us
  waiting for transfers between devices: 19.2 us -> 17.2 us
    ppermute x17 -> x16, waiting for transfers between devices: 14.8 us -> 11 us  [permute(): return lax.ppermute(x, 'occ', [(i, i ^ flip) for i in range(n)])]
    ppermute x17 -> x16, starting transfers between devices: 15.7 us -> 18.1 us  [permute(): return lax.ppermute(x, 'occ', [(i, i ^ flip) for i in range(n)])]
    ppermute x6, waiting for transfers between devices: 4.44 us -> 6.29 us  [permute(): lax.ppermute(x, ('occ', 'vir'), [(i * v + j, (i ^ flip) * v + (j ^ swap))...]
  transfers between devices with their start and end apart: 23 -> 22, of which waited for: 12 -> 11; matrix products, arithmetic and copies ran while one was open for 0% -> 0% of each run, Pallas kernels for 18% -> 18%
where the time goes in v6:
time: 60.7 us; the launch traced here: 60.5 us
  starting transfers between devices  27.7 us (46%)
  waiting for transfers between devices  17.2 us (28%)
  Pallas kernels  13.7 us (23%)
  local copies, waits for them, and re-layouts  1.57 us (3%)
    ppermute x16, starting transfers between devices, permute(): return lax.ppermute(x, 'occ', [(i, i ^ flip) for i in range(n)])  18.1 us
    ppermute x16, waiting for transfers between devices, permute(): return lax.ppermute(x, 'occ', [(i, i ^ flip) for i in range(n)])  11 us
    ppermute x6, starting transfers between devices, permute(): lax.ppermute(x, ('occ', 'vir'), [(i * v + j, (i ^ flip) * v + (j ^ swap))...  9.61 us
    ppermute x6, waiting for transfers between devices, permute(): lax.ppermute(x, ('occ', 'vir'), [(i * v + j, (i ^ flip) * v + (j ^ swap))...  6.29 us
    pallas_call x1, Pallas kernels, near_of(): pl.pallas_call(functools.partial(near_kernel, step), grid=(triples // ste...  4.04 us
    pallas_call x2, Pallas kernels, gram(): pl.pallas_call(gram_kernel, in_specs=[VMEM()] * (len(xs) + 1), out_specs=...  1.89 us
    pallas_call x1, Pallas kernels, prepare(): pl.pallas_call(prepare_kernel, grid=(1,), in_specs=[whole(lam), whole(fir...  1.85 us
    pallas_call x1, Pallas kernels, early_output(): pl.pallas_call(functools.partial(early_kernel, scale), grid=(1,), in_spec...  1.66 us
  transfers between devices with their start and end apart: 22, of which 11 were waited for; matrix products, arithmetic and copies ran while one was open for 0% of the time, Pallas kernels for 18%

profile of v6, /device:TPU:0, one launch (start us, length us, event | category | flops | bytes accessed | tf_op | source)
XLA Modules:
  0.0 60.5 jit_solution(10036589971819283086)
XLA Ops:
  0.0 1.5 %pack.1.first_ref = bf16[56,5120]{1,0:T(8,128)(2,1)S(1)} custom-call(bf16[16,160,320]{2,1,0:T(8,128)(2,1)} %lam_ref.5, bf16[160,320]{1,0:T(8,128)(2,1)} %bitcast.2, bf16[40,160]{1,0:T(8,128)(2,1)} %doubles_ref.3), custom_call_target="tpu_custom_call" | custom-call | flops 491520 | bytes 983040 | tf_op jit(solution)/shard_map/pack/pallas_call | solution.py:86
  1.5 3.0 %collective-permute-start.1 = (bf16[56,5120]{1,0:T(8,128)(2,1)S(1)}, bf16[56,5120]{1,0:T(8,128)(2,1)S(1)}, u32[]{:S(2)}, u32[]{:S(2)}) collective-permute-start(bf16[56,5120]{1,0:T(8,128)(2,1)S(1)} %pack.1.first_ref), channel_id=1, source_target_pairs={{0,1},{1,0},{2,3},{3,2},{4,5},{5,4},{6,7},{7,6},{8,9},{9,8},{10,11... | collective-permute-start | bytes 1720328 | tf_op jit(solution)/shard_map/ppermute | solution.py:319
  4.5 0.1 fusion.keep_ref
  4.6 1.5 %copy-done.1 = bf16[16,160,320]{2,1,0:T(8,128)(2,1)S(1)} copy-done((bf16[16,160,320]{2,1,0:T(8,128)(2,1)S(1)}, bf16[16,160,320]{2,1,0:T(8,128)(2,1)}, u32[]{:S(2)}) %copy-start.1) | copy-done | bytes 1638424
  6.1 1.9 %prepare.1 = (bf16[48,5120]{1,0:T(8,128)(2,1)S(1)}, bf16[64,5120]{1,0:T(8,128)(2,1)S(1)}, bf16[160,5120]{1,0:T(8,128)(2,1)S(1)}, f32[40,640]{1,0:T(8,128)S(1)}) custom-call(bf16[16,160,320]{2,1,0:T(8,128)(2,1)S(1)} %copy-done, bf16[56,5120]{1,0:T(8,128)(2,1)S(1)} %pack.1.first_ref, bf16[16,160,320]{2,1,0:T(8,128)(2,1)S(1)} %copy-done.1, ...), custom_call_target="tpu_custom_call" | custom-call | flops 262144000 | bytes 4915200 | tf_op jit(solution)/shard_map/prepare/pallas_call | solution.py:143
  8.0 0.3 collective-permute-start.9
  8.3 0.0 collective-permute-start.2
  8.3 1.8 %collective-permute-start.3 = (f32[40,640]{1,0:T(8,128)S(1)}, f32[40,640]{1,0:T(8,128)S(1)}, u32[]{:S(2)}, u32[]{:S(2)}) collective-permute-start(f32[40,640]{1,0:T(8,128)S(1)} %get-tuple-element.17), channel_id=1, source_target_pairs={{0,4},{2,6},{4,0},{6,2},{8,12},{10,14},{12,8},{14,10},{16,20},{18,... | collective-permute-start | bytes 307208 | tf_op jit(solution)/shard_map/ppermute | solution.py:318
  10.1 0.1 collective-permute-start.4
  10.2 0.0 collective-permute-done.2
  10.3 1.7 %collective-permute-start = (bf16[64,5120]{1,0:T(8,128)(2,1)S(1)}, bf16[64,5120]{1,0:T(8,128)(2,1)S(1)}, u32[]{:S(2)}, u32[]{:S(2)}) collective-permute-start(bf16[64,5120]{1,0:T(8,128)(2,1)S(1)} %get-tuple-element.16), channel_id=1, source_target_pairs={{0,1},{1,0},{2,3},{3,2},{4,5},{5,4},{6,7},{7,6},{8,9},{9,8},{10,11... | collective-permute-start | bytes 1966088 | tf_op jit(solution)/shard_map/ppermute | solution.py:319
  11.9 2.0 %collective-permute-done.3 = f32[40,640]{1,0:T(8,128)S(1)} collective-permute-done((f32[40,640]{1,0:T(8,128)S(1)}, f32[40,640]{1,0:T(8,128)S(1)}, u32[]{:S(2)}, u32[]{:S(2)}) %collective-permute-start.3) | collective-permute-done | bytes 102432 | tf_op jit(solution)/shard_map/ppermute | solution.py:318
  14.0 1.6 %collective-permute-done.4 = f32[40,640]{1,0:T(8,128)S(1)} collective-permute-done((f32[40,640]{1,0:T(8,128)S(1)}, f32[40,640]{1,0:T(8,128)S(1)}, u32[]{:S(2)}, u32[]{:S(2)}) %collective-permute-start.4) | collective-permute-done | bytes 102432 | tf_op jit(solution)/shard_map/ppermute | solution.py:318
  15.6 2.7 %collective-permute-done.1.refs_0_.refs_1_ = bf16[56,5120]{1,0:T(8,128)(2,1)S(1)} collective-permute-done((bf16[56,5120]{1,0:T(8,128)(2,1)S(1)}, bf16[56,5120]{1,0:T(8,128)(2,1)S(1)}, u32[]{:S(2)}, u32[]{:S(2)}) %collective-permute-start.1) | collective-permute-done | bytes 573472 | tf_op jit(solution)/shard_map/ppermute | solution.py:319
  18.3 0.0 collective-permute-start.5
  18.3 3.2 %collective-permute-start.6 = (f32[40,640]{1,0:T(8,128)S(1)}, f32[40,640]{1,0:T(8,128)S(1)}, u32[]{:S(2)}, u32[]{:S(2)}) collective-permute-start(f32[40,640]{1,0:T(8,128)S(1)} %add_add_fusion.1), channel_id=1, source_target_pairs={{0,16},{2,18},{4,20},{6,22},{8,24},{10,26},{12,28},{14,30},{16,0},... | collective-permute-start | bytes 307208 | tf_op jit(solution)/shard_map/ppermute | solution.py:318
  21.5 1.3 %collective-permute-start.7 = (f32[40,640]{1,0:T(8,128)S(1)}, f32[40,640]{1,0:T(8,128)S(1)}, u32[]{:S(2)}, u32[]{:S(2)}) collective-permute-start(f32[40,640]{1,0:T(8,128)S(1)} %add_add_fusion.1), channel_id=1, source_target_pairs={{0,24},{2,26},{4,28},{6,30},{8,16},{10,18},{12,20},{14,22},{16,8},... | collective-permute-start | bytes 307208 | tf_op jit(solution)/shard_map/ppermute | solution.py:318
  22.9 0.0 collective-permute-done.5.other_ref
  22.9 0.2 collective-permute-start.8
  23.1 4.0 %near.1.near_ref = f32[16,160,320]{2,1,0:T(8,128)S(1)} custom-call(f32[16,320]{1,0:T(8,128)S(1)} %fusion.keep_ref, bf16[16,160,320]{2,1,0:T(8,128)(2,1)S(1)} %copy-done, bf16[16,160,320]{2,1,0:T(8,128)(2,1)S(1)} %copy-done.2, bf16[40,320]{1,0:T(8,128)(2,1)S(1)} %bitcast.4, bf16[160,320]{1,0:T(8,128)(2,1)S(1)} %bitcast.3, bf16[40,160]{1,0:T(8,128)(2,1)S(1)} %copy-done.4, ...), custom_call_target="tpu_custom_call" | custom-call | flops 629145600 | bytes 6553600 | tf_op jit(solution)/shard_map/near/pallas_call | solution.py:204
  27.2 1.7 %collective-permute-done.9.refs_1_.refs_2_ = bf16[48,5120]{1,0:T(8,128)(2,1)S(1)} collective-permute-done((bf16[48,5120]{1,0:T(8,128)(2,1)S(1)}, bf16[48,5120]{1,0:T(8,128)(2,1)S(1)}, u32[]{:S(2)}, u32[]{:S(2)}) %collective-permute-start.9) | collective-permute-done | bytes 491552 | tf_op jit(solution)/shard_map/ppermute | solution.py:319
  28.8 1.2 %gram.2 = f32[24,640]{1,0:T(8,128)S(1)} custom-call(bf16[56,5120]{1,0:T(8,128)(2,1)S(1)} %collective-permute-done.1.refs_0_.refs_1_, bf16[48,5120]{1,0:T(8,128)(2,1)S(1)} %collective-permute-done.9.refs_1_.refs_2_, bf16[160,5120]{1,0:T(8,128)(2,1)S(1)} %get-tuple-element.21.refs_2_.refs_1_), custom_call_target="tpu_custom_call" | custom-call | flops 157286400 | bytes 2621440 | tf_op jit(solution)/shard_map/gram/pallas_call | solution.py:163
  30.0 0.1 collective-permute-start.10
  30.1 1.2 %collective-permute-done.10 = f32[24,640]{1,0:T(8,128)S(1)} collective-permute-done((f32[24,640]{1,0:T(8,128)S(1)}, f32[24,640]{1,0:T(8,128)S(1)}, u32[]{:S(2)}, u32[]{:S(2)}) %collective-permute-start.10) | collective-permute-done | bytes 61472 | tf_op jit(solution)/shard_map/ppermute | solution.py:318
  31.3 2.2 %collective-permute-start.11 = (f32[24,640]{1,0:T(8,128)S(1)}, f32[24,640]{1,0:T(8,128)S(1)}, u32[]{:S(2)}, u32[]{:S(2)}) collective-permute-start(f32[24,640]{1,0:T(8,128)S(1)} %add.54), channel_id=1, source_target_pairs={{0,4},{2,6},{4,0},{6,2},{8,12},{10,14},{12,8},{14,10},{16,20},{18,... | collective-permute-start | bytes 184328 | tf_op jit(solution)/shard_map/ppermute | solution.py:318
  33.5 2.3 %collective-permute-done.11 = f32[24,640]{1,0:T(8,128)S(1)} collective-permute-done((f32[24,640]{1,0:T(8,128)S(1)}, f32[24,640]{1,0:T(8,128)S(1)}, u32[]{:S(2)}, u32[]{:S(2)}) %collective-permute-start.11) | collective-permute-done | bytes 61472 | tf_op jit(solution)/shard_map/ppermute | solution.py:318
  35.8 3.0 %collective-permute-start.18 = (f32[24,640]{1,0:T(8,128)S(1)}, f32[24,640]{1,0:T(8,128)S(1)}, u32[]{:S(2)}, u32[]{:S(2)}) collective-permute-start(f32[24,640]{1,0:T(8,128)S(1)} %add.55), channel_id=1, source_target_pairs={{0,16},{2,18},{4,20},{6,22},{8,24},{10,26},{12,28},{14,30},{16,0},... | collective-permute-start | bytes 184328 | tf_op jit(solution)/shard_map/ppermute | solution.py:318
  38.8 1.3 %collective-permute-start.19 = (f32[24,640]{1,0:T(8,128)S(1)}, f32[24,640]{1,0:T(8,128)S(1)}, u32[]{:S(2)}, u32[]{:S(2)}) collective-permute-start(f32[24,640]{1,0:T(8,128)S(1)} %add.55), channel_id=1, source_target_pairs={{0,24},{2,26},{4,28},{6,30},{8,16},{10,18},{12,20},{14,22},{16,8},... | collective-permute-start | bytes 184328 | tf_op jit(solution)/shard_map/ppermute | solution.py:318
  40.2 0.2 collective-permute-start.20
  40.4 1.5 %add_own.1.refs_3_.near_ref = f32[16,160,320]{2,1,0:T(8,128)S(1)} custom-call(f32[16,320]{1,0:T(8,128)S(1)} %fusion.keep_ref, bf16[16,160,320]{2,1,0:T(8,128)(2,1)S(1)} %copy-done, f32[16,160,320]{2,1,0:T(8,128)S(1)} %near.1.near_ref, f32[40,640]{1,0:T(8,128)S(1)} %add_add_fusion.den_ref), custom_call_target="tpu_custom_call", output_to_operand_aliasing={{}: (2, {})} | custom-call | flops 262144000 | bytes 8192000 | tf_op jit(solution)/shard_map/add_own/pallas_call | solution.py:228
  41.9 0.1 collective-permute-done.refs_0_
  42.0 0.7 %gram.3 = f32[16,640]{1,0:T(8,128)S(1)} custom-call(bf16[64,5120]{1,0:T(8,128)(2,1)S(1)} %collective-permute-done.refs_0_, bf16[160,5120]{1,0:T(8,128)(2,1)S(1)} %get-tuple-element.21.refs_2_.refs_1_), custom_call_target="tpu_custom_call" | custom-call | flops 104857600 | bytes 2293760 | tf_op jit(solution)/shard_map/gram/pallas_call | solution.py:163
  42.8 0.1 collective-permute-start.12
  42.8 1.2 %collective-permute-done.12 = f32[16,640]{1,0:T(8,128)S(1)} collective-permute-done((f32[16,640]{1,0:T(8,128)S(1)}, f32[16,640]{1,0:T(8,128)S(1)}, u32[]{:S(2)}, u32[]{:S(2)}) %collective-permute-start.12) | collective-permute-done | bytes 40992 | tf_op jit(solution)/shard_map/ppermute | solution.py:318
  44.1 2.8 %collective-permute-start.13 = (f32[16,640]{1,0:T(8,128)S(1)}, f32[16,640]{1,0:T(8,128)S(1)}, u32[]{:S(2)}, u32[]{:S(2)}) collective-permute-start(f32[16,640]{1,0:T(8,128)S(1)} %add.56), channel_id=1, source_target_pairs={{0,16},{2,18},{4,20},{6,22},{8,24},{10,26},{12,28},{14,30},{16,0},... | collective-permute-start | bytes 122888 | tf_op jit(solution)/shard_map/ppermute | solution.py:318
  46.9 1.3 %collective-permute-start.14 = (f32[16,640]{1,0:T(8,128)S(1)}, f32[16,640]{1,0:T(8,128)S(1)}, u32[]{:S(2)}, u32[]{:S(2)}) collective-permute-start(f32[16,640]{1,0:T(8,128)S(1)} %add.56), channel_id=1, source_target_pairs={{0,24},{2,26},{4,28},{6,30},{8,16},{10,18},{12,20},{14,22},{16,8},... | collective-permute-start | bytes 122888 | tf_op jit(solution)/shard_map/ppermute | solution.py:318
  48.2 0.0 collective-permute-done.18
  48.3 0.2 collective-permute-start.15
  48.5 0.0 collective-permute-done.19
  48.5 0.0 collective-permute-done.20
  48.5 1.6 %collective-permute-start.21 = (bf16[24,640]{1,0:T(8,128)(2,1)S(1)}, bf16[24,640]{1,0:T(8,128)(2,1)S(1)}, u32[]{:S(2)}, u32[]{:S(2)}) collective-permute-start(bf16[24,640]{1,0:T(8,128)(2,1)S(1)} %multiply_convert_fusion), channel_id=1, source_target_pairs={{0,1},{1,0},{2,3},{3,2},{4,5},{5,4},{6,7},{7,6},{8,9},{9,8},{10,11... | collective-permute-start | bytes 92168 | tf_op jit(solution)/shard_map/ppermute | solution.py:319
  50.1 2.6 %collective-permute-done.14 = f32[16,640]{1,0:T(8,128)S(1)} collective-permute-done((f32[16,640]{1,0:T(8,128)S(1)}, f32[16,640]{1,0:T(8,128)S(1)}, u32[]{:S(2)}, u32[]{:S(2)}) %collective-permute-start.14) | collective-permute-done | bytes 40992 | tf_op jit(solution)/shard_map/ppermute | solution.py:318
  52.7 2.5 %collective-permute-start.16 = (f32[16,640]{1,0:T(8,128)S(1)}, f32[16,640]{1,0:T(8,128)S(1)}, u32[]{:S(2)}, u32[]{:S(2)}) collective-permute-start(f32[16,640]{1,0:T(8,128)S(1)} %add_add_fusion.2), channel_id=1, source_target_pairs={{0,5},{1,4},{2,7},{3,6},{4,1},{5,0},{6,3},{7,2},{8,13},{9,12},{10,... | collective-permute-start | bytes 122888 | tf_op jit(solution)/shard_map/ppermute | solution.py:319
  55.2 0.5 collective-permute-start.17
  55.8 1.7 %early.1 = (bf16[16,160,320]{2,1,0:T(8,128)(2,1)}, bf16[160,5120]{1,0:T(8,128)(2,1)S(1)}) custom-call(f32[16,320]{1,0:T(8,128)S(1)} %fusion.keep_ref, bf16[24,640]{1,0:T(8,128)(2,1)S(1)} %collective-permute-done.21.den_ref, bf16[64,5120]{1,0:T(8,128)(2,1)S(1)} %collective-permute-done.refs_0_, bf16[56,5120]{1,0:T(8,128)(2,1)S(1)} %collective-permute-done.1.refs_0_.refs_1_, ...), custom_call_target="tpu_custom_call" | custom-call | flops 262144000 | bytes 4915200 | tf_op jit(solution)/shard_map/early/pallas_call | solution.py:274
  57.4 0.2 collective-permute-done.16
  57.7 1.5 %collective-permute-done.17 = f32[16,640]{1,0:T(8,128)S(1)} collective-permute-done((f32[16,640]{1,0:T(8,128)S(1)}, f32[16,640]{1,0:T(8,128)S(1)}, u32[]{:S(2)}, u32[]{:S(2)}) %collective-permute-start.17) | collective-permute-done | bytes 40992 | tf_op jit(solution)/shard_map/ppermute | solution.py:319
  59.2 1.3 %late.1 = bf16[16,160,320]{2,1,0:T(8,128)(2,1)} custom-call(f32[16,320]{1,0:T(8,128)S(1)} %fusion.keep_ref, bf16[16,640]{1,0:T(8,128)(2,1)S(1)} %multiply_convert_fusion.1.den_ref, bf16[160,5120]{1,0:T(8,128)(2,1)S(1)} %get-tuple-element.25.got_ref, f32[16,160,320]{2,1,0:T(8,128)S(1)} %add_own.1.refs_3_.near_ref, ...), custom_call_target="tpu_custom_call", output_to_operand_aliasing={{}: (4, {})} | custom-call | flops 104857600 | bytes 1966080 | tf_op jit(solution)/shard_map/late/pallas_call | solution.py:302
  (28 shorter events, 0.2 us)
Async XLA Ops:
  0.0 4.6 %copy-start = (bf16[16,160,320]{2,1,0:T(8,128)(2,1)S(1)}, bf16[16,160,320]{2,1,0:T(8,128)(2,1)}, u32[]{:S(2)}) copy-start(bf16[16,160,320]{2,1,0:T(8,128)(2,1)} %lam_ref.5) | copy-start | bytes 4915204
  0.0 4.5 %copy-start.6 = (s32[16]{0:T(128)S(1)}, s32[16]{0:T(128)}, u32[]{:S(2)}) copy-start(s32[16]{0:T(128)} %param.8) | copy-start | bytes 196
  1.5 16.8 %collective-permute-start.1 = (bf16[56,5120]{1,0:T(8,128)(2,1)S(1)}, bf16[56,5120]{1,0:T(8,128)(2,1)S(1)}, u32[]{:S(2)}, u32[]{:S(2)}) collective-permute-start(bf16[56,5120]{1,0:T(8,128)(2,1)S(1)} %pack.1.first_ref), channel_id=1, source_target_pairs={{0,1},{1,0},{2,3},{3,2},{4,5},{5,4},{6,7},{7,6},{8,9},{9,8},{10,11... | collective-permute-start | bytes 1720328 | tf_op jit(solution)/shard_map/ppermute | solution.py:319
  4.6 1.5 %copy-start.1 = (bf16[16,160,320]{2,1,0:T(8,128)(2,1)S(1)}, bf16[16,160,320]{2,1,0:T(8,128)(2,1)}, u32[]{:S(2)}) copy-start(bf16[16,160,320]{2,1,0:T(8,128)(2,1)} %amp_ref.3) | copy-start | bytes 4915204
  6.1 17.0 %copy-start.2 = (bf16[16,160,320]{2,1,0:T(8,128)(2,1)S(1)}, bf16[16,160,320]{2,1,0:T(8,128)(2,1)}, u32[]{:S(2)}) copy-start(bf16[16,160,320]{2,1,0:T(8,128)(2,1)} %amp_ref.3) | copy-start | bytes 4915204
  6.1 17.0 %copy-start.3 = (bf16[320,160]{0,1:T(8,128)(2,1)S(1)}, bf16[320,160]{0,1:T(8,128)(2,1)}, u32[]{:S(2)}) copy-start(bf16[320,160]{0,1:T(8,128)(2,1)} %param.9) | copy-start | bytes 307204
  6.1 17.0 %copy-start.4 = (bf16[40,160]{1,0:T(8,128)(2,1)S(1)}, bf16[40,160]{1,0:T(8,128)(2,1)}, u32[]{:S(2)}) copy-start(bf16[40,160]{1,0:T(8,128)(2,1)} %doubles_ref.3) | copy-start | bytes 38404
  6.1 17.0 %copy-start.5 = (bf16[320,40]{0,1:T(8,128)(2,1)S(1)}, bf16[320,40]{0,1:T(8,128)(2,1)}, u32[]{:S(2)}) copy-start(bf16[320,40]{0,1:T(8,128)(2,1)} %param.10) | copy-start | bytes 76804
  8.0 20.8 %collective-permute-start.9 = (bf16[48,5120]{1,0:T(8,128)(2,1)S(1)}, bf16[48,5120]{1,0:T(8,128)(2,1)S(1)}, u32[]{:S(2)}, u32[]{:S(2)}) collective-permute-start(bf16[48,5120]{1,0:T(8,128)(2,1)S(1)} %get-tuple-element.19), channel_id=1, source_target_pairs={{0,1},{1,0},{2,3},{3,2},{4,5},{5,4},{6,7},{7,6},{8,9},{9,8},{10,11... | collective-permute-start | bytes 1474568 | tf_op jit(solution)/shard_map/ppermute | solution.py:319
  8.3 2.0 %collective-permute-start.2 = (f32[40,640]{1,0:T(8,128)S(1)}, f32[40,640]{1,0:T(8,128)S(1)}, u32[]{:S(2)}, u32[]{:S(2)}) collective-permute-start(f32[40,640]{1,0:T(8,128)S(1)} %get-tuple-element.17), channel_id=1, source_target_pairs={{0,2},{2,0},{4,6},{6,4},{8,10},{10,8},{12,14},{14,12},{16,18},{18,... | collective-permute-start | bytes 307208 | tf_op jit(solution)/shard_map/ppermute | solution.py:318
  8.3 5.7 %collective-permute-start.3 = (f32[40,640]{1,0:T(8,128)S(1)}, f32[40,640]{1,0:T(8,128)S(1)}, u32[]{:S(2)}, u32[]{:S(2)}) collective-permute-start(f32[40,640]{1,0:T(8,128)S(1)} %get-tuple-element.17), channel_id=1, source_target_pairs={{0,4},{2,6},{4,0},{6,2},{8,12},{10,14},{12,8},{14,10},{16,20},{18,... | collective-permute-start | bytes 307208 | tf_op jit(solution)/shard_map/ppermute | solution.py:318
  10.1 5.4 %collective-permute-start.4 = (f32[40,640]{1,0:T(8,128)S(1)}, f32[40,640]{1,0:T(8,128)S(1)}, u32[]{:S(2)}, u32[]{:S(2)}) collective-permute-start(f32[40,640]{1,0:T(8,128)S(1)} %get-tuple-element.17), channel_id=1, source_target_pairs={{0,6},{2,4},{4,2},{6,0},{8,14},{10,12},{12,10},{14,8},{16,22},{18,... | collective-permute-start | bytes 307208 | tf_op jit(solution)/shard_map/ppermute | solution.py:318
  10.3 31.8 %collective-permute-start = (bf16[64,5120]{1,0:T(8,128)(2,1)S(1)}, bf16[64,5120]{1,0:T(8,128)(2,1)S(1)}, u32[]{:S(2)}, u32[]{:S(2)}) collective-permute-start(bf16[64,5120]{1,0:T(8,128)(2,1)S(1)} %get-tuple-element.16), channel_id=1, source_target_pairs={{0,1},{1,0},{2,3},{3,2},{4,5},{5,4},{6,7},{7,6},{8,9},{9,8},{10,11... | collective-permute-start | bytes 1966088 | tf_op jit(solution)/shard_map/ppermute | solution.py:319
  18.3 4.6 %collective-permute-start.5 = (bf16[8,5120]{1,0:T(8,128)(2,1)S(1)}, bf16[8,5120]{1,0:T(8,128)(2,1)S(1)}, u32[]{:S(2)}, u32[]{:S(2)}) collective-permute-start(bf16[8,5120]{1,0:T(8,128)(2,1)S(1)} %slice.3.mine_ref), channel_id=1, source_target_pairs={{0,2},{2,0},{4,6},{6,4},{8,10},{10,8},{12,14},{14,12},{16,18},{18,... | collective-permute-start | bytes 245768 | tf_op jit(solution)/shard_map/ppermute | solution.py:318
  18.3 15.2 %collective-permute-start.6 = (f32[40,640]{1,0:T(8,128)S(1)}, f32[40,640]{1,0:T(8,128)S(1)}, u32[]{:S(2)}, u32[]{:S(2)}) collective-permute-start(f32[40,640]{1,0:T(8,128)S(1)} %add_add_fusion.1), channel_id=1, source_target_pairs={{0,16},{2,18},{4,20},{6,22},{8,24},{10,26},{12,28},{14,30},{16,0},... | collective-permute-start | bytes 307208 | tf_op jit(solution)/shard_map/ppermute | solution.py:318
  21.5 12.0 %collective-permute-start.7 = (f32[40,640]{1,0:T(8,128)S(1)}, f32[40,640]{1,0:T(8,128)S(1)}, u32[]{:S(2)}, u32[]{:S(2)}) collective-permute-start(f32[40,640]{1,0:T(8,128)S(1)} %add_add_fusion.1), channel_id=1, source_target_pairs={{0,24},{2,26},{4,28},{6,30},{8,16},{10,18},{12,20},{14,22},{16,8},... | collective-permute-start | bytes 307208 | tf_op jit(solution)/shard_map/ppermute | solution.py:318
  22.9 10.6 %collective-permute-start.8 = (f32[40,640]{1,0:T(8,128)S(1)}, f32[40,640]{1,0:T(8,128)S(1)}, u32[]{:S(2)}, u32[]{:S(2)}) collective-permute-start(f32[40,640]{1,0:T(8,128)S(1)} %add_add_fusion.1), channel_id=1, source_target_pairs={{0,8},{2,10},{4,12},{6,14},{8,0},{10,2},{12,4},{14,6},{16,24},{18,... | collective-permute-start | bytes 307208 | tf_op jit(solution)/shard_map/ppermute | solution.py:318
  30.0 1.3 %collective-permute-start.10 = (f32[24,640]{1,0:T(8,128)S(1)}, f32[24,640]{1,0:T(8,128)S(1)}, u32[]{:S(2)}, u32[]{:S(2)}) collective-permute-start(f32[24,640]{1,0:T(8,128)S(1)} %gram.2), channel_id=1, source_target_pairs={{0,2},{2,0},{4,6},{6,4},{8,10},{10,8},{12,14},{14,12},{16,18},{18,... | collective-permute-start | bytes 184328 | tf_op jit(solution)/shard_map/ppermute | solution.py:318
  31.3 4.5 %collective-permute-start.11 = (f32[24,640]{1,0:T(8,128)S(1)}, f32[24,640]{1,0:T(8,128)S(1)}, u32[]{:S(2)}, u32[]{:S(2)}) collective-permute-start(f32[24,640]{1,0:T(8,128)S(1)} %add.54), channel_id=1, source_target_pairs={{0,4},{2,6},{4,0},{6,2},{8,12},{10,14},{12,8},{14,10},{16,20},{18,... | collective-permute-start | bytes 184328 | tf_op jit(solution)/shard_map/ppermute | solution.py:318
  35.8 12.4 %collective-permute-start.18 = (f32[24,640]{1,0:T(8,128)S(1)}, f32[24,640]{1,0:T(8,128)S(1)}, u32[]{:S(2)}, u32[]{:S(2)}) collective-permute-start(f32[24,640]{1,0:T(8,128)S(1)} %add.55), channel_id=1, source_target_pairs={{0,16},{2,18},{4,20},{6,22},{8,24},{10,26},{12,28},{14,30},{16,0},... | collective-permute-start | bytes 184328 | tf_op jit(solution)/shard_map/ppermute | solution.py:318
  38.8 9.6 %collective-permute-start.19 = (f32[24,640]{1,0:T(8,128)S(1)}, f32[24,640]{1,0:T(8,128)S(1)}, u32[]{:S(2)}, u32[]{:S(2)}) collective-permute-start(f32[24,640]{1,0:T(8,128)S(1)} %add.55), channel_id=1, source_target_pairs={{0,24},{2,26},{4,28},{6,30},{8,16},{10,18},{12,20},{14,22},{16,8},... | collective-permute-start | bytes 184328 | tf_op jit(solution)/shard_map/ppermute | solution.py:318
  40.2 8.3 %collective-permute-start.20 = (f32[24,640]{1,0:T(8,128)S(1)}, f32[24,640]{1,0:T(8,128)S(1)}, u32[]{:S(2)}, u32[]{:S(2)}) collective-permute-start(f32[24,640]{1,0:T(8,128)S(1)} %add.55), channel_id=1, source_target_pairs={{0,8},{2,10},{4,12},{6,14},{8,0},{10,2},{12,4},{14,6},{16,24},{18,... | collective-permute-start | bytes 184328 | tf_op jit(solution)/shard_map/ppermute | solution.py:318
  42.8 1.3 %collective-permute-start.12 = (f32[16,640]{1,0:T(8,128)S(1)}, f32[16,640]{1,0:T(8,128)S(1)}, u32[]{:S(2)}, u32[]{:S(2)}) collective-permute-start(f32[16,640]{1,0:T(8,128)S(1)} %gram.3), channel_id=1, source_target_pairs={{0,2},{2,0},{4,6},{6,4},{8,10},{10,8},{12,14},{14,12},{16,18},{18,... | collective-permute-start | bytes 122888 | tf_op jit(solution)/shard_map/ppermute | solution.py:318
  44.1 6.0 %collective-permute-start.13 = (f32[16,640]{1,0:T(8,128)S(1)}, f32[16,640]{1,0:T(8,128)S(1)}, u32[]{:S(2)}, u32[]{:S(2)}) collective-permute-start(f32[16,640]{1,0:T(8,128)S(1)} %add.56), channel_id=1, source_target_pairs={{0,16},{2,18},{4,20},{6,22},{8,24},{10,26},{12,28},{14,30},{16,0},... | collective-permute-start | bytes 122888 | tf_op jit(solution)/shard_map/ppermute | solution.py:318
  46.9 5.8 %collective-permute-start.14 = (f32[16,640]{1,0:T(8,128)S(1)}, f32[16,640]{1,0:T(8,128)S(1)}, u32[]{:S(2)}, u32[]{:S(2)}) collective-permute-start(f32[16,640]{1,0:T(8,128)S(1)} %add.56), channel_id=1, source_target_pairs={{0,24},{2,26},{4,28},{6,30},{8,16},{10,18},{12,20},{14,22},{16,8},... | collective-permute-start | bytes 122888 | tf_op jit(solution)/shard_map/ppermute | solution.py:318
  48.3 4.5 %collective-permute-start.15 = (f32[16,640]{1,0:T(8,128)S(1)}, f32[16,640]{1,0:T(8,128)S(1)}, u32[]{:S(2)}, u32[]{:S(2)}) collective-permute-start(f32[16,640]{1,0:T(8,128)S(1)} %add.56), channel_id=1, source_target_pairs={{0,8},{2,10},{4,12},{6,14},{8,0},{10,2},{12,4},{14,6},{16,24},{18,... | collective-permute-start | bytes 122888 | tf_op jit(solution)/shard_map/ppermute | solution.py:318
  48.5 7.3 %collective-permute-start.21 = (bf16[24,640]{1,0:T(8,128)(2,1)S(1)}, bf16[24,640]{1,0:T(8,128)(2,1)S(1)}, u32[]{:S(2)}, u32[]{:S(2)}) collective-permute-start(bf16[24,640]{1,0:T(8,128)(2,1)S(1)} %multiply_convert_fusion), channel_id=1, source_target_pairs={{0,1},{1,0},{2,3},{3,2},{4,5},{5,4},{6,7},{7,6},{8,9},{9,8},{10,11... | collective-permute-start | bytes 92168 | tf_op jit(solution)/shard_map/ppermute | solution.py:319
  52.7 5.0 %collective-permute-start.16 = (f32[16,640]{1,0:T(8,128)S(1)}, f32[16,640]{1,0:T(8,128)S(1)}, u32[]{:S(2)}, u32[]{:S(2)}) collective-permute-start(f32[16,640]{1,0:T(8,128)S(1)} %add_add_fusion.2), channel_id=1, source_target_pairs={{0,5},{1,4},{2,7},{3,6},{4,1},{5,0},{6,3},{7,2},{8,13},{9,12},{10,... | collective-permute-start | bytes 122888 | tf_op jit(solution)/shard_map/ppermute | solution.py:319
  55.2 4.0 %collective-permute-start.17 = (f32[16,640]{1,0:T(8,128)S(1)}, f32[16,640]{1,0:T(8,128)S(1)}, u32[]{:S(2)}, u32[]{:S(2)}) collective-permute-start(f32[16,640]{1,0:T(8,128)S(1)} %add_add_fusion.2), channel_id=1, source_target_pairs={{0,1},{1,0},{2,3},{3,2},{4,5},{5,4},{6,7},{7,6},{8,9},{9,8},{10,11... | collective-permute-start | bytes 122888 | tf_op jit(solution)/shard_map/ppermute | solution.py:319
